TPU v7x, 128 devices: a whole 4x4x4 slice. The times are simulated.
128 devices in a mesh: seq: 8 (over y, core), head: 16 (over x, z).
Axes of the slice: x: 4, y: 4, z: 4, core: 2. Of those that a mesh axis runs over, the one named last changes fastest.
Arguments:
- tokens: bfloat16 [16384, 2048], P('seq', 'head'), may hold values from -12 to 12
- w_query: bfloat16 [2048, 2048], P(None, 'head')
- w_key: bfloat16 [2048, 2048], P(None, 'head')
- w_value: bfloat16 [2048, 2048], P(None, 'head'), may hold values from -0.125 to 0.125
- w_out: bfloat16 [2048, 2048], P('head'), may hold values from -0.125 to 0.125
- cluster_id: int32 [16384, 16], P('seq', 'head'), may hold values from 0 to 63, as said below
- slot_index: int32 [16384, 16], P('seq', 'head'), may hold values from 0 to 32767, as said below
Outputs:
- mixed: bfloat16 [16384, 2048], P(('seq', 'head'))
Inputs may be any that keep to these rules, and one draw needn't show every extreme that they name: `slot_index`: for each head the slots of all tokens are distinct. The slot of a token of the s-th block of 2048 tokens is b * 512 + s * 64 + j with 0 <= j < 64. For each head some block is filled by all tokens, and from each block of 2048 tokens the 512 slots that it may take in 8 consecutive blocks starting at a multiple of 8 are all filled. `cluster_id`: the cluster of a token in a head is that of its block in slot_index: consecutive blocks form runs, and a run's cluster is the index of its first block.
All inputs are finite; a program needn't handle non-finite values.
Results may differ from a plain program's by a relative error of at most 0.0053.
Values may be sent and summed in bfloat16 or wider, within the bound.
No kernel may reach another device: no remote copies, remote signals or barrier semaphores. Data moves between devices by JAX's collectives and lax.ppermute only.
A program may use at most 128 MiB of HBM per device.

v0:
```python
import math

import jax
import jax.numpy as jnp
from jax import lax
from jax.experimental import pallas as pl
from jax.experimental.pallas import tpu as pltpu
from jax.sharding import Mesh, PartitionSpec as P


HD = 128
BLOCK = 512
TOK = 2048
HALF = TOK // 2
SEQ = 8
SIDE = 4
HEADS = 16
WIDTH = 2048
BLK = 8
MOST = 64
ROWS = SEQ * BLK * MOST
MID = BLK // 2
TOLD = (BLK - MID + 1 + (BLK - MID) // 2) * MOST
SENT = TOLD + 16
REST = (MID - 1 + 1 + MID // 2) * MOST
LINE = 4
EMPTY = 1 << 20
POS = 1 << 14
OFFSETS = (0, -1, 1, 2)
SCALE = HD ** (-0.5) * math.log2(math.e)
BF = jnp.bfloat16
F32 = jnp.float32


VMEM = pl.BlockSpec(memory_space=pltpu.VMEM)
SMEM = pl.BlockSpec(memory_space=pltpu.SMEM)
HBM = pl.BlockSpec(memory_space=pltpu.HBM)


def params(mib):
    return pltpu.CompilerParams(vmem_limit_bytes=mib * 1024 * 1024)


def ring(by):
    return [(i, (i + by) % SIDE) for i in range(SIDE)]


def ring_gather(piece, axis):
    back = lax.ppermute(piece, axis, ring(1))
    ahead = lax.ppermute(piece, axis, ring(-1))
    half = piece.shape[0] // 2
    far_low = lax.ppermute(back[:half], axis, ring(1))
    far_high = lax.ppermute(ahead[half:], axis, ring(-1))
    return back, ahead, far_low, far_high


def gather_near(part, first, second):
    back, ahead, far_low, far_high = ring_gather(part, first)
    low = jnp.concatenate([part, back], 0)
    high = jnp.concatenate([ahead, far_low, far_high], 0)
    back_low = lax.ppermute(low, second, ring(1))
    ahead_low = lax.ppermute(low, second, ring(-1))
    ahead_high = lax.ppermute(high, second, ring(-1))
    back_high = lax.ppermute(high, second, ring(1))
    return low, high, back_low, back_high, ahead_low, ahead_high


def gather_far(near, second):
    return lax.ppermute(near[2], second, ring(1)), lax.ppermute(near[5], second, ring(-1))


def wrap(index, by):
    return lax.rem(index + (by + SIDE), SIDE)


def slice_of(place_ref, swapped, outer, inner):
    x, z = place_ref[0], place_ref[1]
    if swapped:
        return wrap(x, outer) * SIDE + wrap(z, inner)
    return wrap(x, inner) * SIDE + wrap(z, outer)


def piece_list(refs, outers):
    return [
        (refs[2 * n + m // 2], m % 2, outer, inner)
        for n, outer in enumerate(outers)
        for m, inner in enumerate(OFFSETS)
    ]


def fill_weights(place_ref, weights, target, swapped, outers):
    row = 0
    for outer in outers:
        for inner in OFFSETS:
            src = pl.multiple_of(slice_of(place_ref, swapped, outer, inner) * HD, HD)
            for n, w in enumerate(weights):
                target[row : row + HD, n * HD : (n + 1) * HD] = w[pl.ds(src, HD), :]
            row += HD


def pick_own(place_ref, halves, own_ref):
    head = place_ref[0] * SIDE + place_ref[1]
    per = HALF // HD
    for swapped, pieces in halves:
        row = head - per if swapped else head

        @pl.when((head >= per) if swapped else (head < per))
        def _():
            for ref, at, outer, inner in pieces:
                col = pl.multiple_of(slice_of(place_ref, swapped, outer, inner) * HD, HD)
                rows = pl.multiple_of(at * HALF + row * HD, HD)
                own_ref[:, pl.ds(col, HD)] = ref[pl.ds(rows, HD), :]


TILE = 256


def multiply(pieces, base, w, finish):
    def step(i, carry):
        lhs = jnp.concatenate(
            [
                ref[pl.ds(pl.multiple_of(at * HALF + i * TILE, TILE), TILE), :]
                for ref, at, _, _ in pieces
            ],
            1,
        )
        rows = pl.ds(pl.multiple_of(base + i * TILE, TILE), TILE)
        finish(rows, jnp.dot(lhs, w[...], preferred_element_type=F32))
        return carry

    lax.fori_loop(0, HALF // TILE, step, 0)


def project_near(place_ref, wq, wk, wv, *refs):
    acc_ref, own_ref, wa, wb = refs[12:]
    a, b = piece_list(refs[:6], OFFSETS[:3]), piece_list(refs[6:12], OFFSETS[:3])
    fill_weights(place_ref, (wq, wk, wv), wa, False, OFFSETS[:3])
    fill_weights(place_ref, (wq, wk, wv), wb, True, OFFSETS[:3])

    def finish(rows, total):
        acc_ref[rows, :] = total

    multiply(a, 0, wa, finish)
    multiply(b, HALF, wb, finish)
    pick_own(place_ref, ((False, a), (True, b)), own_ref)


def scatter_rows(index_ref, src, pad):
    def step(i, carry):
        for k in range(16):
            t = i * 16 + k
            pad[index_ref[t]] = src[t]
        return carry

    lax.fori_loop(0, TOK // 16, step, 0)


def project_far(place_ref, index_ref, wq, wk, wv, told, acc, own_in, a0, a1, b0, b1, *refs):
    out_ref, rest_refs, own_ref = refs[0], refs[1 : 1 + SEQ], refs[1 + SEQ]
    wa, wb, rows, pad, full, rest, sems, rest_sems = refs[2 + SEQ :]
    a, b = piece_list((a0, a1), OFFSETS[3:]), piece_list((b0, b1), OFFSETS[3:])
    fill_weights(place_ref, (wq, wk, wv), wa, False, OFFSETS[3:])
    fill_weights(place_ref, (wq, wk, wv), wb, True, OFFSETS[3:])

    def finish(at, total):
        total = (acc[at, :] + total).astype(BF).astype(F32)
        twice = pl.multiple_of(at.start * (ROWS // TOK), TILE)
        pad[pl.ds(twice, TILE * ROWS // TOK)] = jnp.zeros((TILE * ROWS // TOK, LINE, HD), F32)
        flat = rows.reshape(TOK * LINE, HD)
        start = pl.multiple_of(at.start * LINE, LINE)
        for k in range(3):
            flat[pl.ds(start + k, TILE, stride=LINE), :] = total[:, k * HD : (k + 1) * HD]

    multiply(a, 0, wa, finish)
    multiply(b, HALF, wb, finish)
    own_ref[...] = own_in[...]
    pick_own(place_ref, ((False, a), (True, b)), own_ref)
    scatter_rows(index_ref, rows, pad)
    flat = pad.reshape(ROWS * LINE, HD)

    def line(o, b, *kinds):
        at = (o * BLK + b) * MOST * LINE
        return jnp.concatenate(
            [flat[pl.ds(at + k, MOST, stride=LINE), :] for k in kinds], 1
        ).astype(BF)

    def put(target, o, n, value):
        target[o, n * MOST : (n + 1) * MOST, :] = value

    def queries(o, b):
        return jnp.concatenate([line(o, b, 0), line(o, b + 1, 0)], 1)

    def send(o):
        return pltpu.make_async_copy(full.at[o], out_ref.at[o], sems.at[o])

    def send_rest(d):
        o = lax.rem(place_ref[3] + d, SEQ)
        return pltpu.make_async_copy(rest.at[o], rest_refs[d], rest_sems.at[d])

    for o in range(SEQ):
        for n in range(MID - 1, BLK):
            put(full, o, n - (MID - 1), line(o, n, 1, 2))
        for n in range(MID, BLK, 2):
            put(full, o, BLK - MID + 1 + (n - MID) // 2, queries(o, n))
        full[o, TOLD:, :] = told[o]
        send(o).start()
    for o in range(SEQ):
        for n in range(MID - 1):
            put(rest, o, n, line(o, n, 1, 2))
        put(rest, o, MID - 1, line(o, -1, 1, 2) if o else jnp.zeros((MOST, 2 * HD), BF))
        for n in range(0, MID, 2):
            put(rest, o, MID + n // 2, queries(o, n))
    for d in range(SEQ):
        send_rest(d).start()
    for o in range(SEQ):
        send(o).wait()
    for d in range(SEQ):
        send_rest(d).wait()


def place_values(index_ref, value_ref, empty_ref, out_ref):
    pltpu.sync_copy(empty_ref, out_ref)

    def step(i, carry):
        for k in range(16):
            t = i * 16 + k
            out_ref[index_ref[t]] = value_ref[t]
        return carry

    lax.fori_loop(0, TOK // 16, step, 0)


QT = 128


def told_lines(got):
    digits = got[:, TOLD:, :].astype(F32)
    value = digits[:, 0:3] + digits[:, 3:6] * 256.0 + digits[:, 6:9] * 65536.0
    lines = []
    for b in range(-1, BLK):
        row, at = (2, 0) if b < 0 else (b // 4, b % 4 * MOST)
        lines.append(
            jnp.concatenate([value[s, row : row + 1, at : at + MOST] for s in range(SEQ)], 1)
        )
    return lines


def attend_blocks(blocks, lines, query_of, pair_of, scores, tops, full, send):
    column = jnp.concatenate(lines[1:], 0).T
    ones = jnp.ones((BLOCK, HD), BF)
    tiles = [(n, i) for n in range(len(blocks)) for i in range(BLOCK // QT)]

    def size(i):
        return QT // MOST * (i + 1), QT * (i + 1)

    def score(t):
        n, i = tiles[t]
        b = blocks[n]
        srcs, wide = size(i)
        base = jnp.floor(jnp.min(lines[b + 1], axis=1, keepdims=True) * (1.0 / POS)) * POS
        earlier = jnp.where(lines[b] >= base, lines[b], float(EMPTY))
        query = query_of(b, srcs)[i * QT :, :]
        mine = column[i * QT : (i + 1) * QT, b : b + 1]
        top = None
        for k, (which, line) in enumerate(((b - 1, earlier), (b, lines[b + 1]))):
            part = lax.dot_general(
                query,
                pair_of(which, srcs)[:, :HD],
                (((1,), (1,)), ((), ())),
                preferred_element_type=F32,
            )
            part = jnp.where(line[:, :wide] <= mine, part, F32(-1e30))
            scores[t % 2][:, k * wide : (k + 1) * wide] = part
            part = jnp.max(part, axis=1, keepdims=True)
            top = part if top is None else jnp.maximum(top, part)
        tops[t % 2][...] = jnp.broadcast_to(top, (QT, HD))

    def finish(t):
        n, i = tiles[t]
        b = blocks[n]
        srcs, wide = size(i)
        mixed = None
        for k, which in enumerate((b - 1, b)):
            top = jnp.concatenate([tops[t % 2][...]] * (wide // HD), 1)
            part = scores[t % 2][:, k * wide : (k + 1) * wide]
            expon = jnp.exp2((part - top) * F32(SCALE)).astype(BF)
            values = jnp.concatenate([pair_of(which, srcs)[:, HD:], ones[:wide]], 1)
            prod = jnp.dot(expon, values, preferred_element_type=F32)
            mixed = prod if mixed is None else mixed + prod
        done = (mixed[:, :HD] / mixed[:, HD:]).astype(BF)
        full[QT // MOST * i : srcs, n] = done.reshape(QT // MOST, MOST, HD)
        if i == BLOCK // QT - 1:
            send(n).start()

    score(0)
    for t in range(len(tiles)):
        if t + 1 < len(tiles):
            score(t + 1)
        finish(t)
    for n in range(len(blocks)):
        send(n).wait()


def rows_of(ref, n, srcs):
    return ref[:srcs, n * MOST : (n + 1) * MOST, :].reshape(srcs * MOST, 2 * HD)


def attend_late(got, out_ref, s0, s1, t0, t1, full, sems):
    def query_of(b, srcs):
        half = b % 2 * HD
        return rows_of(got, BLK - MID + 1 + (b - MID) // 2, srcs)[:, half : half + HD]

    def pair_of(b, srcs):
        return rows_of(got, b - (MID - 1), srcs)

    def send(n):
        return pltpu.make_async_copy(full.at[:, n], out_ref.at[:, n], sems.at[n])

    attend_blocks(
        range(MID, BLK), told_lines(got), query_of, pair_of, (s0, s1), (t0, t1), full, send
    )


def attend_early(place_ref, got, *refs):
    parts, out_ref = refs[:SEQ], refs[SEQ]
    rest, s0, s1, t0, t1, full, sems = refs[SEQ + 1 :]
    for d in range(SEQ):
        rest[lax.rem(place_ref[3] + (SEQ - d), SEQ)] = parts[d][...]

    def query_of(b, srcs):
        half = b % 2 * HD
        return rows_of(rest, MID + b // 2, srcs)[:, half : half + HD]

    def pair_of(b, srcs):
        if b == MID - 1:
            return rows_of(got, 0, srcs)
        return rows_of(rest, MID - 1 if b < 0 else b, srcs)

    def send(n):
        return pltpu.make_async_copy(full.at[:, n], out_ref.at[:, n], sems.at[n])

    attend_blocks(range(MID), told_lines(got), query_of, pair_of, (s0, s1), (t0, t1), full, send)


def take_rows(index_ref, early_ref, late_ref, out_ref, wide, taken):
    flat = wide.reshape(ROWS, HD)
    per = MID * MOST
    for o in range(SEQ):
        for n, ref in enumerate((early_ref, late_ref)):
            at = (2 * o + n) * per
            flat[at : at + per, :] = ref[o * per : (o + 1) * per, :].astype(F32)

    def step(i, carry):
        for k in range(16):
            t = i * 16 + k
            taken[t] = wide[index_ref[t]]
        return carry

    lax.fori_loop(0, TOK // 16, step, 0)
    out_ref[...] = taken.reshape(TOK, HD)[...].astype(BF)


COLS = 256


def combine(place_ref, rows_ref, *refs):
    near, far = refs[:5], refs[5:10]
    own_ref, out_ref, lhs = refs[10:]
    n = pl.program_id(0)

    @pl.when(n == 0)
    def _():
        for k, outer in enumerate(OFFSETS):
            for m, inner in enumerate(OFFSETS):
                h = slice_of(place_ref, False, outer, inner)
                col = (k * SIDE + m) * HD
                lhs[:, col : col + HD] = rows_ref[h]

    core = place_ref[2]
    for group, which in ((near, core), (far, 1 - core)):
        total, row = None, 0
        for w in group:
            depth = w.shape[0]
            prod = jnp.dot(lhs[:, row : row + depth], w[...], preferred_element_type=F32)
            total = prod if total is None else total + prod
            row += depth
        col = pl.ds(pl.multiple_of(which * (WIDTH // 2) + n * COLS, COLS), COLS)
        out_ref[:, col] = (total + own_ref[:, col].astype(F32)).astype(BF)


def estimate(flops, mib):
    return pl.CostEstimate(flops=flops, bytes_accessed=mib << 20, transcendentals=0)


def shape(dims, kind):
    return jax.ShapeDtypeStruct(dims, kind)


def sublayer(tokens, w_query, w_key, w_value, w_out, cluster_id, slot_index):
    x, z, seq = lax.axis_index("hx"), lax.axis_index("hz"), lax.axis_index("seq")
    core = lax.rem(seq, 2)
    place = jnp.stack([x, z, core, seq]).astype(jnp.int32)

    slots = slot_index.reshape(TOK)
    index = (slots // BLOCK) * MOST + slots % MOST
    value = cluster_id.reshape(TOK) * POS + seq * TOK + jnp.arange(TOK, dtype=jnp.int32)

    near_a = gather_near(tokens[:HALF], "hx", "hz")
    near_b = gather_near(tokens[HALF:], "hz", "hx")
    tied, _ = lax.optimization_barrier((index, near_b[5]))
    values = pl.pallas_call(
        place_values,
        out_shape=shape((ROWS,), jnp.int32),
        in_specs=[SMEM, SMEM, pl.BlockSpec(memory_space=pl.ANY)],
        out_specs=SMEM,
        name="place_values",
        cost_estimate=estimate(0, 12),
    )(tied, value, jnp.full((ROWS,), EMPTY, jnp.int32)).reshape(SEQ, BLK, MOST)
    halo = jnp.concatenate(
        [jnp.full((1, MOST), EMPTY, jnp.int32), values[: SEQ - 1, BLK - 1]], 0
    )
    halo = jnp.pad(halo, ((0, 0), (0, 2 * HD - MOST)))[:, None]
    values = jnp.concatenate([values.reshape(SEQ, 2, 2 * HD), halo], 1)
    told = jnp.concatenate([values & 255, (values >> 8) & 255, values >> 16], 1)
    told = jnp.pad(told, ((0, 0), (0, SENT - TOLD - 9), (0, 0))).astype(BF)

    weights = (w_query, w_key, w_value)
    acc, own = pl.pallas_call(
        project_near,
        out_shape=(shape((TOK, 3 * HD), F32), shape((HD, WIDTH), BF)),
        in_specs=[SMEM] + [VMEM] * 15,
        out_specs=(VMEM, VMEM),
        scratch_shapes=[pltpu.VMEM((12 * HD, 3 * HD), BF)] * 2,
        compiler_params=params(20),
        name="project_near",
        cost_estimate=estimate(2 * TOK * 12 * HD * 3 * HD, 10),
    )(place, *weights, *near_a, *near_b)
    far_a = gather_far(near_a, "hz")
    far_b = gather_far(near_b, "hx")
    sent, *rest, own = pl.pallas_call(
        project_far,
        out_shape=(
            pltpu.HBM((SEQ, SENT, 2 * HD), BF),
            *[pltpu.HBM((REST, 2 * HD), BF)] * SEQ,
            shape((HD, WIDTH), BF),
        ),
        in_specs=[SMEM, SMEM] + [VMEM] * 10,
        out_specs=(HBM,) * (1 + SEQ) + (VMEM,),
        scratch_shapes=[pltpu.VMEM((4 * HD, 3 * HD), BF)] * 2
        + [
            pltpu.VMEM((TOK, LINE, HD), F32),
            pltpu.VMEM((ROWS, LINE, HD), F32),
            pltpu.VMEM((SEQ, SENT, 2 * HD), BF),
            pltpu.VMEM((SEQ, REST, 2 * HD), BF),
            pltpu.SemaphoreType.DMA((SEQ,)),
            pltpu.SemaphoreType.DMA((SEQ,)),
        ],
        compiler_params=params(28),
        name="project_far",
        cost_estimate=estimate(2 * TOK * 4 * HD * 3 * HD, 24),
    )(place, index, *weights, told, acc, own, *far_a, *far_b)
    got = lax.all_to_all(sent, "seq", 0, 0, tiled=True)
    parts = [rest[0]]
    for d in range(1, SEQ):
        parts.append(lax.ppermute(rest[d], "seq", [(i, (i + d) % SEQ) for i in range(SEQ)]))

    w_half = lax.dynamic_slice_in_dim(w_out, core * (WIDTH // 2), WIDTH // 2, 1)
    w_half, _ = lax.optimization_barrier((w_half, own))
    w_row = jnp.concatenate((w_half,) + ring_gather(w_half, "hx"), 0)
    w_near = (w_row,) + ring_gather(w_row, "hz")
    w_far = tuple(lax.ppermute(w, "seq", [(i, i ^ 1) for i in range(SEQ)]) for w in w_near)

    scratch = [
        *[pltpu.VMEM((QT, 2 * BLOCK), F32)] * 2,
        *[pltpu.VMEM((QT, HD), F32)] * 2,
        pltpu.VMEM((SEQ, MID, MOST, HD), BF),
        pltpu.SemaphoreType.DMA((MID,)),
    ]
    late = pl.pallas_call(
        attend_late,
        out_shape=pltpu.HBM((SEQ, MID, MOST, HD), BF),
        in_specs=[VMEM],
        out_specs=HBM,
        scratch_shapes=scratch,
        compiler_params=params(12),
        name="attend_late",
        cost_estimate=estimate(4 * MID * BLOCK * 2 * BLOCK * HD, 6),
    )(got)
    late = lax.all_to_all(late, "seq", 0, 0, tiled=True).reshape(ROWS // 2, HD)
    early = pl.pallas_call(
        attend_early,
        out_shape=pltpu.HBM((SEQ, MID, MOST, HD), BF),
        in_specs=[SMEM] + [VMEM] * (1 + SEQ),
        out_specs=HBM,
        scratch_shapes=[pltpu.VMEM((SEQ, REST, 2 * HD), BF)] + scratch,
        compiler_params=params(16),
        name="attend_early",
        cost_estimate=estimate(4 * MID * BLOCK * 2 * BLOCK * HD, 8),
    )(place, got, *parts)
    early = lax.all_to_all(early, "seq", 0, 0, tiled=True).reshape(ROWS // 2, HD)
    taken = pl.pallas_call(
        take_rows,
        out_shape=shape((TOK, HD), BF),
        in_specs=[SMEM, VMEM, VMEM],
        out_specs=VMEM,
        scratch_shapes=[pltpu.VMEM((ROWS, 1, HD), F32), pltpu.VMEM((TOK, 1, HD), F32)],
        compiler_params=params(10),
        name="take_rows",
        cost_estimate=estimate(0, 8),
    )(index, early, late)
    all_heads = lax.all_to_all(
        taken.reshape(HEADS, HD, HD), ("hx", "hz"), 0, 0, tiled=True
    )
    whole = lambda *dims: pl.BlockSpec(dims, lambda n: (0,) * len(dims))
    w_specs = [
        pl.BlockSpec((depth, COLS), lambda n: (0, n)) for depth in (512, 512, 512, 256, 256)
    ]
    return pl.pallas_call(
        combine,
        grid=(WIDTH // 2 // COLS,),
        out_shape=shape((HD, WIDTH), BF),
        in_specs=[SMEM, whole(HEADS, HD, HD)] + w_specs * 2 + [whole(HD, WIDTH)],
        out_specs=whole(HD, WIDTH),
        scratch_shapes=[pltpu.VMEM((HD, WIDTH), BF)],
        compiler_params=params(16),
        name="combine",
        cost_estimate=estimate(2 * HD * WIDTH * WIDTH, 10),
    )(place, all_heads, *w_near, *w_far, own)


def solution(mesh):
    grid = Mesh(mesh.devices.reshape(SEQ, SIDE, SIDE), ("seq", "hx", "hz"))
    head = ("hx", "hz")
    in_specs = (
        P("seq", head),
        P(None, head),
        P(None, head),
        P(None, head),
        P(head, None),
        P("seq", head),
        P("seq", head),
    )
    out_specs = P(("seq", "hx", "hz"), None)
    return jax.shard_map(sublayer, mesh=grid, in_specs=in_specs, out_specs=out_specs, check_vma=False)
```

profile of v0, /device:TPU:0, one launch (start us, length us, event | category | flops | bytes accessed | tf_op | source)
XLA Modules:
  0.0 204.2 jit_solution(12611264057802592743)
XLA Ops:
  1.1 4.2 %collective-permute-start = (bf16[1024,128]{1,0:T(8,128)(2,1)S(1)}, bf16[1024,128]{1,0:T(8,128)(2,1)S(1)}, u32[]{:S(2)}, u32[]{:S(2)}) collective-permute-start(bf16[1024,128]{1,0:T(8,128)(2,1)S(1)} %get-tuple-element.34), channel_id=1, source_target_pairs={{0,3},{1,0},{2,1},{3,2},{4,7},{5,4},{6,5},{7,6},{8,11},{9,8},{10,9... | collective-permute-start | bytes 786440 | tf_op jit(solution)/shard_map/ppermute | solution.py:50
  9.3 5.0 %collective-permute-done.5 = bf16[1024,128]{1,0:T(8,128)(2,1)S(1)} collective-permute-done((bf16[1024,128]{1,0:T(8,128)(2,1)S(1)}, bf16[1024,128]{1,0:T(8,128)(2,1)S(1)}, u32[]{:S(2)}, u32[]{:S(2)}) %collective-permute-start.5) | collective-permute-done | bytes 262176 | tf_op jit(solution)/shard_map/ppermute | solution.py:49
  14.5 3.2 %collective-permute-start.11 = (bf16[2048,128]{1,0:T(8,128)(2,1)S(1)}, bf16[2048,128]{1,0:T(8,128)(2,1)S(1)}, u32[]{:S(2)}, u32[]{:S(2)}) collective-permute-start(bf16[2048,128]{1,0:T(8,128)(2,1)S(1)} %pad_maximum_fusion.refs_0_), channel_id=1, source_target_pairs={{0,3},{1,0},{2,1},{3,2},{4,7},{5,4},{6,5},{7,6},{8,11},{9,8},{10,9... | collective-permute-start | bytes 1572872 | tf_op jit(solution)/shard_map/ppermute | solution.py:62
  19.2 2.7 %collective-permute-start.3 = (bf16[512,128]{1,0:T(8,128)(2,1)S(1)}, bf16[512,128]{1,0:T(8,128)(2,1)S(1)}, u32[]{:S(2)}, u32[]{:S(2)}) collective-permute-start(bf16[512,128]{1,0:T(8,128)(2,1)S(1)} %slice.45), channel_id=1, source_target_pairs={{0,3},{1,0},{2,1},{3,2},{4,7},{5,4},{6,5},{7,6},{8,11},{9,8},{10,9... | collective-permute-start | bytes 393224 | tf_op jit(solution)/shard_map/ppermute | solution.py:53
  28.5 2.5 %collective-permute-done.2 = bf16[512,128]{1,0:T(8,128)(2,1)S(1)} collective-permute-done((bf16[512,128]{1,0:T(8,128)(2,1)S(1)}, bf16[512,128]{1,0:T(8,128)(2,1)S(1)}, u32[]{:S(2)}, u32[]{:S(2)}) %collective-permute-start.2) | collective-permute-done | bytes 131104 | tf_op jit(solution)/shard_map/ppermute | solution.py:52
  34.4 2.9 %collective-permute-start.4 = (bf16[2048,128]{1,0:T(8,128)(2,1)}, bf16[2048,128]{1,0:T(8,128)(2,1)}, u32[]{:S(2)}, u32[]{:S(2)}) collective-permute-start(bf16[2048,128]{1,0:T(8,128)(2,1)} %constant_dynamic-update-slice_fusion.refs_7_), channel_id=1, source_target_pairs={{0,12},{4,0},{8,4},{12,8},{1,13},{5,1},{9,5},{13,9},{2,14},{6,2},{... | collective-permute-start | bytes 1572872 | tf_op jit(solution)/shard_map/ppermute | solution.py:63
  40.6 3.2 %collective-permute-start.12 = (bf16[2048,128]{1,0:T(8,128)(2,1)}, bf16[2048,128]{1,0:T(8,128)(2,1)}, u32[]{:S(2)}, u32[]{:S(2)}) collective-permute-start(bf16[2048,128]{1,0:T(8,128)(2,1)} %constant_dynamic-update-slice_fusion.3.refs_1_), channel_id=1, source_target_pairs={{0,3},{1,0},{2,1},{3,2},{4,7},{5,4},{6,5},{7,6},{8,11},{9,8},{10,9... | collective-permute-start | bytes 1572872 | tf_op jit(solution)/shard_map/ppermute | solution.py:63
  44.4 5.4 %collective-permute-done.4.refs_11_ = bf16[2048,128]{1,0:T(8,128)(2,1)} collective-permute-done((bf16[2048,128]{1,0:T(8,128)(2,1)}, bf16[2048,128]{1,0:T(8,128)(2,1)}, u32[]{:S(2)}, u32[]{:S(2)}) %collective-permute-start.4) | collective-permute-done | bytes 524320 | tf_op jit(solution)/shard_map/ppermute | solution.py:63
  51.1 6.2 %place_values.1 = s32[4096]{0:T(1024)} custom-call(s32[2048]{0:T(1024)} %fusion.7.index_ref, s32[2048]{0:T(1024)} %iota_add_fusion.value_ref, s32[4096]{0:T(1024)} %broadcast_in_dim.7.empty_ref), custom_call_target="tpu_custom_call" | custom-call | bytes 12582912 | tf_op jit(solution)/shard_map/place_values/pallas_call | solution.py:411
  58.9 1.9 collective-permute-start.18
  60.9 1.9 collective-permute-start.19
  62.8 3.1 %collective-permute-start.17 = (bf16[2048,128]{1,0:T(8,128)(2,1)}, bf16[2048,128]{1,0:T(8,128)(2,1)S(1)}, u32[]{:S(2)}, u32[]{:S(2)}) collective-permute-start(bf16[2048,128]{1,0:T(8,128)(2,1)} %collective-permute-done.12.refs_5_), channel_id=1, source_target_pairs={{0,3},{1,0},{2,1},{3,2},{4,7},{5,4},{6,5},{7,6},{8,11},{9,8},{10,9... | collective-permute-start | bytes 1572872 | tf_op jit(solution)/shard_map/ppermute | solution.py:69
  68.2 7.4 %project_near.1 = (f32[2048,384]{1,0:T(8,128)S(1)}, bf16[128,2048]{1,0:T(8,128)(2,1)S(1)}) custom-call(s32[4]{0:T(128)S(1)} %pad_add_fusion.1.place_ref, bf16[2048,128]{1,0:T(8,128)(2,1)S(1)} %copy-done.1, bf16[2048,128]{1,0:T(8,128)(2,1)S(1)} %copy-done.2, bf16[2048,128]{1,0:T(8,128)(2,1)S(1)} %copy-done.3, bf16[2048,128]{1,0:T(8,128)(2,1)S(1)} %pad_maximum_fusion.refs_0_, ...), custom_call_target="tpu_custom_call" | custom-call | flops 2415919104 | bytes 10485760 | tf_op jit(solution)/shard_map/project_near/pallas_call | solution.py:428
  75.6 8.6 %project_far.1 = (bf16[8,464,256]{2,1,0:T(8,128)(2,1)}, bf16[384,256]{1,0:T(8,128)(2,1)}, bf16[384,256]{1,0:T(8,128)(2,1)}, bf16[384,256]{1,0:T(8,128)(2,1)}, bf...) custom-call(s32[4]{0:T(128)S(1)} %pad_add_fusion.1.place_ref, ...), custom_call_target="tpu_custom_call" | custom-call | flops 805306368 | bytes 25165824 | tf_op jit(solution)/shard_map/project_far/pallas_call | solution.py:440
  85.0 4.5 %all-to-all-start = ((bf16[8,464,256]{2,1,0:T(8,128)(2,1)}), bf16[8,464,256]{2,1,0:T(8,128)(2,1)S(1)}, u32[]{:S(2)}, u32[]{:S(2)}) async-start(bf16[8,464,256]{2,1,0:T(8,128)(2,1)} %get-tuple-element.22), calls=%async_computation | async-start | bytes 3801088 | tf_op jit(solution)/shard_map/all_to_all | solution.py:462
  93.7 6.0 %collective-permute-done.27 = bf16[128,1024]{1,0:T(8,128)(2,1)S(1)} collective-permute-done((bf16[128,1024]{1,0:T(8,128)(2,1)S(1)}, bf16[128,1024]{1,0:T(8,128)(2,1)S(1)}, u32[]{:S(2)}, u32[]{:S(2)}) %collective-permute-start.27) | collective-permute-done | bytes 262176 | tf_op jit(solution)/shard_map/ppermute | solution.py:49
  100.0 3.1 %collective-permute-start.30 = (bf16[64,1024]{1,0:T(8,128)(2,1)S(1)}, bf16[64,1024]{1,0:T(8,128)(2,1)S(1)}, u32[]{:S(2)}, u32[]{:S(2)}) collective-permute-start(bf16[64,1024]{1,0:T(8,128)(2,1)S(1)} %slice.50), channel_id=1, source_target_pairs={{0,12},{4,0},{8,4},{12,8},{1,13},{5,1},{9,5},{13,9},{2,14},{6,2},{... | collective-permute-start | bytes 393224 | tf_op jit(solution)/shard_map/ppermute | solution.py:53
  107.3 3.2 %collective-permute-start.32 = (bf16[512,1024]{1,0:T(8,128)(2,1)}, bf16[512,1024]{1,0:T(8,128)(2,1)}, u32[]{:S(2)}, u32[]{:S(2)}) collective-permute-start(bf16[512,1024]{1,0:T(8,128)(2,1)} %constant_dynamic-update-slice_fusion.6.refs_0_), channel_id=1, source_target_pairs={{0,3},{1,0},{2,1},{3,2},{4,7},{5,4},{6,5},{7,6},{8,11},{9,8},{10,9... | collective-permute-start | bytes 3145736 | tf_op jit(solution)/shard_map/ppermute | solution.py:50
  113.9 3.8 %collective-permute-done.20.refs_1_ = bf16[384,256]{1,0:T(8,128)(2,1)S(1)} collective-permute-done((bf16[384,256]{1,0:T(8,128)(2,1)}, bf16[384,256]{1,0:T(8,128)(2,1)S(1)}, u32[]{:S(2)}, u32[]{:S(2)}) %collective-permute-start.20) | collective-permute-done | bytes 196640 | tf_op jit(solution)/shard_map/ppermute | solution.py:465
  122.2 3.1 %collective-permute-done.22.refs_3_ = bf16[384,256]{1,0:T(8,128)(2,1)S(1)} collective-permute-done((bf16[384,256]{1,0:T(8,128)(2,1)}, bf16[384,256]{1,0:T(8,128)(2,1)S(1)}, u32[]{:S(2)}, u32[]{:S(2)}) %collective-permute-start.22) | collective-permute-done | bytes 196640 | tf_op jit(solution)/shard_map/ppermute | solution.py:465
  125.9 3.3 %collective-permute-done.23.refs_4_ = bf16[384,256]{1,0:T(8,128)(2,1)S(1)} collective-permute-done((bf16[384,256]{1,0:T(8,128)(2,1)}, bf16[384,256]{1,0:T(8,128)(2,1)S(1)}, u32[]{:S(2)}, u32[]{:S(2)}) %collective-permute-start.23) | collective-permute-done | bytes 196640 | tf_op jit(solution)/shard_map/ppermute | solution.py:465
  130.5 2.1 %collective-permute-done.25.refs_6_ = bf16[384,256]{1,0:T(8,128)(2,1)S(1)} collective-permute-done((bf16[384,256]{1,0:T(8,128)(2,1)}, bf16[384,256]{1,0:T(8,128)(2,1)S(1)}, u32[]{:S(2)}, u32[]{:S(2)}) %collective-permute-start.25) | collective-permute-done | bytes 196640 | tf_op jit(solution)/shard_map/ppermute | solution.py:465
  142.9 4.6 %attend_early.1 = bf16[8,4,64,128]{3,2,1,0:T(8,128)(2,1)} custom-call(s32[4]{0:T(128)S(1)} %pad_add_fusion.1.place_ref, bf16[8,464,256]{2,1,0:T(8,128)(2,1)S(1)} %all-to-all-done.got, bf16[384,256]{1,0:T(8,128)(2,1)S(1)} %copy-done.6, bf16[384,256]{1,0:T(8,128)(2,1)S(1)} %copy-done.8, bf16[384,256]{1,0:T(8,128)(2,1)S(1)} %copy-done.10, ...), custom_call_target="tpu_custom_call" | custom-call | flops 1073741824 | bytes 8388608 | tf_op jit(solution)/shard_map/attend_early/pallas_call | solution.py:490
  147.5 4.3 %all-to-all-start.1 = ((bf16[8,4,64,128]{3,2,1,0:T(8,128)(2,1)}), bf16[8,4,64,128]{3,2,1,0:T(8,128)(2,1)}, u32[]{:S(2)}, u32[]{:S(2)}) async-start(bf16[8,4,64,128]{3,2,1,0:T(8,128)(2,1)} %attend_early.1), calls=%async_computation.1 | async-start | bytes 1048576 | tf_op jit(solution)/shard_map/all_to_all | solution.py:500
  155.1 3.2 %collective-permute-start.34 = (bf16[256,1024]{1,0:T(8,128)(2,1)}, bf16[256,1024]{1,0:T(8,128)(2,1)}, u32[]{:S(2)}, u32[]{:S(2)}) collective-permute-start(bf16[256,1024]{1,0:T(8,128)(2,1)} %slice.52), channel_id=1, source_target_pairs={{0,3},{1,0},{2,1},{3,2},{4,7},{5,4},{6,5},{7,6},{8,11},{9,8},{10,9... | collective-permute-start | bytes 1572872 | tf_op jit(solution)/shard_map/ppermute | solution.py:53
  158.8 4.0 %attend_late.1 = bf16[8,4,64,128]{3,2,1,0:T(8,128)(2,1)} custom-call(bf16[8,464,256]{2,1,0:T(8,128)(2,1)S(1)} %all-to-all-done.got), custom_call_target="tpu_custom_call" | custom-call | flops 1073741824 | bytes 6291456 | tf_op jit(solution)/shard_map/attend_late/pallas_call | solution.py:479
  162.9 4.6 %all-to-all-start.2 = ((bf16[8,4,64,128]{3,2,1,0:T(8,128)(2,1)}), bf16[8,4,64,128]{3,2,1,0:T(8,128)(2,1)S(1)}, u32[]{:S(2)}, u32[]{:S(2)}) async-start(bf16[8,4,64,128]{3,2,1,0:T(8,128)(2,1)} %attend_late.1), calls=%async_computation.2 | async-start | bytes 1048576 | tf_op jit(solution)/shard_map/all_to_all | solution.py:489
  169.7 8.0 %all-to-all-done.2 = bf16[8,4,64,128]{3,2,1,0:T(8,128)(2,1)S(1)} async-done(((bf16[8,4,64,128]{3,2,1,0:T(8,128)(2,1)}), bf16[8,4,64,128]{3,2,1,0:T(8,128)(2,1)S(1)}, u32[]{:S(2)}, u32[]{:S(2)}) %all-to-all-start.2) | async-done | bytes 524320 | tf_op jit(solution)/shard_map/all_to_all | solution.py:489
  177.7 4.3 %take_rows.1 = bf16[2048,128]{1,0:T(8,128)(2,1)} custom-call(s32[2048]{0:T(1024)S(1)} %copy-done.21, bf16[2048,128]{1,0:T(8,128)(2,1)} %bitcast.7.early_ref, bf16[2048,128]{1,0:T(8,128)(2,1)S(1)} %bitcast.12), custom_call_target="tpu_custom_call" | custom-call | bytes 8388608 | tf_op jit(solution)/shard_map/take_rows/pallas_call | solution.py:501
  182.0 5.6 %all-to-all-start.3 = ((bf16[16,128,128]{2,1,0:T(8,128)(2,1)}), bf16[16,128,128]{2,1,0:T(8,128)(2,1)S(1)}, u32[]{:S(2)}, u32[]{:S(2)}) async-start(bf16[16,128,128]{2,1,0:T(8,128)(2,1)} %bitcast.9), calls=%async_computation.3 | async-start | bytes 1048576 | tf_op jit(solution)/shard_map/all_to_all | solution.py:511
  187.7 11.1 %all-to-all-done.3.rows_ref = bf16[16,128,128]{2,1,0:T(8,128)(2,1)S(1)} async-done(((bf16[16,128,128]{2,1,0:T(8,128)(2,1)}), bf16[16,128,128]{2,1,0:T(8,128)(2,1)S(1)}, u32[]{:S(2)}, u32[]{:S(2)}) %all-to-all-start.3) | async-done | bytes 524320 | tf_op jit(solution)/shard_map/all_to_all | solution.py:511
  198.8 5.4 %combine.1 = bf16[128,2048]{1,0:T(8,128)(2,1)} custom-call(s32[4]{0:T(128)S(1)} %pad_add_fusion.1.place_ref, bf16[16,128,128]{2,1,0:T(8,128)(2,1)S(1)} %all-to-all-done.3.rows_ref, bf16[512,1024]{1,0:T(8,128)(2,1)} %constant_dynamic-update-slice_fusion.6.refs_0_, bf16[512,1024]{1,0:T(8,128)(2,1)S(1)} %collective-permute-done.31.refs_1_, ...), custom_call_target="tpu_custom_call" | custom-call | flops 1073741824 | bytes 10485760 | tf_op jit(solution)/shard_map/combine/pallas_call | solution.py:518
  (161 shorter events, 61.3 us)
Async XLA Ops:
  1.1 16.6 %collective-permute-start = (bf16[1024,128]{1,0:T(8,128)(2,1)S(1)}, bf16[1024,128]{1,0:T(8,128)(2,1)S(1)}, u32[]{:S(2)}, u32[]{:S(2)}) collective-permute-start(bf16[1024,128]{1,0:T(8,128)(2,1)S(1)} %get-tuple-element.34), channel_id=1, source_target_pairs={{0,3},{1,0},{2,1},{3,2},{4,7},{5,4},{6,5},{7,6},{8,11},{9,8},{10,9... | collective-permute-start | bytes 786440 | tf_op jit(solution)/shard_map/ppermute | solution.py:50
  5.4 12.3 %collective-permute-start.1 = (bf16[1024,128]{1,0:T(8,128)(2,1)S(1)}, bf16[1024,128]{1,0:T(8,128)(2,1)S(1)}, u32[]{:S(2)}, u32[]{:S(2)}) collective-permute-start(bf16[1024,128]{1,0:T(8,128)(2,1)S(1)} %get-tuple-element.34), channel_id=1, source_target_pairs={{0,1},{1,2},{2,3},{3,0},{4,5},{5,6},{6,7},{7,4},{8,9},{9,10},{10,1... | collective-permute-start | bytes 786440 | tf_op jit(solution)/shard_map/ppermute | solution.py:49
  6.9 18.7 %collective-permute-start.6 = (bf16[1024,128]{1,0:T(8,128)(2,1)S(1)}, bf16[1024,128]{1,0:T(8,128)(2,1)}, u32[]{:S(2)}, u32[]{:S(2)}) collective-permute-start(bf16[1024,128]{1,0:T(8,128)(2,1)S(1)} %get-tuple-element.33), channel_id=1, source_target_pairs={{0,12},{4,0},{8,4},{12,8},{1,13},{5,1},{9,5},{13,9},{2,14},{6,2},{... | collective-permute-start | bytes 786440 | tf_op jit(solution)/shard_map/ppermute | solution.py:50
  14.4 25.3 %collective-permute-start.9 = (bf16[2048,128]{1,0:T(8,128)(2,1)S(1)}, bf16[2048,128]{1,0:T(8,128)(2,1)S(1)}, u32[]{:S(2)}, u32[]{:S(2)}) collective-permute-start(bf16[2048,128]{1,0:T(8,128)(2,1)S(1)} %pad_maximum_fusion.refs_0_), channel_id=1, source_target_pairs={{0,1},{1,2},{2,3},{3,0},{4,5},{5,6},{6,7},{7,4},{8,9},{9,10},{10,1... | collective-permute-start | bytes 1572872 | tf_op jit(solution)/shard_map/ppermute | solution.py:61
  14.5 25.2 %collective-permute-start.11 = (bf16[2048,128]{1,0:T(8,128)(2,1)S(1)}, bf16[2048,128]{1,0:T(8,128)(2,1)S(1)}, u32[]{:S(2)}, u32[]{:S(2)}) collective-permute-start(bf16[2048,128]{1,0:T(8,128)(2,1)S(1)} %pad_maximum_fusion.refs_0_), channel_id=1, source_target_pairs={{0,3},{1,0},{2,1},{3,2},{4,7},{5,4},{6,5},{7,6},{8,11},{9,8},{10,9... | collective-permute-start | bytes 1572872 | tf_op jit(solution)/shard_map/ppermute | solution.py:62
  17.7 13.3 %collective-permute-start.2 = (bf16[512,128]{1,0:T(8,128)(2,1)S(1)}, bf16[512,128]{1,0:T(8,128)(2,1)S(1)}, u32[]{:S(2)}, u32[]{:S(2)}) collective-permute-start(bf16[512,128]{1,0:T(8,128)(2,1)S(1)} %slice.44), channel_id=1, source_target_pairs={{0,1},{1,2},{2,3},{3,0},{4,5},{5,6},{6,7},{7,4},{8,9},{9,10},{10,1... | collective-permute-start | bytes 393224 | tf_op jit(solution)/shard_map/ppermute | solution.py:52
  19.2 14.1 %collective-permute-start.3 = (bf16[512,128]{1,0:T(8,128)(2,1)S(1)}, bf16[512,128]{1,0:T(8,128)(2,1)S(1)}, u32[]{:S(2)}, u32[]{:S(2)}) collective-permute-start(bf16[512,128]{1,0:T(8,128)(2,1)S(1)} %slice.45), channel_id=1, source_target_pairs={{0,3},{1,0},{2,1},{3,2},{4,7},{5,4},{6,5},{7,6},{8,11},{9,8},{10,9... | collective-permute-start | bytes 393224 | tf_op jit(solution)/shard_map/ppermute | solution.py:53
  33.3 25.5 %collective-permute-start.13 = (bf16[2048,128]{1,0:T(8,128)(2,1)S(1)}, bf16[2048,128]{1,0:T(8,128)(2,1)}, u32[]{:S(2)}, u32[]{:S(2)}) collective-permute-start(bf16[2048,128]{1,0:T(8,128)(2,1)S(1)} %pad_maximum_fusion.1.refs_6_), channel_id=1, source_target_pairs={{0,4},{4,8},{8,12},{12,0},{1,5},{5,9},{9,13},{13,1},{2,6},{6,10},{... | collective-permute-start | bytes 1572872 | tf_op jit(solution)/shard_map/ppermute | solution.py:61
  34.4 15.5 %collective-permute-start.4 = (bf16[2048,128]{1,0:T(8,128)(2,1)}, bf16[2048,128]{1,0:T(8,128)(2,1)}, u32[]{:S(2)}, u32[]{:S(2)}) collective-permute-start(bf16[2048,128]{1,0:T(8,128)(2,1)} %constant_dynamic-update-slice_fusion.refs_7_), channel_id=1, source_target_pairs={{0,12},{4,0},{8,4},{12,8},{1,13},{5,1},{9,5},{13,9},{2,14},{6,2},{... | collective-permute-start | bytes 1572872 | tf_op jit(solution)/shard_map/ppermute | solution.py:63
  37.9 21.0 %collective-permute-start.15 = (bf16[2048,128]{1,0:T(8,128)(2,1)S(1)}, bf16[2048,128]{1,0:T(8,128)(2,1)}, u32[]{:S(2)}, u32[]{:S(2)}) collective-permute-start(bf16[2048,128]{1,0:T(8,128)(2,1)S(1)} %pad_maximum_fusion.1.refs_6_), channel_id=1, source_target_pairs={{0,12},{4,0},{8,4},{12,8},{1,13},{5,1},{9,5},{13,9},{2,14},{6,2},{... | collective-permute-start | bytes 1572872 | tf_op jit(solution)/shard_map/ppermute | solution.py:62
  39.7 21.1 %collective-permute-start.10 = (bf16[2048,128]{1,0:T(8,128)(2,1)}, bf16[2048,128]{1,0:T(8,128)(2,1)}, u32[]{:S(2)}, u32[]{:S(2)}) collective-permute-start(bf16[2048,128]{1,0:T(8,128)(2,1)} %constant_dynamic-update-slice_fusion.3.refs_1_), channel_id=1, source_target_pairs={{0,1},{1,2},{2,3},{3,0},{4,5},{5,6},{6,7},{7,4},{8,9},{9,10},{10,1... | collective-permute-start | bytes 1572872 | tf_op jit(solution)/shard_map/ppermute | solution.py:64
  40.6 22.2 %collective-permute-start.12 = (bf16[2048,128]{1,0:T(8,128)(2,1)}, bf16[2048,128]{1,0:T(8,128)(2,1)}, u32[]{:S(2)}, u32[]{:S(2)}) collective-permute-start(bf16[2048,128]{1,0:T(8,128)(2,1)} %constant_dynamic-update-slice_fusion.3.refs_1_), channel_id=1, source_target_pairs={{0,3},{1,0},{2,1},{3,2},{4,7},{5,4},{6,5},{7,6},{8,11},{9,8},{10,9... | collective-permute-start | bytes 1572872 | tf_op jit(solution)/shard_map/ppermute | solution.py:63
  49.9 16.2 %collective-permute-start.14 = (bf16[2048,128]{1,0:T(8,128)(2,1)}, bf16[2048,128]{1,0:T(8,128)(2,1)}, u32[]{:S(2)}, u32[]{:S(2)}) collective-permute-start(bf16[2048,128]{1,0:T(8,128)(2,1)} %constant_dynamic-update-slice_fusion.refs_7_), channel_id=1, source_target_pairs={{0,4},{4,8},{8,12},{12,0},{1,5},{5,9},{9,13},{13,1},{2,6},{6,10},{... | collective-permute-start | bytes 1572872 | tf_op jit(solution)/shard_map/ppermute | solution.py:64
  58.8 16.7 %collective-permute-start.16 = (bf16[2048,128]{1,0:T(8,128)(2,1)}, bf16[2048,128]{1,0:T(8,128)(2,1)S(1)}, u32[]{:S(2)}, u32[]{:S(2)}) collective-permute-start(bf16[2048,128]{1,0:T(8,128)(2,1)} %copy-done.22), channel_id=1, source_target_pairs={{0,1},{1,2},{2,3},{3,0},{4,5},{5,6},{6,7},{7,4},{8,9},{9,10},{10,1... | collective-permute-start | bytes 1572872 | tf_op jit(solution)/shard_map/ppermute | solution.py:69
  58.9 16.7 %collective-permute-start.18 = (bf16[2048,128]{1,0:T(8,128)(2,1)}, bf16[2048,128]{1,0:T(8,128)(2,1)S(1)}, u32[]{:S(2)}, u32[]{:S(2)}) collective-permute-start(bf16[2048,128]{1,0:T(8,128)(2,1)} %collective-permute-done.13.refs_8_), channel_id=1, source_target_pairs={{0,4},{4,8},{8,12},{12,0},{1,5},{5,9},{9,13},{13,1},{2,6},{6,10},{... | collective-permute-start | bytes 1572872 | tf_op jit(solution)/shard_map/ppermute | solution.py:69
  60.9 14.7 %collective-permute-start.19 = (bf16[2048,128]{1,0:T(8,128)(2,1)}, bf16[2048,128]{1,0:T(8,128)(2,1)S(1)}, u32[]{:S(2)}, u32[]{:S(2)}) collective-permute-start(bf16[2048,128]{1,0:T(8,128)(2,1)} %collective-permute-done.4.refs_11_), channel_id=1, source_target_pairs={{0,12},{4,0},{8,4},{12,8},{1,13},{5,1},{9,5},{13,9},{2,14},{6,2},{... | collective-permute-start | bytes 1572872 | tf_op jit(solution)/shard_map/ppermute | solution.py:69
  62.8 12.8 %collective-permute-start.17 = (bf16[2048,128]{1,0:T(8,128)(2,1)}, bf16[2048,128]{1,0:T(8,128)(2,1)S(1)}, u32[]{:S(2)}, u32[]{:S(2)}) collective-permute-start(bf16[2048,128]{1,0:T(8,128)(2,1)} %collective-permute-done.12.refs_5_), channel_id=1, source_target_pairs={{0,3},{1,0},{2,1},{3,2},{4,7},{5,4},{6,5},{7,6},{8,11},{9,8},{10,9... | collective-permute-start | bytes 1572872 | tf_op jit(solution)/shard_map/ppermute | solution.py:69
  85.0 50.5 %all-to-all-start = ((bf16[8,464,256]{2,1,0:T(8,128)(2,1)}), bf16[8,464,256]{2,1,0:T(8,128)(2,1)S(1)}, u32[]{:S(2)}, u32[]{:S(2)}) async-start(bf16[8,464,256]{2,1,0:T(8,128)(2,1)} %get-tuple-element.22), calls=%async_computation | async-start | bytes 3801088 | tf_op jit(solution)/shard_map/all_to_all | solution.py:462
  107.3 45.0 %collective-permute-start.31 = (bf16[512,1024]{1,0:T(8,128)(2,1)}, bf16[512,1024]{1,0:T(8,128)(2,1)S(1)}, u32[]{:S(2)}, u32[]{:S(2)}) collective-permute-start(bf16[512,1024]{1,0:T(8,128)(2,1)} %constant_dynamic-update-slice_fusion.6.refs_0_), channel_id=1, source_target_pairs={{0,1},{1,2},{2,3},{3,0},{4,5},{5,6},{6,7},{7,4},{8,9},{9,10},{10,1... | collective-permute-start | bytes 3145736 | tf_op jit(solution)/shard_map/ppermute | solution.py:49
  107.3 45.8 %collective-permute-start.32 = (bf16[512,1024]{1,0:T(8,128)(2,1)}, bf16[512,1024]{1,0:T(8,128)(2,1)}, u32[]{:S(2)}, u32[]{:S(2)}) collective-permute-start(bf16[512,1024]{1,0:T(8,128)(2,1)} %constant_dynamic-update-slice_fusion.6.refs_0_), channel_id=1, source_target_pairs={{0,3},{1,0},{2,1},{3,2},{4,7},{5,4},{6,5},{7,6},{8,11},{9,8},{10,9... | collective-permute-start | bytes 3145736 | tf_op jit(solution)/shard_map/ppermute | solution.py:50
  112.1 13.1 %collective-permute-start.22 = (bf16[384,256]{1,0:T(8,128)(2,1)}, bf16[384,256]{1,0:T(8,128)(2,1)S(1)}, u32[]{:S(2)}, u32[]{:S(2)}) collective-permute-start(bf16[384,256]{1,0:T(8,128)(2,1)} %get-tuple-element.26), channel_id=1, source_target_pairs={{0,48},{16,64},{32,80},{48,96},{64,112},{80,0},{96,16},{112,32},{1... | collective-permute-start | bytes 589832 | tf_op jit(solution)/shard_map/ppermute | solution.py:465
  118.4 10.8 %collective-permute-start.23 = (bf16[384,256]{1,0:T(8,128)(2,1)}, bf16[384,256]{1,0:T(8,128)(2,1)S(1)}, u32[]{:S(2)}, u32[]{:S(2)}) collective-permute-start(bf16[384,256]{1,0:T(8,128)(2,1)} %get-tuple-element.27), channel_id=1, source_target_pairs={{0,64},{16,80},{32,96},{48,112},{64,0},{80,16},{96,32},{112,48},{1... | collective-permute-start | bytes 589832 | tf_op jit(solution)/shard_map/ppermute | solution.py:465
  147.5 15.4 %all-to-all-start.1 = ((bf16[8,4,64,128]{3,2,1,0:T(8,128)(2,1)}), bf16[8,4,64,128]{3,2,1,0:T(8,128)(2,1)}, u32[]{:S(2)}, u32[]{:S(2)}) async-start(bf16[8,4,64,128]{3,2,1,0:T(8,128)(2,1)} %attend_early.1), calls=%async_computation.1 | async-start | bytes 1048576 | tf_op jit(solution)/shard_map/all_to_all | solution.py:500
  151.8 35.8 %collective-permute-start.35 = (bf16[512,1024]{1,0:T(8,128)(2,1)}, bf16[512,1024]{1,0:T(8,128)(2,1)}, u32[]{:S(2)}, u32[]{:S(2)}) collective-permute-start(bf16[512,1024]{1,0:T(8,128)(2,1)} %constant_dynamic-update-slice_fusion.6.refs_0_), channel_id=1, source_target_pairs={{0,16},{16,0},{32,48},{48,32},{64,80},{80,64},{96,112},{112,96},{1... | collective-permute-start | bytes 3145736 | tf_op jit(solution)/shard_map/ppermute | solution.py:471
  153.2 15.4 %collective-permute-start.33 = (bf16[256,1024]{1,0:T(8,128)(2,1)}, bf16[256,1024]{1,0:T(8,128)(2,1)}, u32[]{:S(2)}, u32[]{:S(2)}) collective-permute-start(bf16[256,1024]{1,0:T(8,128)(2,1)} %slice.51), channel_id=1, source_target_pairs={{0,1},{1,2},{2,3},{3,0},{4,5},{5,6},{6,7},{7,4},{8,9},{9,10},{10,1... | collective-permute-start | bytes 1572872 | tf_op jit(solution)/shard_map/ppermute | solution.py:52
  155.1 14.6 %collective-permute-start.34 = (bf16[256,1024]{1,0:T(8,128)(2,1)}, bf16[256,1024]{1,0:T(8,128)(2,1)}, u32[]{:S(2)}, u32[]{:S(2)}) collective-permute-start(bf16[256,1024]{1,0:T(8,128)(2,1)} %slice.52), channel_id=1, source_target_pairs={{0,3},{1,0},{2,1},{3,2},{4,7},{5,4},{6,5},{7,6},{8,11},{9,8},{10,9... | collective-permute-start | bytes 1572872 | tf_op jit(solution)/shard_map/ppermute | solution.py:53
  158.3 29.3 %collective-permute-start.36 = (bf16[512,1024]{1,0:T(8,128)(2,1)S(1)}, bf16[512,1024]{1,0:T(8,128)(2,1)}, u32[]{:S(2)}, u32[]{:S(2)}) collective-permute-start(bf16[512,1024]{1,0:T(8,128)(2,1)S(1)} %collective-permute-done.31.refs_1_), channel_id=1, source_target_pairs={{0,16},{16,0},{32,48},{48,32},{64,80},{80,64},{96,112},{112,96},{1... | collective-permute-start | bytes 3145736 | tf_op jit(solution)/shard_map/ppermute | solution.py:471
  158.3 29.3 %collective-permute-start.37 = (bf16[512,1024]{1,0:T(8,128)(2,1)}, bf16[512,1024]{1,0:T(8,128)(2,1)}, u32[]{:S(2)}, u32[]{:S(2)}) collective-permute-start(bf16[512,1024]{1,0:T(8,128)(2,1)} %collective-permute-done.32.refs_2_), channel_id=1, source_target_pairs={{0,16},{16,0},{32,48},{48,32},{64,80},{80,64},{96,112},{112,96},{1... | collective-permute-start | bytes 3145736 | tf_op jit(solution)/shard_map/ppermute | solution.py:471
  162.9 14.9 %all-to-all-start.2 = ((bf16[8,4,64,128]{3,2,1,0:T(8,128)(2,1)}), bf16[8,4,64,128]{3,2,1,0:T(8,128)(2,1)S(1)}, u32[]{:S(2)}, u32[]{:S(2)}) async-start(bf16[8,4,64,128]{3,2,1,0:T(8,128)(2,1)} %attend_late.1), calls=%async_computation.2 | async-start | bytes 1048576 | tf_op jit(solution)/shard_map/all_to_all | solution.py:489
  168.5 19.1 %collective-permute-start.38 = (bf16[256,1024]{1,0:T(8,128)(2,1)}, bf16[256,1024]{1,0:T(8,128)(2,1)S(1)}, u32[]{:S(2)}, u32[]{:S(2)}) collective-permute-start(bf16[256,1024]{1,0:T(8,128)(2,1)} %collective-permute-done.33.refs_3_), channel_id=1, source_target_pairs={{0,16},{16,0},{32,48},{48,32},{64,80},{80,64},{96,112},{112,96},{1... | collective-permute-start | bytes 1572872 | tf_op jit(solution)/shard_map/ppermute | solution.py:471
  169.7 17.9 %collective-permute-start.39 = (bf16[256,1024]{1,0:T(8,128)(2,1)}, bf16[256,1024]{1,0:T(8,128)(2,1)}, u32[]{:S(2)}, u32[]{:S(2)}) collective-permute-start(bf16[256,1024]{1,0:T(8,128)(2,1)} %collective-permute-done.34.refs_4_), channel_id=1, source_target_pairs={{0,16},{16,0},{32,48},{48,32},{64,80},{80,64},{96,112},{112,96},{1... | collective-permute-start | bytes 1572872 | tf_op jit(solution)/shard_map/ppermute | solution.py:471
  182.0 16.8 %all-to-all-start.3 = ((bf16[16,128,128]{2,1,0:T(8,128)(2,1)}), bf16[16,128,128]{2,1,0:T(8,128)(2,1)S(1)}, u32[]{:S(2)}, u32[]{:S(2)}) async-start(bf16[16,128,128]{2,1,0:T(8,128)(2,1)} %bitcast.9), calls=%async_computation.3 | async-start | bytes 1048576 | tf_op jit(solution)/shard_map/all_to_all | solution.py:511
  (43 other events, 439.3 us)
where the time goes:
time: 205 us; the launch traced here: 204 us
  starting transfers between devices  68.5 us (33%)
  waiting for transfers between devices  57 us (28%)
  Pallas kernels  40.4 us (20%)
  local copies, waits for them, and re-layouts  34.7 us (17%)
  other arithmetic  3.18 us (2%)
    unnamed x71, local copies, waits for them, and re-layouts  24.8 us
    ppermute x7, waiting for transfers between devices, sublayer(): lax.ppermute(rest[d], 'seq', [(i, (i + d) % SEQ) for i in range(SEQ)])  15.1 us
    all_to_all x1, waiting for transfers between devices, sublayer(): lax.all_to_all(taken.reshape(HEADS, HD, HD), ('hx', 'hz'), 0, 0, tiled=True)  11.1 us
    ppermute x4, starting transfers between devices, ring_gather(): ahead = lax.ppermute(piece, axis, ring(-1))  11 us
    ppermute x4, waiting for transfers between devices, ring_gather(): back = lax.ppermute(piece, axis, ring(1))  11 us
    ppermute x4, starting transfers between devices, ring_gather(): far_high = lax.ppermute(ahead[half:], axis, ring(-1))  10.7 us
    pallas_call x1, Pallas kernels, sublayer(): pl.pallas_call(project_far, out_shape=(pltpu.HBM((SEQ, SENT, 2 * HD), BF)...  8.59 us
    all_to_all x1, waiting for transfers between devices, sublayer(): late = lax.all_to_all(late, 'seq', 0, 0, tiled=True).reshape(ROWS // 2, HD)  8.04 us
  transfers between devices with their start and end apart: 44, of which 15 were waited for; matrix products, arithmetic and copies ran while one was open for 10% of the time, Pallas kernels for 13%

commit v1 on v0

--- a/solution.py
+++ b/solution.py
@@ -45,12 +45,16 @@
     return [(i, (i + by) % SIDE) for i in range(SIDE)]
 
 
+def shift(piece, axis, by):
+    return lax.ppermute(piece, axis, ring(by))
+
+
 def ring_gather(piece, axis):
-    back = lax.ppermute(piece, axis, ring(1))
-    ahead = lax.ppermute(piece, axis, ring(-1))
+    back = shift(piece, axis, 1)
+    ahead = shift(piece, axis, -1)
     half = piece.shape[0] // 2
-    far_low = lax.ppermute(back[:half], axis, ring(1))
-    far_high = lax.ppermute(ahead[half:], axis, ring(-1))
+    far_low = shift(back[:half], axis, 1)
+    far_high = shift(ahead[half:], axis, -1)
     return back, ahead, far_low, far_high
 
 
@@ -58,15 +62,15 @@
     back, ahead, far_low, far_high = ring_gather(part, first)
     low = jnp.concatenate([part, back], 0)
     high = jnp.concatenate([ahead, far_low, far_high], 0)
-    back_low = lax.ppermute(low, second, ring(1))
-    ahead_low = lax.ppermute(low, second, ring(-1))
-    ahead_high = lax.ppermute(high, second, ring(-1))
-    back_high = lax.ppermute(high, second, ring(1))
+    back_low = shift(low, second, 1)
+    ahead_low = shift(low, second, -1)
+    ahead_high = shift(high, second, -1)
+    back_high = shift(high, second, 1)
     return low, high, back_low, back_high, ahead_low, ahead_high
 
 
 def gather_far(near, second):
-    return lax.ppermute(near[2], second, ring(1)), lax.ppermute(near[5], second, ring(-1))
+    return (shift(near[2], second, 1), shift(near[5], second, -1))
 
 
 def wrap(index, by):
@@ -155,7 +159,7 @@
     lax.fori_loop(0, TOK // 16, step, 0)
 
 
-def project_far(place_ref, index_ref, wq, wk, wv, told, acc, own_in, a0, a1, b0, b1, *refs):
+def project_far(place_ref, index_ref, wq, wk, wv, told_ref, acc, own_in, a0, a1, b0, b1, *refs):
     out_ref, rest_refs, own_ref = refs[0], refs[1 : 1 + SEQ], refs[1 + SEQ]
     wa, wb, rows, pad, full, rest, sems, rest_sems = refs[2 + SEQ :]
     a, b = piece_list((a0, a1), OFFSETS[3:]), piece_list((b0, b1), OFFSETS[3:])
@@ -170,6 +174,7 @@
         start = pl.multiple_of(at.start * LINE, LINE)
         for k in range(3):
             flat[pl.ds(start + k, TILE, stride=LINE), :] = total[:, k * HD : (k + 1) * HD]
+        flat[pl.ds(start + 3, TILE, stride=LINE), :] = told_ref[at, :]
 
     multiply(a, 0, wa, finish)
     multiply(b, HALF, wb, finish)
@@ -190,6 +195,31 @@
     def queries(o, b):
         return jnp.concatenate([line(o, b, 0), line(o, b + 1, 0)], 1)
 
+    lane = lax.broadcasted_iota(jnp.int32, (MOST, HD), 1)
+    slot = lax.broadcasted_iota(jnp.int32, (MOST, HD), 0)
+
+    def told(o, b, shift):
+        at = (o * BLK + b) * MOST * LINE + 3
+        return jnp.where(lane == slot + shift, flat[pl.ds(at, MOST, stride=LINE), :], 0.0)
+
+    def told_pair(o, b):
+        return jnp.sum(told(o, b, 0) + told(o, b + 1, MOST), axis=0, keepdims=True)
+
+    def digits(o):
+        halo = told(o, -1, 0) if o else jnp.zeros((MOST, HD), F32)
+        halo = jnp.sum(halo, axis=0, keepdims=True)
+        values = [
+            jnp.concatenate([told_pair(o, 0), told_pair(o, 2)], 1),
+            jnp.concatenate([told_pair(o, 4), told_pair(o, 6)], 1),
+            jnp.concatenate([halo, jnp.zeros_like(halo)], 1),
+        ]
+        high = [jnp.floor(v * (1.0 / 65536)) for v in values]
+        left = [v - h * 65536.0 for v, h in zip(values, high)]
+        middle = [jnp.floor(v * (1.0 / 256)) for v in left]
+        low = [v - m * 256.0 for v, m in zip(left, middle)]
+        unused = jnp.zeros((SENT - TOLD - 9, 2 * HD), F32)
+        return jnp.concatenate(low + middle + high + [unused], 0).astype(BF)
+
     def send(o):
         return pltpu.make_async_copy(full.at[o], out_ref.at[o], sems.at[o])
 
@@ -202,7 +232,7 @@
             put(full, o, n - (MID - 1), line(o, n, 1, 2))
         for n in range(MID, BLK, 2):
             put(full, o, BLK - MID + 1 + (n - MID) // 2, queries(o, n))
-        full[o, TOLD:, :] = told[o]
+        full[o, TOLD:, :] = digits(o)
         send(o).start()
     for o in range(SEQ):
         for n in range(MID - 1):
@@ -218,24 +248,13 @@
         send_rest(d).wait()
 
 
-def place_values(index_ref, value_ref, empty_ref, out_ref):
-    pltpu.sync_copy(empty_ref, out_ref)
-
-    def step(i, carry):
-        for k in range(16):
-            t = i * 16 + k
-            out_ref[index_ref[t]] = value_ref[t]
-        return carry
-
-    lax.fori_loop(0, TOK // 16, step, 0)
-
-
 QT = 128
 
 
 def told_lines(got):
     digits = got[:, TOLD:, :].astype(F32)
     value = digits[:, 0:3] + digits[:, 3:6] * 256.0 + digits[:, 6:9] * 65536.0
+    value = jnp.where(value > 0.0, value - 1.0, float(EMPTY))
     lines = []
     for b in range(-1, BLK):
         row, at = (2, 0) if b < 0 else (b // 4, b % 4 * MOST)
@@ -403,26 +422,13 @@
 
     slots = slot_index.reshape(TOK)
     index = (slots // BLOCK) * MOST + slots % MOST
-    value = cluster_id.reshape(TOK) * POS + seq * TOK + jnp.arange(TOK, dtype=jnp.int32)
+    value = cluster_id * POS + 1 + seq * TOK + lax.broadcasted_iota(jnp.int32, (TOK, 1), 0)
+    told = jnp.broadcast_to(value.astype(F32), (TOK, HD))
 
     near_a = gather_near(tokens[:HALF], "hx", "hz")
     near_b = gather_near(tokens[HALF:], "hz", "hx")
-    tied, _ = lax.optimization_barrier((index, near_b[5]))
-    values = pl.pallas_call(
-        place_values,
-        out_shape=shape((ROWS,), jnp.int32),
-        in_specs=[SMEM, SMEM, pl.BlockSpec(memory_space=pl.ANY)],
-        out_specs=SMEM,
-        name="place_values",
-        cost_estimate=estimate(0, 12),
-    )(tied, value, jnp.full((ROWS,), EMPTY, jnp.int32)).reshape(SEQ, BLK, MOST)
-    halo = jnp.concatenate(
-        [jnp.full((1, MOST), EMPTY, jnp.int32), values[: SEQ - 1, BLK - 1]], 0
-    )
-    halo = jnp.pad(halo, ((0, 0), (0, 2 * HD - MOST)))[:, None]
-    values = jnp.concatenate([values.reshape(SEQ, 2, 2 * HD), halo], 1)
-    told = jnp.concatenate([values & 255, (values >> 8) & 255, values >> 16], 1)
-    told = jnp.pad(told, ((0, 0), (0, SENT - TOLD - 9), (0, 0))).astype(BF)
+    w_half = lax.dynamic_slice_in_dim(w_out, core * (WIDTH // 2), WIDTH // 2, 1)
+    w_row = (w_half,) + ring_gather(w_half, "hx")
 
     weights = (w_query, w_key, w_value)
     acc, own = pl.pallas_call(
@@ -464,9 +470,8 @@
     for d in range(1, SEQ):
         parts.append(lax.ppermute(rest[d], "seq", [(i, (i + d) % SEQ) for i in range(SEQ)]))
 
-    w_half = lax.dynamic_slice_in_dim(w_out, core * (WIDTH // 2), WIDTH // 2, 1)
-    w_half, _ = lax.optimization_barrier((w_half, own))
-    w_row = jnp.concatenate((w_half,) + ring_gather(w_half, "hx"), 0)
+    w_row, _ = lax.optimization_barrier((w_row, own))
+    w_row = jnp.concatenate(w_row, 0)
     w_near = (w_row,) + ring_gather(w_row, "hz")
     w_far = tuple(lax.ppermute(w, "seq", [(i, i ^ 1) for i in range(SEQ)]) for w in w_near)
 

time: 205 us -> 196 us (0.956)
  local copies, waits for them, and re-layouts: 34.7 us -> 27.8 us
  Pallas kernels: 40.4 us -> 34.8 us
  waiting for transfers between devices: 57 us -> 62.2 us
  other arithmetic: 3.18 us -> 0.18 us
    ppermute x28, waiting for transfers between devices: 22.7 us -> 33.1 us  [shift(): return lax.ppermute(piece, axis, ring(by))]
    pallas_call x1 -> x0, Pallas kernels: 6.19 us -> none  [sublayer(): pl.pallas_call(place_values, out_shape=shape((ROWS,), jnp.int32), in_spec...]
    ppermute x7, waiting for transfers between devices: 15.1 us -> 11.2 us  [sublayer(): lax.ppermute(rest[d], 'seq', [(i, (i + d) % SEQ) for i in range(SEQ)])]
    unnamed x71 -> x76, local copies, waits for them, and re-layouts: 24.8 us -> 21.6 us
    slice x10 -> x9, local copies, waits for them, and re-layouts: 5.76 us -> 3.97 us  [the longest x4 1.92 us: ring_gather(): far_high = shift(ahead[half:], axis, -1)]
  transfers between devices with their start and end apart: 44 -> 44, of which waited for: 15 -> 18; matrix products, arithmetic and copies ran while one was open for 10% -> 5% of each run, Pallas kernels for 13% -> 10%
where the time goes in v1:
time: 196 us; the launch traced here: 195 us
  starting transfers between devices  69.3 us (35%)
  waiting for transfers between devices  62.2 us (32%)
  Pallas kernels  34.8 us (18%)
  local copies, waits for them, and re-layouts  27.8 us (14%)
    ppermute x28, starting transfers between devices, shift(): return lax.ppermute(piece, axis, ring(by))  42.9 us
    ppermute x28, waiting for transfers between devices, shift(): return lax.ppermute(piece, axis, ring(by))  33.1 us
    unnamed x76, local copies, waits for them, and re-layouts  21.6 us
    ppermute x7, waiting for transfers between devices, sublayer(): lax.ppermute(rest[d], 'seq', [(i, (i + d) % SEQ) for i in range(SEQ)])  11.2 us
    all_to_all x1, waiting for transfers between devices, sublayer(): lax.all_to_all(taken.reshape(HEADS, HD, HD), ('hx', 'hz'), 0, 0, tiled=True)  11.1 us
    pallas_call x1, Pallas kernels, sublayer(): pl.pallas_call(project_far, out_shape=(pltpu.HBM((SEQ, SENT, 2 * HD), BF)...  9.08 us
    pallas_call x1, Pallas kernels, sublayer(): pl.pallas_call(project_near, out_shape=(shape((TOK, 3 * HD), F32), shape(...  7.38 us
    all_to_all x1, waiting for transfers between devices, sublayer(): late = lax.all_to_all(late, 'seq', 0, 0, tiled=True).reshape(ROWS // 2, HD)  6.76 us
  transfers between devices with their start and end apart: 44, of which 18 were waited for; matrix products, arithmetic and copies ran while one was open for 5% of the time, Pallas kernels for 10%

profile of v1, /device:TPU:0, one launch (start us, length us, event | category | flops | bytes accessed | tf_op | source)
XLA Modules:
  0.0 194.8 jit_solution(2260671420685539720)
XLA Ops:
  6.5 2.1 %collective-permute-start.9 = (bf16[1024,128]{1,0:T(8,128)(2,1)S(1)}, bf16[1024,128]{1,0:T(8,128)(2,1)S(1)}, u32[]{:S(2)}, u32[]{:S(2)}) collective-permute-start(bf16[1024,128]{1,0:T(8,128)(2,1)S(1)} %get-tuple-element.39), channel_id=1, source_target_pairs={{0,3},{1,0},{2,1},{3,2},{4,7},{5,4},{6,5},{7,6},{8,11},{9,8},{10,9... | collective-permute-start | bytes 786440 | tf_op jit(solution)/shard_map/ppermute | solution.py:49
  10.4 2.2 %collective-permute-start.4 = (bf16[2048,128]{1,0:T(8,128)(2,1)S(1)}, bf16[2048,128]{1,0:T(8,128)(2,1)S(1)}, u32[]{:S(2)}, u32[]{:S(2)}) collective-permute-start(bf16[2048,128]{1,0:T(8,128)(2,1)S(1)} %pad_maximum_fusion.refs_0_), channel_id=1, source_target_pairs={{0,1},{1,2},{2,3},{3,0},{4,5},{5,6},{6,7},{7,4},{8,9},{9,10},{10,1... | collective-permute-start | bytes 1572872 | tf_op jit(solution)/shard_map/ppermute | solution.py:49
  12.6 2.2 %collective-permute-start.6 = (bf16[2048,128]{1,0:T(8,128)(2,1)S(1)}, bf16[2048,128]{1,0:T(8,128)(2,1)S(1)}, u32[]{:S(2)}, u32[]{:S(2)}) collective-permute-start(bf16[2048,128]{1,0:T(8,128)(2,1)S(1)} %pad_maximum_fusion.refs_0_), channel_id=1, source_target_pairs={{0,3},{1,0},{2,1},{3,2},{4,7},{5,4},{6,5},{7,6},{8,11},{9,8},{10,9... | collective-permute-start | bytes 1572872 | tf_op jit(solution)/shard_map/ppermute | solution.py:49
  15.2 3.0 %collective-permute-start.3 = (bf16[512,128]{1,0:T(8,128)(2,1)S(1)}, bf16[512,128]{1,0:T(8,128)(2,1)S(1)}, u32[]{:S(2)}, u32[]{:S(2)}) collective-permute-start(bf16[512,128]{1,0:T(8,128)(2,1)S(1)} %slice.41), channel_id=1, source_target_pairs={{0,12},{4,0},{8,4},{12,8},{1,13},{5,1},{9,5},{13,9},{2,14},{6,2},{... | collective-permute-start | bytes 393224 | tf_op jit(solution)/shard_map/ppermute | solution.py:49
  21.7 2.1 %collective-permute-start.11 = (bf16[512,128]{1,0:T(8,128)(2,1)S(1)}, bf16[512,128]{1,0:T(8,128)(2,1)S(1)}, u32[]{:S(2)}, u32[]{:S(2)}) collective-permute-start(bf16[512,128]{1,0:T(8,128)(2,1)S(1)} %slice.43), channel_id=1, source_target_pairs={{0,3},{1,0},{2,1},{3,2},{4,7},{5,4},{6,5},{7,6},{8,11},{9,8},{10,9... | collective-permute-start | bytes 393224 | tf_op jit(solution)/shard_map/ppermute | solution.py:49
  24.5 4.1 %collective-permute-done.10 = bf16[512,128]{1,0:T(8,128)(2,1)S(1)} collective-permute-done((bf16[512,128]{1,0:T(8,128)(2,1)S(1)}, bf16[512,128]{1,0:T(8,128)(2,1)S(1)}, u32[]{:S(2)}, u32[]{:S(2)}) %collective-permute-start.10) | collective-permute-done | bytes 131104 | tf_op jit(solution)/shard_map/ppermute | solution.py:49
  31.5 3.2 %collective-permute-start.7 = (bf16[2048,128]{1,0:T(8,128)(2,1)}, bf16[2048,128]{1,0:T(8,128)(2,1)}, u32[]{:S(2)}, u32[]{:S(2)}) collective-permute-start(bf16[2048,128]{1,0:T(8,128)(2,1)} %constant_dynamic-update-slice_fusion.refs_1_), channel_id=1, source_target_pairs={{0,3},{1,0},{2,1},{3,2},{4,7},{5,4},{6,5},{7,6},{8,11},{9,8},{10,9... | collective-permute-start | bytes 1572872 | tf_op jit(solution)/shard_map/ppermute | solution.py:49
  37.6 5.9 %collective-permute-done.14.refs_10_ = bf16[2048,128]{1,0:T(8,128)(2,1)} collective-permute-done((bf16[2048,128]{1,0:T(8,128)(2,1)S(1)}, bf16[2048,128]{1,0:T(8,128)(2,1)}, u32[]{:S(2)}, u32[]{:S(2)}) %collective-permute-start.14) | collective-permute-done | bytes 524320 | tf_op jit(solution)/shard_map/ppermute | solution.py:49
  43.5 2.3 %collective-permute-done.5.refs_3_ = bf16[2048,128]{1,0:T(8,128)(2,1)} collective-permute-done((bf16[2048,128]{1,0:T(8,128)(2,1)}, bf16[2048,128]{1,0:T(8,128)(2,1)}, u32[]{:S(2)}, u32[]{:S(2)}) %collective-permute-start.5) | collective-permute-done | bytes 524320 | tf_op jit(solution)/shard_map/ppermute | solution.py:49
  47.9 4.4 %collective-permute-done.15.refs_11_ = bf16[2048,128]{1,0:T(8,128)(2,1)} collective-permute-done((bf16[2048,128]{1,0:T(8,128)(2,1)}, bf16[2048,128]{1,0:T(8,128)(2,1)}, u32[]{:S(2)}, u32[]{:S(2)}) %collective-permute-start.15) | collective-permute-done | bytes 524320 | tf_op jit(solution)/shard_map/ppermute | solution.py:49
  52.3 2.7 %collective-permute-start.19 = (bf16[2048,128]{1,0:T(8,128)(2,1)}, bf16[2048,128]{1,0:T(8,128)(2,1)S(1)}, u32[]{:S(2)}, u32[]{:S(2)}) collective-permute-start(bf16[2048,128]{1,0:T(8,128)(2,1)} %collective-permute-done.15.refs_11_), channel_id=1, source_target_pairs={{0,12},{4,0},{8,4},{12,8},{1,13},{5,1},{9,5},{13,9},{2,14},{6,2},{... | collective-permute-start | bytes 1572872 | tf_op jit(solution)/shard_map/ppermute | solution.py:49
  57.1 7.4 %project_near.1 = (f32[2048,384]{1,0:T(8,128)S(1)}, bf16[128,2048]{1,0:T(8,128)(2,1)S(1)}) custom-call(s32[4]{0:T(128)S(1)} %pad_add_fusion.place_ref, bf16[2048,128]{1,0:T(8,128)(2,1)S(1)} %copy-done.1, bf16[2048,128]{1,0:T(8,128)(2,1)S(1)} %copy-done.2, bf16[2048,128]{1,0:T(8,128)(2,1)S(1)} %copy-done.3, bf16[2048,128]{1,0:T(8,128)(2,1)S(1)} %pad_maximum_fusion.refs_0_, ...), custom_call_target="tpu_custom_call" | custom-call | flops 2415919104 | bytes 10485760 | tf_op jit(solution)/shard_map/project_near/pallas_call | solution.py:434
  64.9 9.1 %project_far.1 = (bf16[8,464,256]{2,1,0:T(8,128)(2,1)}, bf16[384,256]{1,0:T(8,128)(2,1)}, bf16[384,256]{1,0:T(8,128)(2,1)}, bf16[384,256]{1,0:T(8,128)(2,1)}, bf...) custom-call(s32[4]{0:T(128)S(1)} %pad_add_fusion.place_ref, ...), custom_call_target="tpu_custom_call" | custom-call | flops 805306368 | bytes 25165824 | tf_op jit(solution)/shard_map/project_far/pallas_call | solution.py:446
  74.8 4.5 %all-to-all-start = ((bf16[8,464,256]{2,1,0:T(8,128)(2,1)}), bf16[8,464,256]{2,1,0:T(8,128)(2,1)S(1)}, u32[]{:S(2)}, u32[]{:S(2)}) async-start(bf16[8,464,256]{2,1,0:T(8,128)(2,1)} %get-tuple-element.24), calls=%async_computation | async-start | bytes 3801088 | tf_op jit(solution)/shard_map/all_to_all | solution.py:468
  79.5 3.2 %collective-permute-start.28 = (bf16[128,1024]{1,0:T(8,128)(2,1)S(1)}, bf16[128,1024]{1,0:T(8,128)(2,1)S(1)}, u32[]{:S(2)}, u32[]{:S(2)}) collective-permute-start(bf16[128,1024]{1,0:T(8,128)(2,1)S(1)} %constant_dynamic-slice_fusion), channel_id=1, source_target_pairs={{0,12},{4,0},{8,4},{12,8},{1,13},{5,1},{9,5},{13,9},{2,14},{6,2},{... | collective-permute-start | bytes 786440 | tf_op jit(solution)/shard_map/ppermute | solution.py:49
  82.7 6.9 %collective-permute-done.27 = bf16[128,1024]{1,0:T(8,128)(2,1)S(1)} collective-permute-done((bf16[128,1024]{1,0:T(8,128)(2,1)S(1)}, bf16[128,1024]{1,0:T(8,128)(2,1)S(1)}, u32[]{:S(2)}, u32[]{:S(2)}) %collective-permute-start.27) | collective-permute-done | bytes 262176 | tf_op jit(solution)/shard_map/ppermute | solution.py:49
  89.7 3.3 %collective-permute-start.30 = (bf16[64,1024]{1,0:T(8,128)(2,1)S(1)}, bf16[64,1024]{1,0:T(8,128)(2,1)S(1)}, u32[]{:S(2)}, u32[]{:S(2)}) collective-permute-start(bf16[64,1024]{1,0:T(8,128)(2,1)S(1)} %slice.45), channel_id=1, source_target_pairs={{0,12},{4,0},{8,4},{12,8},{1,13},{5,1},{9,5},{13,9},{2,14},{6,2},{... | collective-permute-start | bytes 393224 | tf_op jit(solution)/shard_map/ppermute | solution.py:49
  93.0 3.1 %collective-permute-done.29 = bf16[64,1024]{1,0:T(8,128)(2,1)S(1)} collective-permute-done((bf16[64,1024]{1,0:T(8,128)(2,1)S(1)}, bf16[64,1024]{1,0:T(8,128)(2,1)S(1)}, u32[]{:S(2)}, u32[]{:S(2)}) %collective-permute-start.29) | collective-permute-done | bytes 131104 | tf_op jit(solution)/shard_map/ppermute | solution.py:49
  99.6 3.2 %collective-permute-start.32 = (bf16[512,1024]{1,0:T(8,128)(2,1)}, bf16[512,1024]{1,0:T(8,128)(2,1)}, u32[]{:S(2)}, u32[]{:S(2)}) collective-permute-start(bf16[512,1024]{1,0:T(8,128)(2,1)} %constant_dynamic-update-slice_fusion.6.refs_0_), channel_id=1, source_target_pairs={{0,3},{1,0},{2,1},{3,2},{4,7},{5,4},{6,5},{7,6},{8,11},{9,8},{10,9... | collective-permute-start | bytes 3145736 | tf_op jit(solution)/shard_map/ppermute | solution.py:49
  108.7 2.8 %collective-permute-done.21.refs_2_ = bf16[384,256]{1,0:T(8,128)(2,1)S(1)} collective-permute-done((bf16[384,256]{1,0:T(8,128)(2,1)S(1)}, bf16[384,256]{1,0:T(8,128)(2,1)S(1)}, u32[]{:S(2)}, u32[]{:S(2)}) %collective-permute-start.21) | collective-permute-done | bytes 196640 | tf_op jit(solution)/shard_map/ppermute | solution.py:471
  116.5 4.0 %collective-permute-done.23.refs_4_ = bf16[384,256]{1,0:T(8,128)(2,1)S(1)} collective-permute-done((bf16[384,256]{1,0:T(8,128)(2,1)S(1)}, bf16[384,256]{1,0:T(8,128)(2,1)S(1)}, u32[]{:S(2)}, u32[]{:S(2)}) %collective-permute-start.23) | collective-permute-done | bytes 196640 | tf_op jit(solution)/shard_map/ppermute | solution.py:471
  132.8 4.6 %attend_early.1 = bf16[8,4,64,128]{3,2,1,0:T(8,128)(2,1)} custom-call(s32[4]{0:T(128)S(1)} %pad_add_fusion.place_ref, bf16[8,464,256]{2,1,0:T(8,128)(2,1)S(1)} %all-to-all-done.got, bf16[384,256]{1,0:T(8,128)(2,1)S(1)} %copy-done.6, bf16[384,256]{1,0:T(8,128)(2,1)S(1)} %copy-done.8, bf16[384,256]{1,0:T(8,128)(2,1)S(1)} %copy-done.10, ...), custom_call_target="tpu_custom_call" | custom-call | flops 1073741824 | bytes 8388608 | tf_op jit(solution)/shard_map/attend_early/pallas_call | solution.py:495
  137.4 4.7 %all-to-all-start.1 = ((bf16[8,4,64,128]{3,2,1,0:T(8,128)(2,1)}), bf16[8,4,64,128]{3,2,1,0:T(8,128)(2,1)}, u32[]{:S(2)}, u32[]{:S(2)}) async-start(bf16[8,4,64,128]{3,2,1,0:T(8,128)(2,1)} %attend_early.1), calls=%async_computation.1 | async-start | bytes 1048576 | tf_op jit(solution)/shard_map/all_to_all | solution.py:505
  146.5 3.2 %collective-permute-start.34 = (bf16[256,1024]{1,0:T(8,128)(2,1)}, bf16[256,1024]{1,0:T(8,128)(2,1)}, u32[]{:S(2)}, u32[]{:S(2)}) collective-permute-start(bf16[256,1024]{1,0:T(8,128)(2,1)} %slice.47), channel_id=1, source_target_pairs={{0,3},{1,0},{2,1},{3,2},{4,7},{5,4},{6,5},{7,6},{8,11},{9,8},{10,9... | collective-permute-start | bytes 1572872 | tf_op jit(solution)/shard_map/ppermute | solution.py:49
  150.2 4.0 %attend_late.1 = bf16[8,4,64,128]{3,2,1,0:T(8,128)(2,1)} custom-call(bf16[8,464,256]{2,1,0:T(8,128)(2,1)S(1)} %all-to-all-done.got), custom_call_target="tpu_custom_call" | custom-call | flops 1073741824 | bytes 6291456 | tf_op jit(solution)/shard_map/attend_late/pallas_call | solution.py:484
  154.2 3.6 %all-to-all-start.2 = ((bf16[8,4,64,128]{3,2,1,0:T(8,128)(2,1)}), bf16[8,4,64,128]{3,2,1,0:T(8,128)(2,1)S(1)}, u32[]{:S(2)}, u32[]{:S(2)}) async-start(bf16[8,4,64,128]{3,2,1,0:T(8,128)(2,1)} %attend_late.1), calls=%async_computation.2 | async-start | bytes 1048576 | tf_op jit(solution)/shard_map/all_to_all | solution.py:494
  157.9 2.3 %collective-permute-done.33.refs_3_ = bf16[256,1024]{1,0:T(8,128)(2,1)} collective-permute-done((bf16[256,1024]{1,0:T(8,128)(2,1)}, bf16[256,1024]{1,0:T(8,128)(2,1)}, u32[]{:S(2)}, u32[]{:S(2)}) %collective-permute-start.33) | collective-permute-done | bytes 524320 | tf_op jit(solution)/shard_map/ppermute | solution.py:49
  161.4 6.8 %all-to-all-done.2 = bf16[8,4,64,128]{3,2,1,0:T(8,128)(2,1)S(1)} async-done(((bf16[8,4,64,128]{3,2,1,0:T(8,128)(2,1)}), bf16[8,4,64,128]{3,2,1,0:T(8,128)(2,1)S(1)}, u32[]{:S(2)}, u32[]{:S(2)}) %all-to-all-start.2) | async-done | bytes 524320 | tf_op jit(solution)/shard_map/all_to_all | solution.py:494
  168.1 4.3 %take_rows.1 = bf16[2048,128]{1,0:T(8,128)(2,1)} custom-call(s32[2048]{0:T(1024)S(1)} %fusion.2.index_ref, bf16[2048,128]{1,0:T(8,128)(2,1)} %bitcast.6.early_ref, bf16[2048,128]{1,0:T(8,128)(2,1)S(1)} %bitcast.9), custom_call_target="tpu_custom_call" | custom-call | bytes 8388608 | tf_op jit(solution)/shard_map/take_rows/pallas_call | solution.py:506
  172.4 5.8 %all-to-all-start.3 = ((bf16[16,128,128]{2,1,0:T(8,128)(2,1)}), bf16[16,128,128]{2,1,0:T(8,128)(2,1)S(1)}, u32[]{:S(2)}, u32[]{:S(2)}) async-start(bf16[16,128,128]{2,1,0:T(8,128)(2,1)} %bitcast.8), calls=%async_computation.3 | async-start | bytes 1048576 | tf_op jit(solution)/shard_map/all_to_all | solution.py:516
  178.2 11.1 %all-to-all-done.3.rows_ref = bf16[16,128,128]{2,1,0:T(8,128)(2,1)S(1)} async-done(((bf16[16,128,128]{2,1,0:T(8,128)(2,1)}), bf16[16,128,128]{2,1,0:T(8,128)(2,1)S(1)}, u32[]{:S(2)}, u32[]{:S(2)}) %all-to-all-start.3) | async-done | bytes 524320 | tf_op jit(solution)/shard_map/all_to_all | solution.py:516
  189.3 5.4 %combine.1 = bf16[128,2048]{1,0:T(8,128)(2,1)} custom-call(s32[4]{0:T(128)S(1)} %pad_add_fusion.place_ref, bf16[16,128,128]{2,1,0:T(8,128)(2,1)S(1)} %all-to-all-done.3.rows_ref, bf16[512,1024]{1,0:T(8,128)(2,1)} %constant_dynamic-update-slice_fusion.6.refs_0_, bf16[512,1024]{1,0:T(8,128)(2,1)S(1)} %collective-permute-done.31.refs_1_, ...), custom_call_target="tpu_custom_call" | custom-call | flops 1073741824 | bytes 10485760 | tf_op jit(solution)/shard_map/combine/pallas_call | solution.py:523
  (157 shorter events, 56.8 us)
Async XLA Ops:
  2.8 12.0 %collective-permute-start.1 = (bf16[1024,128]{1,0:T(8,128)(2,1)S(1)}, bf16[1024,128]{1,0:T(8,128)(2,1)S(1)}, u32[]{:S(2)}, u32[]{:S(2)}) collective-permute-start(bf16[1024,128]{1,0:T(8,128)(2,1)S(1)} %get-tuple-element.40), channel_id=1, source_target_pairs={{0,12},{4,0},{8,4},{12,8},{1,13},{5,1},{9,5},{13,9},{2,14},{6,2},{... | collective-permute-start | bytes 786440 | tf_op jit(solution)/shard_map/ppermute | solution.py:49
  4.4 10.8 %collective-permute-start.8 = (bf16[1024,128]{1,0:T(8,128)(2,1)S(1)}, bf16[1024,128]{1,0:T(8,128)(2,1)S(1)}, u32[]{:S(2)}, u32[]{:S(2)}) collective-permute-start(bf16[1024,128]{1,0:T(8,128)(2,1)S(1)} %get-tuple-element.39), channel_id=1, source_target_pairs={{0,1},{1,2},{2,3},{3,0},{4,5},{5,6},{6,7},{7,4},{8,9},{9,10},{10,1... | collective-permute-start | bytes 786440 | tf_op jit(solution)/shard_map/ppermute | solution.py:49
  6.5 12.6 %collective-permute-start.9 = (bf16[1024,128]{1,0:T(8,128)(2,1)S(1)}, bf16[1024,128]{1,0:T(8,128)(2,1)S(1)}, u32[]{:S(2)}, u32[]{:S(2)}) collective-permute-start(bf16[1024,128]{1,0:T(8,128)(2,1)S(1)} %get-tuple-element.39), channel_id=1, source_target_pairs={{0,3},{1,0},{2,1},{3,2},{4,7},{5,4},{6,5},{7,6},{8,11},{9,8},{10,9... | collective-permute-start | bytes 786440 | tf_op jit(solution)/shard_map/ppermute | solution.py:49
  10.4 21.0 %collective-permute-start.4 = (bf16[2048,128]{1,0:T(8,128)(2,1)S(1)}, bf16[2048,128]{1,0:T(8,128)(2,1)S(1)}, u32[]{:S(2)}, u32[]{:S(2)}) collective-permute-start(bf16[2048,128]{1,0:T(8,128)(2,1)S(1)} %pad_maximum_fusion.refs_0_), channel_id=1, source_target_pairs={{0,1},{1,2},{2,3},{3,0},{4,5},{5,6},{6,7},{7,4},{8,9},{9,10},{10,1... | collective-permute-start | bytes 1572872 | tf_op jit(solution)/shard_map/ppermute | solution.py:49
  12.6 22.1 %collective-permute-start.6 = (bf16[2048,128]{1,0:T(8,128)(2,1)S(1)}, bf16[2048,128]{1,0:T(8,128)(2,1)S(1)}, u32[]{:S(2)}, u32[]{:S(2)}) collective-permute-start(bf16[2048,128]{1,0:T(8,128)(2,1)S(1)} %pad_maximum_fusion.refs_0_), channel_id=1, source_target_pairs={{0,3},{1,0},{2,1},{3,2},{4,7},{5,4},{6,5},{7,6},{8,11},{9,8},{10,9... | collective-permute-start | bytes 1572872 | tf_op jit(solution)/shard_map/ppermute | solution.py:49
  21.1 15.3 %collective-permute-start.12 = (bf16[2048,128]{1,0:T(8,128)(2,1)S(1)}, bf16[2048,128]{1,0:T(8,128)(2,1)}, u32[]{:S(2)}, u32[]{:S(2)}) collective-permute-start(bf16[2048,128]{1,0:T(8,128)(2,1)S(1)} %pad_maximum_fusion.1.refs_6_), channel_id=1, source_target_pairs={{0,4},{4,8},{8,12},{12,0},{1,5},{5,9},{9,13},{13,1},{2,6},{6,10},{... | collective-permute-start | bytes 1572872 | tf_op jit(solution)/shard_map/ppermute | solution.py:49
  28.6 14.9 %collective-permute-start.14 = (bf16[2048,128]{1,0:T(8,128)(2,1)S(1)}, bf16[2048,128]{1,0:T(8,128)(2,1)}, u32[]{:S(2)}, u32[]{:S(2)}) collective-permute-start(bf16[2048,128]{1,0:T(8,128)(2,1)S(1)} %pad_maximum_fusion.1.refs_6_), channel_id=1, source_target_pairs={{0,12},{4,0},{8,4},{12,8},{1,13},{5,1},{9,5},{13,9},{2,14},{6,2},{... | collective-permute-start | bytes 1572872 | tf_op jit(solution)/shard_map/ppermute | solution.py:49
  30.8 15.0 %collective-permute-start.5 = (bf16[2048,128]{1,0:T(8,128)(2,1)}, bf16[2048,128]{1,0:T(8,128)(2,1)}, u32[]{:S(2)}, u32[]{:S(2)}) collective-permute-start(bf16[2048,128]{1,0:T(8,128)(2,1)} %constant_dynamic-update-slice_fusion.refs_1_), channel_id=1, source_target_pairs={{0,1},{1,2},{2,3},{3,0},{4,5},{5,6},{6,7},{7,4},{8,9},{9,10},{10,1... | collective-permute-start | bytes 1572872 | tf_op jit(solution)/shard_map/ppermute | solution.py:49
  31.5 15.4 %collective-permute-start.7 = (bf16[2048,128]{1,0:T(8,128)(2,1)}, bf16[2048,128]{1,0:T(8,128)(2,1)}, u32[]{:S(2)}, u32[]{:S(2)}) collective-permute-start(bf16[2048,128]{1,0:T(8,128)(2,1)} %constant_dynamic-update-slice_fusion.refs_1_), channel_id=1, source_target_pairs={{0,3},{1,0},{2,1},{3,2},{4,7},{5,4},{6,5},{7,6},{8,11},{9,8},{10,9... | collective-permute-start | bytes 1572872 | tf_op jit(solution)/shard_map/ppermute | solution.py:49
  35.5 16.7 %collective-permute-start.15 = (bf16[2048,128]{1,0:T(8,128)(2,1)}, bf16[2048,128]{1,0:T(8,128)(2,1)}, u32[]{:S(2)}, u32[]{:S(2)}) collective-permute-start(bf16[2048,128]{1,0:T(8,128)(2,1)} %constant_dynamic-update-slice_fusion.3.refs_7_), channel_id=1, source_target_pairs={{0,12},{4,0},{8,4},{12,8},{1,13},{5,1},{9,5},{13,9},{2,14},{6,2},{... | collective-permute-start | bytes 1572872 | tf_op jit(solution)/shard_map/ppermute | solution.py:49
  36.4 18.7 %collective-permute-start.13 = (bf16[2048,128]{1,0:T(8,128)(2,1)}, bf16[2048,128]{1,0:T(8,128)(2,1)}, u32[]{:S(2)}, u32[]{:S(2)}) collective-permute-start(bf16[2048,128]{1,0:T(8,128)(2,1)} %constant_dynamic-update-slice_fusion.3.refs_7_), channel_id=1, source_target_pairs={{0,4},{4,8},{8,12},{12,0},{1,5},{5,9},{9,13},{13,1},{2,6},{6,10},{... | collective-permute-start | bytes 1572872 | tf_op jit(solution)/shard_map/ppermute | solution.py:49
  43.5 21.0 %collective-permute-start.16 = (bf16[2048,128]{1,0:T(8,128)(2,1)}, bf16[2048,128]{1,0:T(8,128)(2,1)S(1)}, u32[]{:S(2)}, u32[]{:S(2)}) collective-permute-start(bf16[2048,128]{1,0:T(8,128)(2,1)} %copy-done.21), channel_id=1, source_target_pairs={{0,1},{1,2},{2,3},{3,0},{4,5},{5,6},{6,7},{7,4},{8,9},{9,10},{10,1... | collective-permute-start | bytes 1572872 | tf_op jit(solution)/shard_map/ppermute | solution.py:49
  45.8 18.8 %collective-permute-start.18 = (bf16[2048,128]{1,0:T(8,128)(2,1)}, bf16[2048,128]{1,0:T(8,128)(2,1)S(1)}, u32[]{:S(2)}, u32[]{:S(2)}) collective-permute-start(bf16[2048,128]{1,0:T(8,128)(2,1)} %collective-permute-done.12.refs_8_), channel_id=1, source_target_pairs={{0,4},{4,8},{8,12},{12,0},{1,5},{5,9},{9,13},{13,1},{2,6},{6,10},{... | collective-permute-start | bytes 1572872 | tf_op jit(solution)/shard_map/ppermute | solution.py:49
  46.9 17.7 %collective-permute-start.17 = (bf16[2048,128]{1,0:T(8,128)(2,1)}, bf16[2048,128]{1,0:T(8,128)(2,1)S(1)}, u32[]{:S(2)}, u32[]{:S(2)}) collective-permute-start(bf16[2048,128]{1,0:T(8,128)(2,1)} %collective-permute-done.7.refs_5_), channel_id=1, source_target_pairs={{0,3},{1,0},{2,1},{3,2},{4,7},{5,4},{6,5},{7,6},{8,11},{9,8},{10,9... | collective-permute-start | bytes 1572872 | tf_op jit(solution)/shard_map/ppermute | solution.py:49
  52.3 12.3 %collective-permute-start.19 = (bf16[2048,128]{1,0:T(8,128)(2,1)}, bf16[2048,128]{1,0:T(8,128)(2,1)S(1)}, u32[]{:S(2)}, u32[]{:S(2)}) collective-permute-start(bf16[2048,128]{1,0:T(8,128)(2,1)} %collective-permute-done.15.refs_11_), channel_id=1, source_target_pairs={{0,12},{4,0},{8,4},{12,8},{1,13},{5,1},{9,5},{13,9},{2,14},{6,2},{... | collective-permute-start | bytes 1572872 | tf_op jit(solution)/shard_map/ppermute | solution.py:49
  74.8 50.6 %all-to-all-start = ((bf16[8,464,256]{2,1,0:T(8,128)(2,1)}), bf16[8,464,256]{2,1,0:T(8,128)(2,1)S(1)}, u32[]{:S(2)}, u32[]{:S(2)}) async-start(bf16[8,464,256]{2,1,0:T(8,128)(2,1)} %get-tuple-element.24), calls=%async_computation | async-start | bytes 3801088 | tf_op jit(solution)/shard_map/all_to_all | solution.py:468
  79.4 10.2 %collective-permute-start.27 = (bf16[128,1024]{1,0:T(8,128)(2,1)S(1)}, bf16[128,1024]{1,0:T(8,128)(2,1)S(1)}, u32[]{:S(2)}, u32[]{:S(2)}) collective-permute-start(bf16[128,1024]{1,0:T(8,128)(2,1)S(1)} %constant_dynamic-slice_fusion), channel_id=1, source_target_pairs={{0,4},{4,8},{8,12},{12,0},{1,5},{5,9},{9,13},{13,1},{2,6},{6,10},{... | collective-permute-start | bytes 786440 | tf_op jit(solution)/shard_map/ppermute | solution.py:49
  79.5 10.2 %collective-permute-start.28 = (bf16[128,1024]{1,0:T(8,128)(2,1)S(1)}, bf16[128,1024]{1,0:T(8,128)(2,1)S(1)}, u32[]{:S(2)}, u32[]{:S(2)}) collective-permute-start(bf16[128,1024]{1,0:T(8,128)(2,1)S(1)} %constant_dynamic-slice_fusion), channel_id=1, source_target_pairs={{0,12},{4,0},{8,4},{12,8},{1,13},{5,1},{9,5},{13,9},{2,14},{6,2},{... | collective-permute-start | bytes 786440 | tf_op jit(solution)/shard_map/ppermute | solution.py:49
  99.6 43.4 %collective-permute-start.31 = (bf16[512,1024]{1,0:T(8,128)(2,1)}, bf16[512,1024]{1,0:T(8,128)(2,1)S(1)}, u32[]{:S(2)}, u32[]{:S(2)}) collective-permute-start(bf16[512,1024]{1,0:T(8,128)(2,1)} %constant_dynamic-update-slice_fusion.6.refs_0_), channel_id=1, source_target_pairs={{0,1},{1,2},{2,3},{3,0},{4,5},{5,6},{6,7},{7,4},{8,9},{9,10},{10,1... | collective-permute-start | bytes 3145736 | tf_op jit(solution)/shard_map/ppermute | solution.py:49
  99.6 45.0 %collective-permute-start.32 = (bf16[512,1024]{1,0:T(8,128)(2,1)}, bf16[512,1024]{1,0:T(8,128)(2,1)}, u32[]{:S(2)}, u32[]{:S(2)}) collective-permute-start(bf16[512,1024]{1,0:T(8,128)(2,1)} %constant_dynamic-update-slice_fusion.6.refs_0_), channel_id=1, source_target_pairs={{0,3},{1,0},{2,1},{3,2},{4,7},{5,4},{6,5},{7,6},{8,11},{9,8},{10,9... | collective-permute-start | bytes 3145736 | tf_op jit(solution)/shard_map/ppermute | solution.py:49
  104.2 11.7 %collective-permute-start.22 = (bf16[384,256]{1,0:T(8,128)(2,1)S(1)}, bf16[384,256]{1,0:T(8,128)(2,1)S(1)}, u32[]{:S(2)}, u32[]{:S(2)}) collective-permute-start(bf16[384,256]{1,0:T(8,128)(2,1)S(1)} %copy-done.31), channel_id=1, source_target_pairs={{0,48},{16,64},{32,80},{48,96},{64,112},{80,0},{96,16},{112,32},{1... | collective-permute-start | bytes 589832 | tf_op jit(solution)/shard_map/ppermute | solution.py:471
  107.1 13.4 %collective-permute-start.23 = (bf16[384,256]{1,0:T(8,128)(2,1)S(1)}, bf16[384,256]{1,0:T(8,128)(2,1)S(1)}, u32[]{:S(2)}, u32[]{:S(2)}) collective-permute-start(bf16[384,256]{1,0:T(8,128)(2,1)S(1)} %copy-done.30), channel_id=1, source_target_pairs={{0,64},{16,80},{32,96},{48,112},{64,0},{80,16},{96,32},{112,48},{1... | collective-permute-start | bytes 589832 | tf_op jit(solution)/shard_map/ppermute | solution.py:471
  137.4 16.8 %all-to-all-start.1 = ((bf16[8,4,64,128]{3,2,1,0:T(8,128)(2,1)}), bf16[8,4,64,128]{3,2,1,0:T(8,128)(2,1)}, u32[]{:S(2)}, u32[]{:S(2)}) async-start(bf16[8,4,64,128]{3,2,1,0:T(8,128)(2,1)} %attend_early.1), calls=%async_computation.1 | async-start | bytes 1048576 | tf_op jit(solution)/shard_map/all_to_all | solution.py:505
  142.1 36.0 %collective-permute-start.35 = (bf16[512,1024]{1,0:T(8,128)(2,1)}, bf16[512,1024]{1,0:T(8,128)(2,1)}, u32[]{:S(2)}, u32[]{:S(2)}) collective-permute-start(bf16[512,1024]{1,0:T(8,128)(2,1)} %constant_dynamic-update-slice_fusion.6.refs_0_), channel_id=1, source_target_pairs={{0,16},{16,0},{32,48},{48,32},{64,80},{80,64},{96,112},{112,96},{1... | collective-permute-start | bytes 3145736 | tf_op jit(solution)/shard_map/ppermute | solution.py:476
  143.8 16.4 %collective-permute-start.33 = (bf16[256,1024]{1,0:T(8,128)(2,1)}, bf16[256,1024]{1,0:T(8,128)(2,1)}, u32[]{:S(2)}, u32[]{:S(2)}) collective-permute-start(bf16[256,1024]{1,0:T(8,128)(2,1)} %slice.46), channel_id=1, source_target_pairs={{0,1},{1,2},{2,3},{3,0},{4,5},{5,6},{6,7},{7,4},{8,9},{9,10},{10,1... | collective-permute-start | bytes 1572872 | tf_op jit(solution)/shard_map/ppermute | solution.py:49
  146.5 14.9 %collective-permute-start.34 = (bf16[256,1024]{1,0:T(8,128)(2,1)}, bf16[256,1024]{1,0:T(8,128)(2,1)}, u32[]{:S(2)}, u32[]{:S(2)}) collective-permute-start(bf16[256,1024]{1,0:T(8,128)(2,1)} %slice.47), channel_id=1, source_target_pairs={{0,3},{1,0},{2,1},{3,2},{4,7},{5,4},{6,5},{7,6},{8,11},{9,8},{10,9... | collective-permute-start | bytes 1572872 | tf_op jit(solution)/shard_map/ppermute | solution.py:49
  149.7 28.5 %collective-permute-start.36 = (bf16[512,1024]{1,0:T(8,128)(2,1)S(1)}, bf16[512,1024]{1,0:T(8,128)(2,1)}, u32[]{:S(2)}, u32[]{:S(2)}) collective-permute-start(bf16[512,1024]{1,0:T(8,128)(2,1)S(1)} %collective-permute-done.31.refs_1_), channel_id=1, source_target_pairs={{0,16},{16,0},{32,48},{48,32},{64,80},{80,64},{96,112},{112,96},{1... | collective-permute-start | bytes 3145736 | tf_op jit(solution)/shard_map/ppermute | solution.py:476
  149.7 28.5 %collective-permute-start.37 = (bf16[512,1024]{1,0:T(8,128)(2,1)}, bf16[512,1024]{1,0:T(8,128)(2,1)}, u32[]{:S(2)}, u32[]{:S(2)}) collective-permute-start(bf16[512,1024]{1,0:T(8,128)(2,1)} %collective-permute-done.32.refs_2_), channel_id=1, source_target_pairs={{0,16},{16,0},{32,48},{48,32},{64,80},{80,64},{96,112},{112,96},{1... | collective-permute-start | bytes 3145736 | tf_op jit(solution)/shard_map/ppermute | solution.py:476
  154.2 13.9 %all-to-all-start.2 = ((bf16[8,4,64,128]{3,2,1,0:T(8,128)(2,1)}), bf16[8,4,64,128]{3,2,1,0:T(8,128)(2,1)S(1)}, u32[]{:S(2)}, u32[]{:S(2)}) async-start(bf16[8,4,64,128]{3,2,1,0:T(8,128)(2,1)} %attend_late.1), calls=%async_computation.2 | async-start | bytes 1048576 | tf_op jit(solution)/shard_map/all_to_all | solution.py:494
  160.2 18.0 %collective-permute-start.38 = (bf16[256,1024]{1,0:T(8,128)(2,1)}, bf16[256,1024]{1,0:T(8,128)(2,1)S(1)}, u32[]{:S(2)}, u32[]{:S(2)}) collective-permute-start(bf16[256,1024]{1,0:T(8,128)(2,1)} %collective-permute-done.33.refs_3_), channel_id=1, source_target_pairs={{0,16},{16,0},{32,48},{48,32},{64,80},{80,64},{96,112},{112,96},{1... | collective-permute-start | bytes 1572872 | tf_op jit(solution)/shard_map/ppermute | solution.py:476
  161.4 16.8 %collective-permute-start.39 = (bf16[256,1024]{1,0:T(8,128)(2,1)}, bf16[256,1024]{1,0:T(8,128)(2,1)}, u32[]{:S(2)}, u32[]{:S(2)}) collective-permute-start(bf16[256,1024]{1,0:T(8,128)(2,1)} %collective-permute-done.34.refs_4_), channel_id=1, source_target_pairs={{0,16},{16,0},{32,48},{48,32},{64,80},{80,64},{96,112},{112,96},{1... | collective-permute-start | bytes 1572872 | tf_op jit(solution)/shard_map/ppermute | solution.py:476
  172.4 17.0 %all-to-all-start.3 = ((bf16[16,128,128]{2,1,0:T(8,128)(2,1)}), bf16[16,128,128]{2,1,0:T(8,128)(2,1)S(1)}, u32[]{:S(2)}, u32[]{:S(2)}) async-start(bf16[16,128,128]{2,1,0:T(8,128)(2,1)} %bitcast.8), calls=%async_computation.3 | async-start | bytes 1048576 | tf_op jit(solution)/shard_map/all_to_all | solution.py:516
  (46 other events, 612.6 us)

commit v2 on v1

--- a/solution.py
+++ b/solution.py
@@ -428,7 +428,7 @@
     near_a = gather_near(tokens[:HALF], "hx", "hz")
     near_b = gather_near(tokens[HALF:], "hz", "hx")
     w_half = lax.dynamic_slice_in_dim(w_out, core * (WIDTH // 2), WIDTH // 2, 1)
-    w_row = (w_half,) + ring_gather(w_half, "hx")
+    w_row = (w_half,) + tuple(shift(w_half, "hx", -by) for by in OFFSETS[1:])
 
     weights = (w_query, w_key, w_value)
     acc, own = pl.pallas_call(
@@ -473,7 +473,9 @@
     w_row, _ = lax.optimization_barrier((w_row, own))
     w_row = jnp.concatenate(w_row, 0)
     w_near = (w_row,) + ring_gather(w_row, "hz")
-    w_far = tuple(lax.ppermute(w, "seq", [(i, i ^ 1) for i in range(SEQ)]) for w in w_near)
+    w_far = []
+    for w in w_near:
+        w_far.append(lax.ppermute(w, "seq", [(i, i ^ 1) for i in range(SEQ)]))
 
     scratch = [
         *[pltpu.VMEM((QT, 2 * BLOCK), F32)] * 2,
@@ -502,7 +504,8 @@
         name="attend_early",
         cost_estimate=estimate(4 * MID * BLOCK * 2 * BLOCK * HD, 8),
     )(place, got, *parts)
-    early = lax.all_to_all(early, "seq", 0, 0, tiled=True).reshape(ROWS // 2, HD)
+    early = lax.all_to_all(early, "seq", 0, 0, tiled=True)
+    early = early.reshape(ROWS // 2, HD)
     taken = pl.pallas_call(
         take_rows,
         out_shape=shape((TOK, HD), BF),

time: 196 us -> 194 us (0.990)
  starting transfers between devices: 69.3 us -> 66.7 us
  waiting for transfers between devices: 62.2 us -> 64.4 us
    ppermute x28 -> x27, waiting for transfers between devices: 33.1 us -> 35.3 us  [shift(): return lax.ppermute(piece, axis, ring(by))]
    ppermute x28 -> x27, starting transfers between devices: 42.9 us -> 40.8 us  [shift(): return lax.ppermute(piece, axis, ring(by))]
    unnamed x76 -> x61, local copies, waits for them, and re-layouts: 21.6 us -> 20.9 us
  transfers between devices with their start and end apart: 44 -> 43, of which waited for: 18 -> 19; matrix products, arithmetic and copies ran while one was open for 5% -> 5% of each run, Pallas kernels for 10% -> 10%
where the time goes in v2:
time: 194 us
  starting transfers between devices  66.7 us (34%)
  waiting for transfers between devices  64.4 us (33%)
  Pallas kernels  34.8 us (18%)
  local copies, waits for them, and re-layouts  27.2 us (14%)
    ppermute x27, starting transfers between devices, shift(): return lax.ppermute(piece, axis, ring(by))  40.8 us
    ppermute x27, waiting for transfers between devices, shift(): return lax.ppermute(piece, axis, ring(by))  35.3 us
    unnamed x61, local copies, waits for them, and re-layouts  20.9 us
    all_to_all x1, waiting for transfers between devices, sublayer(): lax.all_to_all(taken.reshape(HEADS, HD, HD), ('hx', 'hz'), 0, 0, tiled=True)  11.1 us
    ppermute x7, waiting for transfers between devices, sublayer(): lax.ppermute(rest[d], 'seq', [(i, (i + d) % SEQ) for i in range(SEQ)])  11 us
    pallas_call x1, Pallas kernels, sublayer(): pl.pallas_call(project_far, out_shape=(pltpu.HBM((SEQ, SENT, 2 * HD), BF)...  9.09 us
    ppermute x7, starting transfers between devices, sublayer(): lax.ppermute(rest[d], 'seq', [(i, (i + d) % SEQ) for i in range(SEQ)])  7.52 us
    pallas_call x1, Pallas kernels, sublayer(): pl.pallas_call(project_near, out_shape=(shape((TOK, 3 * HD), F32), shape(...  7.38 us
  transfers between devices with their start and end apart: 43, of which 19 were waited for; matrix products, arithmetic and copies ran while one was open for 5% of the time, Pallas kernels for 10%

profile of v2, /device:TPU:0, one launch (start us, length us, event | category | flops | bytes accessed | tf_op | source)
XLA Modules:
  0.0 193.5 jit_solution(9965386731261339035)
XLA Ops:
  10.4 2.2 %collective-permute-start.4 = (bf16[2048,128]{1,0:T(8,128)(2,1)S(1)}, bf16[2048,128]{1,0:T(8,128)(2,1)S(1)}, u32[]{:S(2)}, u32[]{:S(2)}) collective-permute-start(bf16[2048,128]{1,0:T(8,128)(2,1)S(1)} %pad_maximum_fusion.refs_0_), channel_id=1, source_target_pairs={{0,1},{1,2},{2,3},{3,0},{4,5},{5,6},{6,7},{7,4},{8,9},{9,10},{10,1... | collective-permute-start | bytes 1572872 | tf_op jit(solution)/shard_map/ppermute | solution.py:49
  12.6 2.2 %collective-permute-start.6 = (bf16[2048,128]{1,0:T(8,128)(2,1)S(1)}, bf16[2048,128]{1,0:T(8,128)(2,1)S(1)}, u32[]{:S(2)}, u32[]{:S(2)}) collective-permute-start(bf16[2048,128]{1,0:T(8,128)(2,1)S(1)} %pad_maximum_fusion.refs_0_), channel_id=1, source_target_pairs={{0,3},{1,0},{2,1},{3,2},{4,7},{5,4},{6,5},{7,6},{8,11},{9,8},{10,9... | collective-permute-start | bytes 1572872 | tf_op jit(solution)/shard_map/ppermute | solution.py:49
  15.2 3.0 %collective-permute-start.3 = (bf16[512,128]{1,0:T(8,128)(2,1)S(1)}, bf16[512,128]{1,0:T(8,128)(2,1)S(1)}, u32[]{:S(2)}, u32[]{:S(2)}) collective-permute-start(bf16[512,128]{1,0:T(8,128)(2,1)S(1)} %slice.33), channel_id=1, source_target_pairs={{0,12},{4,0},{8,4},{12,8},{1,13},{5,1},{9,5},{13,9},{2,14},{6,2},{... | collective-permute-start | bytes 393224 | tf_op jit(solution)/shard_map/ppermute | solution.py:49
  21.7 2.1 %collective-permute-start.11 = (bf16[512,128]{1,0:T(8,128)(2,1)S(1)}, bf16[512,128]{1,0:T(8,128)(2,1)S(1)}, u32[]{:S(2)}, u32[]{:S(2)}) collective-permute-start(bf16[512,128]{1,0:T(8,128)(2,1)S(1)} %slice.35), channel_id=1, source_target_pairs={{0,3},{1,0},{2,1},{3,2},{4,7},{5,4},{6,5},{7,6},{8,11},{9,8},{10,9... | collective-permute-start | bytes 393224 | tf_op jit(solution)/shard_map/ppermute | solution.py:49
  24.5 4.1 %collective-permute-done.10 = bf16[512,128]{1,0:T(8,128)(2,1)S(1)} collective-permute-done((bf16[512,128]{1,0:T(8,128)(2,1)S(1)}, bf16[512,128]{1,0:T(8,128)(2,1)S(1)}, u32[]{:S(2)}, u32[]{:S(2)}) %collective-permute-start.10) | collective-permute-done | bytes 131104 | tf_op jit(solution)/shard_map/ppermute | solution.py:49
  31.5 3.2 %collective-permute-start.7 = (bf16[2048,128]{1,0:T(8,128)(2,1)}, bf16[2048,128]{1,0:T(8,128)(2,1)}, u32[]{:S(2)}, u32[]{:S(2)}) collective-permute-start(bf16[2048,128]{1,0:T(8,128)(2,1)} %constant_dynamic-update-slice_fusion.refs_1_), channel_id=1, source_target_pairs={{0,3},{1,0},{2,1},{3,2},{4,7},{5,4},{6,5},{7,6},{8,11},{9,8},{10,9... | collective-permute-start | bytes 1572872 | tf_op jit(solution)/shard_map/ppermute | solution.py:49
  37.6 5.9 %collective-permute-done.14.refs_10_ = bf16[2048,128]{1,0:T(8,128)(2,1)} collective-permute-done((bf16[2048,128]{1,0:T(8,128)(2,1)S(1)}, bf16[2048,128]{1,0:T(8,128)(2,1)}, u32[]{:S(2)}, u32[]{:S(2)}) %collective-permute-start.14) | collective-permute-done | bytes 524320 | tf_op jit(solution)/shard_map/ppermute | solution.py:49
  43.5 2.3 %collective-permute-done.5.refs_3_ = bf16[2048,128]{1,0:T(8,128)(2,1)} collective-permute-done((bf16[2048,128]{1,0:T(8,128)(2,1)}, bf16[2048,128]{1,0:T(8,128)(2,1)}, u32[]{:S(2)}, u32[]{:S(2)}) %collective-permute-start.5) | collective-permute-done | bytes 524320 | tf_op jit(solution)/shard_map/ppermute | solution.py:49
  47.9 4.4 %collective-permute-done.15.refs_11_ = bf16[2048,128]{1,0:T(8,128)(2,1)} collective-permute-done((bf16[2048,128]{1,0:T(8,128)(2,1)}, bf16[2048,128]{1,0:T(8,128)(2,1)}, u32[]{:S(2)}, u32[]{:S(2)}) %collective-permute-start.15) | collective-permute-done | bytes 524320 | tf_op jit(solution)/shard_map/ppermute | solution.py:49
  52.3 2.7 %collective-permute-start.19 = (bf16[2048,128]{1,0:T(8,128)(2,1)}, bf16[2048,128]{1,0:T(8,128)(2,1)S(1)}, u32[]{:S(2)}, u32[]{:S(2)}) collective-permute-start(bf16[2048,128]{1,0:T(8,128)(2,1)} %collective-permute-done.15.refs_11_), channel_id=1, source_target_pairs={{0,12},{4,0},{8,4},{12,8},{1,13},{5,1},{9,5},{13,9},{2,14},{6,2},{... | collective-permute-start | bytes 1572872 | tf_op jit(solution)/shard_map/ppermute | solution.py:49
  57.1 7.4 %project_near.1 = (f32[2048,384]{1,0:T(8,128)S(1)}, bf16[128,2048]{1,0:T(8,128)(2,1)S(1)}) custom-call(s32[4]{0:T(128)S(1)} %pad_add_fusion.place_ref, bf16[2048,128]{1,0:T(8,128)(2,1)S(1)} %copy-done.1, bf16[2048,128]{1,0:T(8,128)(2,1)S(1)} %copy-done.2, bf16[2048,128]{1,0:T(8,128)(2,1)S(1)} %copy-done.3, bf16[2048,128]{1,0:T(8,128)(2,1)S(1)} %pad_maximum_fusion.refs_0_, ...), custom_call_target="tpu_custom_call" | custom-call | flops 2415919104 | bytes 10485760 | tf_op jit(solution)/shard_map/project_near/pallas_call | solution.py:434
  64.9 9.1 %project_far.1 = (bf16[8,464,256]{2,1,0:T(8,128)(2,1)}, bf16[384,256]{1,0:T(8,128)(2,1)}, bf16[384,256]{1,0:T(8,128)(2,1)}, bf16[384,256]{1,0:T(8,128)(2,1)}, bf...) custom-call(s32[4]{0:T(128)S(1)} %pad_add_fusion.place_ref, ...), custom_call_target="tpu_custom_call" | custom-call | flops 805306368 | bytes 25165824 | tf_op jit(solution)/shard_map/project_far/pallas_call | solution.py:446
  74.8 4.5 %all-to-all-start = ((bf16[8,464,256]{2,1,0:T(8,128)(2,1)}), bf16[8,464,256]{2,1,0:T(8,128)(2,1)S(1)}, u32[]{:S(2)}, u32[]{:S(2)}) async-start(bf16[8,464,256]{2,1,0:T(8,128)(2,1)} %get-tuple-element.23), calls=%async_computation | async-start | bytes 3801088 | tf_op jit(solution)/shard_map/all_to_all | solution.py:468
  79.4 3.2 %collective-permute-start.28 = (bf16[128,1024]{1,0:T(8,128)(2,1)S(1)}, bf16[128,1024]{1,0:T(8,128)(2,1)S(1)}, u32[]{:S(2)}, u32[]{:S(2)}) collective-permute-start(bf16[128,1024]{1,0:T(8,128)(2,1)S(1)} %constant_dynamic-slice_fusion), channel_id=1, source_target_pairs={{0,12},{4,0},{8,4},{12,8},{1,13},{5,1},{9,5},{13,9},{2,14},{6,2},{... | collective-permute-start | bytes 786440 | tf_op jit(solution)/shard_map/ppermute | solution.py:49
  84.0 5.5 %collective-permute-done.27 = bf16[128,1024]{1,0:T(8,128)(2,1)S(1)} collective-permute-done((bf16[128,1024]{1,0:T(8,128)(2,1)S(1)}, bf16[128,1024]{1,0:T(8,128)(2,1)S(1)}, u32[]{:S(2)}, u32[]{:S(2)}) %collective-permute-start.27) | collective-permute-done | bytes 262176 | tf_op jit(solution)/shard_map/ppermute | solution.py:49
  89.5 5.0 %collective-permute-done.28 = bf16[128,1024]{1,0:T(8,128)(2,1)S(1)} collective-permute-done((bf16[128,1024]{1,0:T(8,128)(2,1)S(1)}, bf16[128,1024]{1,0:T(8,128)(2,1)S(1)}, u32[]{:S(2)}, u32[]{:S(2)}) %collective-permute-start.28) | collective-permute-done | bytes 262176 | tf_op jit(solution)/shard_map/ppermute | solution.py:49
  99.2 3.2 %collective-permute-start.31 = (bf16[512,1024]{1,0:T(8,128)(2,1)}, bf16[512,1024]{1,0:T(8,128)(2,1)}, u32[]{:S(2)}, u32[]{:S(2)}) collective-permute-start(bf16[512,1024]{1,0:T(8,128)(2,1)} %constant_dynamic-update-slice_fusion.6.refs_0_), channel_id=1, source_target_pairs={{0,3},{1,0},{2,1},{3,2},{4,7},{5,4},{6,5},{7,6},{8,11},{9,8},{10,9... | collective-permute-start | bytes 3145736 | tf_op jit(solution)/shard_map/ppermute | solution.py:49
  108.6 2.5 %collective-permute-done.21.refs_2_ = bf16[384,256]{1,0:T(8,128)(2,1)S(1)} collective-permute-done((bf16[384,256]{1,0:T(8,128)(2,1)}, bf16[384,256]{1,0:T(8,128)(2,1)S(1)}, u32[]{:S(2)}, u32[]{:S(2)}) %collective-permute-start.21) | collective-permute-done | bytes 196640 | tf_op jit(solution)/shard_map/ppermute | solution.py:471
  111.8 2.3 %collective-permute-start.24 = (bf16[384,256]{1,0:T(8,128)(2,1)}, bf16[384,256]{1,0:T(8,128)(2,1)S(1)}, u32[]{:S(2)}, u32[]{:S(2)}) collective-permute-start(bf16[384,256]{1,0:T(8,128)(2,1)} %get-tuple-element.29), channel_id=1, source_target_pairs={{0,80},{16,96},{32,112},{48,0},{64,16},{80,32},{96,48},{112,64},{1... | collective-permute-start | bytes 589832 | tf_op jit(solution)/shard_map/ppermute | solution.py:471
  116.5 3.9 %collective-permute-done.23.refs_4_ = bf16[384,256]{1,0:T(8,128)(2,1)S(1)} collective-permute-done((bf16[384,256]{1,0:T(8,128)(2,1)}, bf16[384,256]{1,0:T(8,128)(2,1)S(1)}, u32[]{:S(2)}, u32[]{:S(2)}) %collective-permute-start.23) | collective-permute-done | bytes 196640 | tf_op jit(solution)/shard_map/ppermute | solution.py:471
  121.8 2.3 %collective-permute-done.25.refs_6_ = bf16[384,256]{1,0:T(8,128)(2,1)S(1)} collective-permute-done((bf16[384,256]{1,0:T(8,128)(2,1)}, bf16[384,256]{1,0:T(8,128)(2,1)S(1)}, u32[]{:S(2)}, u32[]{:S(2)}) %collective-permute-start.25) | collective-permute-done | bytes 196640 | tf_op jit(solution)/shard_map/ppermute | solution.py:471
  133.2 4.6 %attend_early.1 = bf16[8,4,64,128]{3,2,1,0:T(8,128)(2,1)} custom-call(s32[4]{0:T(128)S(1)} %pad_add_fusion.place_ref, bf16[8,464,256]{2,1,0:T(8,128)(2,1)S(1)} %all-to-all-done.got, bf16[384,256]{1,0:T(8,128)(2,1)S(1)} %copy-done.6, bf16[384,256]{1,0:T(8,128)(2,1)S(1)} %copy-done.8, bf16[384,256]{1,0:T(8,128)(2,1)S(1)} %copy-done.10, ...), custom_call_target="tpu_custom_call" | custom-call | flops 1073741824 | bytes 8388608 | tf_op jit(solution)/shard_map/attend_early/pallas_call | solution.py:497
  137.8 4.3 %all-to-all-start.1 = ((bf16[8,4,64,128]{3,2,1,0:T(8,128)(2,1)}), bf16[8,4,64,128]{3,2,1,0:T(8,128)(2,1)}, u32[]{:S(2)}, u32[]{:S(2)}) async-start(bf16[8,4,64,128]{3,2,1,0:T(8,128)(2,1)} %attend_early.1), calls=%async_computation.1 | async-start | bytes 1048576 | tf_op jit(solution)/shard_map/all_to_all | solution.py:507
  146.8 2.7 %collective-permute-start.33 = (bf16[256,1024]{1,0:T(8,128)(2,1)}, bf16[256,1024]{1,0:T(8,128)(2,1)}, u32[]{:S(2)}, u32[]{:S(2)}) collective-permute-start(bf16[256,1024]{1,0:T(8,128)(2,1)} %slice.37), channel_id=1, source_target_pairs={{0,3},{1,0},{2,1},{3,2},{4,7},{5,4},{6,5},{7,6},{8,11},{9,8},{10,9... | collective-permute-start | bytes 1572872 | tf_op jit(solution)/shard_map/ppermute | solution.py:49
  150.0 4.0 %attend_late.1 = bf16[8,4,64,128]{3,2,1,0:T(8,128)(2,1)} custom-call(bf16[8,464,256]{2,1,0:T(8,128)(2,1)S(1)} %all-to-all-done.got), custom_call_target="tpu_custom_call" | custom-call | flops 1073741824 | bytes 6291456 | tf_op jit(solution)/shard_map/attend_late/pallas_call | solution.py:486
  154.1 3.7 %all-to-all-start.2 = ((bf16[8,4,64,128]{3,2,1,0:T(8,128)(2,1)}), bf16[8,4,64,128]{3,2,1,0:T(8,128)(2,1)S(1)}, u32[]{:S(2)}, u32[]{:S(2)}) async-start(bf16[8,4,64,128]{3,2,1,0:T(8,128)(2,1)} %attend_late.1), calls=%async_computation.2 | async-start | bytes 1048576 | tf_op jit(solution)/shard_map/all_to_all | solution.py:496
  157.8 2.3 %collective-permute-done.32.refs_3_ = bf16[256,1024]{1,0:T(8,128)(2,1)} collective-permute-done((bf16[256,1024]{1,0:T(8,128)(2,1)}, bf16[256,1024]{1,0:T(8,128)(2,1)}, u32[]{:S(2)}, u32[]{:S(2)}) %collective-permute-start.32) | collective-permute-done | bytes 524320 | tf_op jit(solution)/shard_map/ppermute | solution.py:49
  161.2 6.9 %all-to-all-done.2 = bf16[8,4,64,128]{3,2,1,0:T(8,128)(2,1)S(1)} async-done(((bf16[8,4,64,128]{3,2,1,0:T(8,128)(2,1)}), bf16[8,4,64,128]{3,2,1,0:T(8,128)(2,1)S(1)}, u32[]{:S(2)}, u32[]{:S(2)}) %all-to-all-start.2) | async-done | bytes 524320 | tf_op jit(solution)/shard_map/all_to_all | solution.py:496
  168.1 4.3 %take_rows.1 = bf16[2048,128]{1,0:T(8,128)(2,1)} custom-call(s32[2048]{0:T(1024)S(1)} %fusion.2.index_ref, bf16[2048,128]{1,0:T(8,128)(2,1)} %bitcast.6.early_ref, bf16[2048,128]{1,0:T(8,128)(2,1)S(1)} %bitcast.9), custom_call_target="tpu_custom_call" | custom-call | bytes 8388608 | tf_op jit(solution)/shard_map/take_rows/pallas_call | solution.py:509
  172.3 4.6 %all-to-all-start.3 = ((bf16[16,128,128]{2,1,0:T(8,128)(2,1)}), bf16[16,128,128]{2,1,0:T(8,128)(2,1)S(1)}, u32[]{:S(2)}, u32[]{:S(2)}) async-start(bf16[16,128,128]{2,1,0:T(8,128)(2,1)} %bitcast.8), calls=%async_computation.3 | async-start | bytes 1048576 | tf_op jit(solution)/shard_map/all_to_all | solution.py:519
  177.0 11.1 %all-to-all-done.3.rows_ref = bf16[16,128,128]{2,1,0:T(8,128)(2,1)S(1)} async-done(((bf16[16,128,128]{2,1,0:T(8,128)(2,1)}), bf16[16,128,128]{2,1,0:T(8,128)(2,1)S(1)}, u32[]{:S(2)}, u32[]{:S(2)}) %all-to-all-start.3) | async-done | bytes 524320 | tf_op jit(solution)/shard_map/all_to_all | solution.py:519
  188.1 5.4 %combine.1 = bf16[128,2048]{1,0:T(8,128)(2,1)} custom-call(s32[4]{0:T(128)S(1)} %pad_add_fusion.place_ref, bf16[16,128,128]{2,1,0:T(8,128)(2,1)S(1)} %all-to-all-done.3.rows_ref, bf16[512,1024]{1,0:T(8,128)(2,1)} %constant_dynamic-update-slice_fusion.6.refs_0_, bf16[512,1024]{1,0:T(8,128)(2,1)S(1)} %collective-permute-done.30.refs_1_, ...), custom_call_target="tpu_custom_call" | custom-call | flops 1073741824 | bytes 10485760 | tf_op jit(solution)/shard_map/combine/pallas_call | solution.py:526
  (138 shorter events, 58.4 us)
Async XLA Ops:
  2.8 12.0 %collective-permute-start.1 = (bf16[1024,128]{1,0:T(8,128)(2,1)S(1)}, bf16[1024,128]{1,0:T(8,128)(2,1)S(1)}, u32[]{:S(2)}, u32[]{:S(2)}) collective-permute-start(bf16[1024,128]{1,0:T(8,128)(2,1)S(1)} %get-tuple-element.38), channel_id=1, source_target_pairs={{0,12},{4,0},{8,4},{12,8},{1,13},{5,1},{9,5},{13,9},{2,14},{6,2},{... | collective-permute-start | bytes 786440 | tf_op jit(solution)/shard_map/ppermute | solution.py:49
  4.4 10.8 %collective-permute-start.8 = (bf16[1024,128]{1,0:T(8,128)(2,1)S(1)}, bf16[1024,128]{1,0:T(8,128)(2,1)S(1)}, u32[]{:S(2)}, u32[]{:S(2)}) collective-permute-start(bf16[1024,128]{1,0:T(8,128)(2,1)S(1)} %get-tuple-element.37), channel_id=1, source_target_pairs={{0,1},{1,2},{2,3},{3,0},{4,5},{5,6},{6,7},{7,4},{8,9},{9,10},{10,1... | collective-permute-start | bytes 786440 | tf_op jit(solution)/shard_map/ppermute | solution.py:49
  6.5 12.6 %collective-permute-start.9 = (bf16[1024,128]{1,0:T(8,128)(2,1)S(1)}, bf16[1024,128]{1,0:T(8,128)(2,1)S(1)}, u32[]{:S(2)}, u32[]{:S(2)}) collective-permute-start(bf16[1024,128]{1,0:T(8,128)(2,1)S(1)} %get-tuple-element.37), channel_id=1, source_target_pairs={{0,3},{1,0},{2,1},{3,2},{4,7},{5,4},{6,5},{7,6},{8,11},{9,8},{10,9... | collective-permute-start | bytes 786440 | tf_op jit(solution)/shard_map/ppermute | solution.py:49
  10.4 21.1 %collective-permute-start.4 = (bf16[2048,128]{1,0:T(8,128)(2,1)S(1)}, bf16[2048,128]{1,0:T(8,128)(2,1)S(1)}, u32[]{:S(2)}, u32[]{:S(2)}) collective-permute-start(bf16[2048,128]{1,0:T(8,128)(2,1)S(1)} %pad_maximum_fusion.refs_0_), channel_id=1, source_target_pairs={{0,1},{1,2},{2,3},{3,0},{4,5},{5,6},{6,7},{7,4},{8,9},{9,10},{10,1... | collective-permute-start | bytes 1572872 | tf_op jit(solution)/shard_map/ppermute | solution.py:49
  12.6 22.1 %collective-permute-start.6 = (bf16[2048,128]{1,0:T(8,128)(2,1)S(1)}, bf16[2048,128]{1,0:T(8,128)(2,1)S(1)}, u32[]{:S(2)}, u32[]{:S(2)}) collective-permute-start(bf16[2048,128]{1,0:T(8,128)(2,1)S(1)} %pad_maximum_fusion.refs_0_), channel_id=1, source_target_pairs={{0,3},{1,0},{2,1},{3,2},{4,7},{5,4},{6,5},{7,6},{8,11},{9,8},{10,9... | collective-permute-start | bytes 1572872 | tf_op jit(solution)/shard_map/ppermute | solution.py:49
  21.1 15.3 %collective-permute-start.12 = (bf16[2048,128]{1,0:T(8,128)(2,1)S(1)}, bf16[2048,128]{1,0:T(8,128)(2,1)}, u32[]{:S(2)}, u32[]{:S(2)}) collective-permute-start(bf16[2048,128]{1,0:T(8,128)(2,1)S(1)} %pad_maximum_fusion.1.refs_6_), channel_id=1, source_target_pairs={{0,4},{4,8},{8,12},{12,0},{1,5},{5,9},{9,13},{13,1},{2,6},{6,10},{... | collective-permute-start | bytes 1572872 | tf_op jit(solution)/shard_map/ppermute | solution.py:49
  28.6 14.9 %collective-permute-start.14 = (bf16[2048,128]{1,0:T(8,128)(2,1)S(1)}, bf16[2048,128]{1,0:T(8,128)(2,1)}, u32[]{:S(2)}, u32[]{:S(2)}) collective-permute-start(bf16[2048,128]{1,0:T(8,128)(2,1)S(1)} %pad_maximum_fusion.1.refs_6_), channel_id=1, source_target_pairs={{0,12},{4,0},{8,4},{12,8},{1,13},{5,1},{9,5},{13,9},{2,14},{6,2},{... | collective-permute-start | bytes 1572872 | tf_op jit(solution)/shard_map/ppermute | solution.py:49
  30.8 15.0 %collective-permute-start.5 = (bf16[2048,128]{1,0:T(8,128)(2,1)}, bf16[2048,128]{1,0:T(8,128)(2,1)}, u32[]{:S(2)}, u32[]{:S(2)}) collective-permute-start(bf16[2048,128]{1,0:T(8,128)(2,1)} %constant_dynamic-update-slice_fusion.refs_1_), channel_id=1, source_target_pairs={{0,1},{1,2},{2,3},{3,0},{4,5},{5,6},{6,7},{7,4},{8,9},{9,10},{10,1... | collective-permute-start | bytes 1572872 | tf_op jit(solution)/shard_map/ppermute | solution.py:49
  31.5 15.4 %collective-permute-start.7 = (bf16[2048,128]{1,0:T(8,128)(2,1)}, bf16[2048,128]{1,0:T(8,128)(2,1)}, u32[]{:S(2)}, u32[]{:S(2)}) collective-permute-start(bf16[2048,128]{1,0:T(8,128)(2,1)} %constant_dynamic-update-slice_fusion.refs_1_), channel_id=1, source_target_pairs={{0,3},{1,0},{2,1},{3,2},{4,7},{5,4},{6,5},{7,6},{8,11},{9,8},{10,9... | collective-permute-start | bytes 1572872 | tf_op jit(solution)/shard_map/ppermute | solution.py:49
  35.6 16.7 %collective-permute-start.15 = (bf16[2048,128]{1,0:T(8,128)(2,1)}, bf16[2048,128]{1,0:T(8,128)(2,1)}, u32[]{:S(2)}, u32[]{:S(2)}) collective-permute-start(bf16[2048,128]{1,0:T(8,128)(2,1)} %constant_dynamic-update-slice_fusion.3.refs_7_), channel_id=1, source_target_pairs={{0,12},{4,0},{8,4},{12,8},{1,13},{5,1},{9,5},{13,9},{2,14},{6,2},{... | collective-permute-start | bytes 1572872 | tf_op jit(solution)/shard_map/ppermute | solution.py:49
  36.4 18.6 %collective-permute-start.13 = (bf16[2048,128]{1,0:T(8,128)(2,1)}, bf16[2048,128]{1,0:T(8,128)(2,1)}, u32[]{:S(2)}, u32[]{:S(2)}) collective-permute-start(bf16[2048,128]{1,0:T(8,128)(2,1)} %constant_dynamic-update-slice_fusion.3.refs_7_), channel_id=1, source_target_pairs={{0,4},{4,8},{8,12},{12,0},{1,5},{5,9},{9,13},{13,1},{2,6},{6,10},{... | collective-permute-start | bytes 1572872 | tf_op jit(solution)/shard_map/ppermute | solution.py:49
  43.5 21.0 %collective-permute-start.16 = (bf16[2048,128]{1,0:T(8,128)(2,1)}, bf16[2048,128]{1,0:T(8,128)(2,1)S(1)}, u32[]{:S(2)}, u32[]{:S(2)}) collective-permute-start(bf16[2048,128]{1,0:T(8,128)(2,1)} %copy-done.21), channel_id=1, source_target_pairs={{0,1},{1,2},{2,3},{3,0},{4,5},{5,6},{6,7},{7,4},{8,9},{9,10},{10,1... | collective-permute-start | bytes 1572872 | tf_op jit(solution)/shard_map/ppermute | solution.py:49
  45.8 18.8 %collective-permute-start.18 = (bf16[2048,128]{1,0:T(8,128)(2,1)}, bf16[2048,128]{1,0:T(8,128)(2,1)S(1)}, u32[]{:S(2)}, u32[]{:S(2)}) collective-permute-start(bf16[2048,128]{1,0:T(8,128)(2,1)} %collective-permute-done.12.refs_8_), channel_id=1, source_target_pairs={{0,4},{4,8},{8,12},{12,0},{1,5},{5,9},{9,13},{13,1},{2,6},{6,10},{... | collective-permute-start | bytes 1572872 | tf_op jit(solution)/shard_map/ppermute | solution.py:49
  46.9 17.7 %collective-permute-start.17 = (bf16[2048,128]{1,0:T(8,128)(2,1)}, bf16[2048,128]{1,0:T(8,128)(2,1)S(1)}, u32[]{:S(2)}, u32[]{:S(2)}) collective-permute-start(bf16[2048,128]{1,0:T(8,128)(2,1)} %collective-permute-done.7.refs_5_), channel_id=1, source_target_pairs={{0,3},{1,0},{2,1},{3,2},{4,7},{5,4},{6,5},{7,6},{8,11},{9,8},{10,9... | collective-permute-start | bytes 1572872 | tf_op jit(solution)/shard_map/ppermute | solution.py:49
  52.3 12.3 %collective-permute-start.19 = (bf16[2048,128]{1,0:T(8,128)(2,1)}, bf16[2048,128]{1,0:T(8,128)(2,1)S(1)}, u32[]{:S(2)}, u32[]{:S(2)}) collective-permute-start(bf16[2048,128]{1,0:T(8,128)(2,1)} %collective-permute-done.15.refs_11_), channel_id=1, source_target_pairs={{0,12},{4,0},{8,4},{12,8},{1,13},{5,1},{9,5},{13,9},{2,14},{6,2},{... | collective-permute-start | bytes 1572872 | tf_op jit(solution)/shard_map/ppermute | solution.py:49
  74.8 50.9 %all-to-all-start = ((bf16[8,464,256]{2,1,0:T(8,128)(2,1)}), bf16[8,464,256]{2,1,0:T(8,128)(2,1)S(1)}, u32[]{:S(2)}, u32[]{:S(2)}) async-start(bf16[8,464,256]{2,1,0:T(8,128)(2,1)} %get-tuple-element.23), calls=%async_computation | async-start | bytes 3801088 | tf_op jit(solution)/shard_map/all_to_all | solution.py:468
  79.4 15.0 %collective-permute-start.28 = (bf16[128,1024]{1,0:T(8,128)(2,1)S(1)}, bf16[128,1024]{1,0:T(8,128)(2,1)S(1)}, u32[]{:S(2)}, u32[]{:S(2)}) collective-permute-start(bf16[128,1024]{1,0:T(8,128)(2,1)S(1)} %constant_dynamic-slice_fusion), channel_id=1, source_target_pairs={{0,12},{4,0},{8,4},{12,8},{1,13},{5,1},{9,5},{13,9},{2,14},{6,2},{... | collective-permute-start | bytes 786440 | tf_op jit(solution)/shard_map/ppermute | solution.py:49
  82.6 13.7 %collective-permute-start.29 = (bf16[128,1024]{1,0:T(8,128)(2,1)S(1)}, bf16[128,1024]{1,0:T(8,128)(2,1)S(1)}, u32[]{:S(2)}, u32[]{:S(2)}) collective-permute-start(bf16[128,1024]{1,0:T(8,128)(2,1)S(1)} %constant_dynamic-slice_fusion), channel_id=1, source_target_pairs={{0,8},{4,12},{8,0},{12,4},{1,9},{5,13},{9,1},{13,5},{2,10},{6,14},... | collective-permute-start | bytes 786440 | tf_op jit(solution)/shard_map/ppermute | solution.py:49
  99.2 43.7 %collective-permute-start.30 = (bf16[512,1024]{1,0:T(8,128)(2,1)}, bf16[512,1024]{1,0:T(8,128)(2,1)S(1)}, u32[]{:S(2)}, u32[]{:S(2)}) collective-permute-start(bf16[512,1024]{1,0:T(8,128)(2,1)} %constant_dynamic-update-slice_fusion.6.refs_0_), channel_id=1, source_target_pairs={{0,1},{1,2},{2,3},{3,0},{4,5},{5,6},{6,7},{7,4},{8,9},{9,10},{10,1... | collective-permute-start | bytes 3145736 | tf_op jit(solution)/shard_map/ppermute | solution.py:49
  99.2 45.7 %collective-permute-start.31 = (bf16[512,1024]{1,0:T(8,128)(2,1)}, bf16[512,1024]{1,0:T(8,128)(2,1)}, u32[]{:S(2)}, u32[]{:S(2)}) collective-permute-start(bf16[512,1024]{1,0:T(8,128)(2,1)} %constant_dynamic-update-slice_fusion.6.refs_0_), channel_id=1, source_target_pairs={{0,3},{1,0},{2,1},{3,2},{4,7},{5,4},{6,5},{7,6},{8,11},{9,8},{10,9... | collective-permute-start | bytes 3145736 | tf_op jit(solution)/shard_map/ppermute | solution.py:49
  104.1 11.4 %collective-permute-start.22 = (bf16[384,256]{1,0:T(8,128)(2,1)}, bf16[384,256]{1,0:T(8,128)(2,1)S(1)}, u32[]{:S(2)}, u32[]{:S(2)}) collective-permute-start(bf16[384,256]{1,0:T(8,128)(2,1)} %get-tuple-element.27), channel_id=1, source_target_pairs={{0,48},{16,64},{32,80},{48,96},{64,112},{80,0},{96,16},{112,32},{1... | collective-permute-start | bytes 589832 | tf_op jit(solution)/shard_map/ppermute | solution.py:471
  107.1 13.3 %collective-permute-start.23 = (bf16[384,256]{1,0:T(8,128)(2,1)}, bf16[384,256]{1,0:T(8,128)(2,1)S(1)}, u32[]{:S(2)}, u32[]{:S(2)}) collective-permute-start(bf16[384,256]{1,0:T(8,128)(2,1)} %get-tuple-element.28), channel_id=1, source_target_pairs={{0,64},{16,80},{32,96},{48,112},{64,0},{80,16},{96,32},{112,48},{1... | collective-permute-start | bytes 589832 | tf_op jit(solution)/shard_map/ppermute | solution.py:471
  137.8 16.3 %all-to-all-start.1 = ((bf16[8,4,64,128]{3,2,1,0:T(8,128)(2,1)}), bf16[8,4,64,128]{3,2,1,0:T(8,128)(2,1)}, u32[]{:S(2)}, u32[]{:S(2)}) async-start(bf16[8,4,64,128]{3,2,1,0:T(8,128)(2,1)} %attend_early.1), calls=%async_computation.1 | async-start | bytes 1048576 | tf_op jit(solution)/shard_map/all_to_all | solution.py:507
  142.1 34.8 %collective-permute-start.34 = (bf16[512,1024]{1,0:T(8,128)(2,1)}, bf16[512,1024]{1,0:T(8,128)(2,1)}, u32[]{:S(2)}, u32[]{:S(2)}) collective-permute-start(bf16[512,1024]{1,0:T(8,128)(2,1)} %constant_dynamic-update-slice_fusion.6.refs_0_), channel_id=1, source_target_pairs={{0,16},{16,0},{32,48},{48,32},{64,80},{80,64},{96,112},{112,96},{1... | collective-permute-start | bytes 3145736 | tf_op jit(solution)/shard_map/ppermute | solution.py:478
  143.8 16.2 %collective-permute-start.32 = (bf16[256,1024]{1,0:T(8,128)(2,1)}, bf16[256,1024]{1,0:T(8,128)(2,1)}, u32[]{:S(2)}, u32[]{:S(2)}) collective-permute-start(bf16[256,1024]{1,0:T(8,128)(2,1)} %slice.36), channel_id=1, source_target_pairs={{0,1},{1,2},{2,3},{3,0},{4,5},{5,6},{6,7},{7,4},{8,9},{9,10},{10,1... | collective-permute-start | bytes 1572872 | tf_op jit(solution)/shard_map/ppermute | solution.py:49
  146.8 14.4 %collective-permute-start.33 = (bf16[256,1024]{1,0:T(8,128)(2,1)}, bf16[256,1024]{1,0:T(8,128)(2,1)}, u32[]{:S(2)}, u32[]{:S(2)}) collective-permute-start(bf16[256,1024]{1,0:T(8,128)(2,1)} %slice.37), channel_id=1, source_target_pairs={{0,3},{1,0},{2,1},{3,2},{4,7},{5,4},{6,5},{7,6},{8,11},{9,8},{10,9... | collective-permute-start | bytes 1572872 | tf_op jit(solution)/shard_map/ppermute | solution.py:49
  149.5 27.4 %collective-permute-start.35 = (bf16[512,1024]{1,0:T(8,128)(2,1)S(1)}, bf16[512,1024]{1,0:T(8,128)(2,1)}, u32[]{:S(2)}, u32[]{:S(2)}) collective-permute-start(bf16[512,1024]{1,0:T(8,128)(2,1)S(1)} %collective-permute-done.30.refs_1_), channel_id=1, source_target_pairs={{0,16},{16,0},{32,48},{48,32},{64,80},{80,64},{96,112},{112,96},{1... | collective-permute-start | bytes 3145736 | tf_op jit(solution)/shard_map/ppermute | solution.py:478
  149.5 27.4 %collective-permute-start.36 = (bf16[512,1024]{1,0:T(8,128)(2,1)}, bf16[512,1024]{1,0:T(8,128)(2,1)}, u32[]{:S(2)}, u32[]{:S(2)}) collective-permute-start(bf16[512,1024]{1,0:T(8,128)(2,1)} %collective-permute-done.31.refs_2_), channel_id=1, source_target_pairs={{0,16},{16,0},{32,48},{48,32},{64,80},{80,64},{96,112},{112,96},{1... | collective-permute-start | bytes 3145736 | tf_op jit(solution)/shard_map/ppermute | solution.py:478
  154.1 14.0 %all-to-all-start.2 = ((bf16[8,4,64,128]{3,2,1,0:T(8,128)(2,1)}), bf16[8,4,64,128]{3,2,1,0:T(8,128)(2,1)S(1)}, u32[]{:S(2)}, u32[]{:S(2)}) async-start(bf16[8,4,64,128]{3,2,1,0:T(8,128)(2,1)} %attend_late.1), calls=%async_computation.2 | async-start | bytes 1048576 | tf_op jit(solution)/shard_map/all_to_all | solution.py:496
  160.0 16.9 %collective-permute-start.37 = (bf16[256,1024]{1,0:T(8,128)(2,1)}, bf16[256,1024]{1,0:T(8,128)(2,1)S(1)}, u32[]{:S(2)}, u32[]{:S(2)}) collective-permute-start(bf16[256,1024]{1,0:T(8,128)(2,1)} %collective-permute-done.32.refs_3_), channel_id=1, source_target_pairs={{0,16},{16,0},{32,48},{48,32},{64,80},{80,64},{96,112},{112,96},{1... | collective-permute-start | bytes 1572872 | tf_op jit(solution)/shard_map/ppermute | solution.py:478
  161.2 15.8 %collective-permute-start.38 = (bf16[256,1024]{1,0:T(8,128)(2,1)}, bf16[256,1024]{1,0:T(8,128)(2,1)}, u32[]{:S(2)}, u32[]{:S(2)}) collective-permute-start(bf16[256,1024]{1,0:T(8,128)(2,1)} %collective-permute-done.33.refs_4_), channel_id=1, source_target_pairs={{0,16},{16,0},{32,48},{48,32},{64,80},{80,64},{96,112},{112,96},{1... | collective-permute-start | bytes 1572872 | tf_op jit(solution)/shard_map/ppermute | solution.py:478
  172.3 15.8 %all-to-all-start.3 = ((bf16[16,128,128]{2,1,0:T(8,128)(2,1)}), bf16[16,128,128]{2,1,0:T(8,128)(2,1)S(1)}, u32[]{:S(2)}, u32[]{:S(2)}) async-start(bf16[16,128,128]{2,1,0:T(8,128)(2,1)} %bitcast.8), calls=%async_computation.3 | async-start | bytes 1048576 | tf_op jit(solution)/shard_map/all_to_all | solution.py:519
  (38 other events, 402.1 us)

commit v3 on v2

--- a/solution.py
+++ b/solution.py
@@ -160,8 +160,8 @@
 
 
 def project_far(place_ref, index_ref, wq, wk, wv, told_ref, acc, own_in, a0, a1, b0, b1, *refs):
-    out_ref, rest_refs, own_ref = refs[0], refs[1 : 1 + SEQ], refs[1 + SEQ]
-    wa, wb, rows, pad, full, rest, sems, rest_sems = refs[2 + SEQ :]
+    out_ref, rest_refs, own_out = refs[0], refs[1 : 1 + SEQ], refs[1 + SEQ]
+    wa, wb, rows, pad, full, rest, own_ref, sems, rest_sems, own_sem = refs[2 + SEQ :]
     a, b = piece_list((a0, a1), OFFSETS[3:]), piece_list((b0, b1), OFFSETS[3:])
     fill_weights(place_ref, (wq, wk, wv), wa, False, OFFSETS[3:])
     fill_weights(place_ref, (wq, wk, wv), wb, True, OFFSETS[3:])
@@ -180,6 +180,8 @@
     multiply(b, HALF, wb, finish)
     own_ref[...] = own_in[...]
     pick_own(place_ref, ((False, a), (True, b)), own_ref)
+    keep = pltpu.make_async_copy(own_ref, own_out, own_sem)
+    keep.start()
     scatter_rows(index_ref, rows, pad)
     flat = pad.reshape(ROWS * LINE, HD)
 
@@ -246,6 +248,7 @@
         send(o).wait()
     for d in range(SEQ):
         send_rest(d).wait()
+    keep.wait()
 
 
 QT = 128
@@ -383,8 +386,8 @@
 
 
 def combine(place_ref, rows_ref, *refs):
-    near, far = refs[:5], refs[5:10]
-    own_ref, out_ref, lhs = refs[10:]
+    near, far = refs[: 2 * SIDE], refs[2 * SIDE : 4 * SIDE]
+    own_ref, out_ref, lhs = refs[4 * SIDE :]
     n = pl.program_id(0)
 
     @pl.when(n == 0)
@@ -448,18 +451,20 @@
         out_shape=(
             pltpu.HBM((SEQ, SENT, 2 * HD), BF),
             *[pltpu.HBM((REST, 2 * HD), BF)] * SEQ,
-            shape((HD, WIDTH), BF),
+            pltpu.HBM((HD, WIDTH), BF),
         ),
         in_specs=[SMEM, SMEM] + [VMEM] * 10,
-        out_specs=(HBM,) * (1 + SEQ) + (VMEM,),
+        out_specs=(HBM,) * (2 + SEQ),
         scratch_shapes=[pltpu.VMEM((4 * HD, 3 * HD), BF)] * 2
         + [
             pltpu.VMEM((TOK, LINE, HD), F32),
             pltpu.VMEM((ROWS, LINE, HD), F32),
             pltpu.VMEM((SEQ, SENT, 2 * HD), BF),
             pltpu.VMEM((SEQ, REST, 2 * HD), BF),
+            pltpu.VMEM((HD, WIDTH), BF),
             pltpu.SemaphoreType.DMA((SEQ,)),
             pltpu.SemaphoreType.DMA((SEQ,)),
+            pltpu.SemaphoreType.DMA,
         ],
         compiler_params=params(28),
         name="project_far",
@@ -471,8 +476,14 @@
         parts.append(lax.ppermute(rest[d], "seq", [(i, (i + d) % SEQ) for i in range(SEQ)]))
 
     w_row, _ = lax.optimization_barrier((w_row, own))
-    w_row = jnp.concatenate(w_row, 0)
-    w_near = (w_row,) + ring_gather(w_row, "hz")
+    w_low, w_high = jnp.concatenate(w_row[:2], 0), jnp.concatenate(w_row[2:], 0)
+    low_back = shift(w_low, "hz", 1)
+    high_ahead = shift(w_high, "hz", -1)
+    low_ahead = shift(w_low, "hz", -1)
+    high_back = shift(w_high, "hz", 1)
+    far_low = shift(low_back, "hz", 1)
+    far_high = shift(high_ahead, "hz", -1)
+    w_near = (w_low, w_high, low_back, high_back, low_ahead, high_ahead, far_low, far_high)
     w_far = []
     for w in w_near:
         w_far.append(lax.ppermute(w, "seq", [(i, i ^ 1) for i in range(SEQ)]))
@@ -493,7 +504,8 @@
         name="attend_late",
         cost_estimate=estimate(4 * MID * BLOCK * 2 * BLOCK * HD, 6),
     )(got)
-    late = lax.all_to_all(late, "seq", 0, 0, tiled=True).reshape(ROWS // 2, HD)
+    late = lax.all_to_all(late, "seq", 0, 0, tiled=True)
+    late = late.reshape(ROWS // 2, HD)
     early = pl.pallas_call(
         attend_early,
         out_shape=pltpu.HBM((SEQ, MID, MOST, HD), BF),
@@ -520,9 +532,7 @@
         taken.reshape(HEADS, HD, HD), ("hx", "hz"), 0, 0, tiled=True
     )
     whole = lambda *dims: pl.BlockSpec(dims, lambda n: (0,) * len(dims))
-    w_specs = [
-        pl.BlockSpec((depth, COLS), lambda n: (0, n)) for depth in (512, 512, 512, 256, 256)
-    ]
+    w_specs = [pl.BlockSpec((SIDE // 2 * HD, COLS), lambda n: (0, n))] * (2 * SIDE)
     return pl.pallas_call(
         combine,
         grid=(WIDTH // 2 // COLS,),

time: 194 us -> 193 us (level)
  local copies, waits for them, and re-layouts: 27.2 us -> 19 us
  starting transfers between devices: 66.7 us -> 74.1 us
    unnamed x61 -> x56, local copies, waits for them, and re-layouts: 20.9 us -> 15.4 us
    ppermute x7, starting transfers between devices: 7.52 us -> 11.1 us  [sublayer(): lax.ppermute(rest[d], 'seq', [(i, (i + d) % SEQ) for i in range(SEQ)])]
    ppermute x5 -> x8, starting transfers between devices: 1.32 us -> 3.33 us  [sublayer(): w_far.append(lax.ppermute(w, 'seq', [(i, i ^ 1) for i in range(SEQ)]))]
    ppermute x27 -> x29, starting transfers between devices: 40.8 us -> 42.2 us  [shift(): return lax.ppermute(piece, axis, ring(by))]
    ppermute x27 -> x29, waiting for transfers between devices: 35.3 us -> 34.5 us  [shift(): return lax.ppermute(piece, axis, ring(by))]
  transfers between devices with their start and end apart: 43 -> 48, of which waited for: 19 -> 17; matrix products, arithmetic and copies ran while one was open for 5% -> 3% of each run, Pallas kernels for 10% -> 10%
where the time goes in v3:
time: 193 us; the launch traced here: 192 us
  starting transfers between devices  74.1 us (38%)
  waiting for transfers between devices  63.6 us (33%)
  Pallas kernels  34.8 us (18%)
  local copies, waits for them, and re-layouts  19 us (10%)
    ppermute x29, starting transfers between devices, shift(): return lax.ppermute(piece, axis, ring(by))  42.2 us
    ppermute x29, waiting for transfers between devices, shift(): return lax.ppermute(piece, axis, ring(by))  34.5 us
    unnamed x56, local copies, waits for them, and re-layouts  15.4 us
    ppermute x7, waiting for transfers between devices, sublayer(): lax.ppermute(rest[d], 'seq', [(i, (i + d) % SEQ) for i in range(SEQ)])  12.6 us
    all_to_all x1, waiting for transfers between devices, sublayer(): lax.all_to_all(taken.reshape(HEADS, HD, HD), ('hx', 'hz'), 0, 0, tiled=True)  11.1 us
    ppermute x7, starting transfers between devices, sublayer(): lax.ppermute(rest[d], 'seq', [(i, (i + d) % SEQ) for i in range(SEQ)])  11.1 us
    pallas_call x1, Pallas kernels, sublayer(): pl.pallas_call(project_far, out_shape=(pltpu.HBM((SEQ, SENT, 2 * HD), BF)...  9.22 us
    pallas_call x1, Pallas kernels, sublayer(): pl.pallas_call(project_near, out_shape=(shape((TOK, 3 * HD), F32), shape(...  7.38 us
  transfers between devices with their start and end apart: 48, of which 17 were waited for; matrix products, arithmetic and copies ran while one was open for 3% of the time, Pallas kernels for 10%

profile of v3, /device:TPU:0, one launch (start us, length us, event | category | flops | bytes accessed | tf_op | source)
XLA Modules:
  0.0 192.3 jit_solution(17157662903371005682)
XLA Ops:
  10.4 2.2 %collective-permute-start.4 = (bf16[2048,128]{1,0:T(8,128)(2,1)S(1)}, bf16[2048,128]{1,0:T(8,128)(2,1)S(1)}, u32[]{:S(2)}, u32[]{:S(2)}) collective-permute-start(bf16[2048,128]{1,0:T(8,128)(2,1)S(1)} %pad_maximum_fusion.refs_0_), channel_id=1, source_target_pairs={{0,1},{1,2},{2,3},{3,0},{4,5},{5,6},{6,7},{7,4},{8,9},{9,10},{10,1... | collective-permute-start | bytes 1572872 | tf_op jit(solution)/shard_map/ppermute | solution.py:49
  12.6 2.2 %collective-permute-start.6 = (bf16[2048,128]{1,0:T(8,128)(2,1)S(1)}, bf16[2048,128]{1,0:T(8,128)(2,1)S(1)}, u32[]{:S(2)}, u32[]{:S(2)}) collective-permute-start(bf16[2048,128]{1,0:T(8,128)(2,1)S(1)} %pad_maximum_fusion.refs_0_), channel_id=1, source_target_pairs={{0,3},{1,0},{2,1},{3,2},{4,7},{5,4},{6,5},{7,6},{8,11},{9,8},{10,9... | collective-permute-start | bytes 1572872 | tf_op jit(solution)/shard_map/ppermute | solution.py:49
  15.2 3.0 %collective-permute-start.3 = (bf16[512,128]{1,0:T(8,128)(2,1)S(1)}, bf16[512,128]{1,0:T(8,128)(2,1)S(1)}, u32[]{:S(2)}, u32[]{:S(2)}) collective-permute-start(bf16[512,128]{1,0:T(8,128)(2,1)S(1)} %slice.25), channel_id=1, source_target_pairs={{0,12},{4,0},{8,4},{12,8},{1,13},{5,1},{9,5},{13,9},{2,14},{6,2},{... | collective-permute-start | bytes 393224 | tf_op jit(solution)/shard_map/ppermute | solution.py:49
  24.5 4.1 %collective-permute-done.10 = bf16[512,128]{1,0:T(8,128)(2,1)S(1)} collective-permute-done((bf16[512,128]{1,0:T(8,128)(2,1)S(1)}, bf16[512,128]{1,0:T(8,128)(2,1)S(1)}, u32[]{:S(2)}, u32[]{:S(2)}) %collective-permute-start.10) | collective-permute-done | bytes 131104 | tf_op jit(solution)/shard_map/ppermute | solution.py:49
  31.5 3.2 %collective-permute-start.7 = (bf16[2048,128]{1,0:T(8,128)(2,1)}, bf16[2048,128]{1,0:T(8,128)(2,1)}, u32[]{:S(2)}, u32[]{:S(2)}) collective-permute-start(bf16[2048,128]{1,0:T(8,128)(2,1)} %constant_dynamic-update-slice_fusion.refs_1_), channel_id=1, source_target_pairs={{0,3},{1,0},{2,1},{3,2},{4,7},{5,4},{6,5},{7,6},{8,11},{9,8},{10,9... | collective-permute-start | bytes 1572872 | tf_op jit(solution)/shard_map/ppermute | solution.py:49
  37.6 5.9 %collective-permute-done.14.refs_10_ = bf16[2048,128]{1,0:T(8,128)(2,1)} collective-permute-done((bf16[2048,128]{1,0:T(8,128)(2,1)S(1)}, bf16[2048,128]{1,0:T(8,128)(2,1)}, u32[]{:S(2)}, u32[]{:S(2)}) %collective-permute-start.14) | collective-permute-done | bytes 524320 | tf_op jit(solution)/shard_map/ppermute | solution.py:49
  43.5 2.3 %collective-permute-done.5.refs_3_ = bf16[2048,128]{1,0:T(8,128)(2,1)} collective-permute-done((bf16[2048,128]{1,0:T(8,128)(2,1)}, bf16[2048,128]{1,0:T(8,128)(2,1)}, u32[]{:S(2)}, u32[]{:S(2)}) %collective-permute-start.5) | collective-permute-done | bytes 524320 | tf_op jit(solution)/shard_map/ppermute | solution.py:49
  47.9 4.3 %collective-permute-done.15.refs_11_ = bf16[2048,128]{1,0:T(8,128)(2,1)} collective-permute-done((bf16[2048,128]{1,0:T(8,128)(2,1)}, bf16[2048,128]{1,0:T(8,128)(2,1)}, u32[]{:S(2)}, u32[]{:S(2)}) %collective-permute-start.15) | collective-permute-done | bytes 524320 | tf_op jit(solution)/shard_map/ppermute | solution.py:49
  52.3 2.7 %collective-permute-start.19 = (bf16[2048,128]{1,0:T(8,128)(2,1)}, bf16[2048,128]{1,0:T(8,128)(2,1)S(1)}, u32[]{:S(2)}, u32[]{:S(2)}) collective-permute-start(bf16[2048,128]{1,0:T(8,128)(2,1)} %collective-permute-done.15.refs_11_), channel_id=1, source_target_pairs={{0,12},{4,0},{8,4},{12,8},{1,13},{5,1},{9,5},{13,9},{2,14},{6,2},{... | collective-permute-start | bytes 1572872 | tf_op jit(solution)/shard_map/ppermute | solution.py:49
  57.1 7.4 %project_near.1 = (f32[2048,384]{1,0:T(8,128)S(1)}, bf16[128,2048]{1,0:T(8,128)(2,1)S(1)}) custom-call(s32[4]{0:T(128)S(1)} %pad_add_fusion.place_ref, bf16[2048,128]{1,0:T(8,128)(2,1)S(1)} %copy-done.1, bf16[2048,128]{1,0:T(8,128)(2,1)S(1)} %copy-done.2, bf16[2048,128]{1,0:T(8,128)(2,1)S(1)} %copy-done.3, bf16[2048,128]{1,0:T(8,128)(2,1)S(1)} %pad_maximum_fusion.refs_0_, ...), custom_call_target="tpu_custom_call" | custom-call | flops 2415919104 | bytes 10485760 | tf_op jit(solution)/shard_map/project_near/pallas_call | solution.py:437
  64.9 9.2 %project_far.1 = (bf16[8,464,256]{2,1,0:T(8,128)(2,1)}, bf16[384,256]{1,0:T(8,128)(2,1)}, bf16[384,256]{1,0:T(8,128)(2,1)}, bf16[384,256]{1,0:T(8,128)(2,1)}, bf...) custom-call(s32[4]{0:T(128)S(1)} %pad_add_fusion.place_ref, ...), custom_call_target="tpu_custom_call" | custom-call | flops 805306368 | bytes 25165824 | tf_op jit(solution)/shard_map/project_far/pallas_call | solution.py:449
  74.1 4.6 %all-to-all-start = ((bf16[8,464,256]{2,1,0:T(8,128)(2,1)}), bf16[8,464,256]{2,1,0:T(8,128)(2,1)S(1)}, u32[]{:S(2)}, u32[]{:S(2)}) async-start(bf16[8,464,256]{2,1,0:T(8,128)(2,1)} %get-tuple-element.23), calls=%async_computation | async-start | bytes 3801088 | tf_op jit(solution)/shard_map/all_to_all | solution.py:473
  78.9 3.2 %collective-permute-start.28 = (bf16[128,1024]{1,0:T(8,128)(2,1)S(1)}, bf16[128,1024]{1,0:T(8,128)(2,1)S(1)}, u32[]{:S(2)}, u32[]{:S(2)}) collective-permute-start(bf16[128,1024]{1,0:T(8,128)(2,1)S(1)} %constant_dynamic-slice_fusion), channel_id=1, source_target_pairs={{0,12},{4,0},{8,4},{12,8},{1,13},{5,1},{9,5},{13,9},{2,14},{6,2},{... | collective-permute-start | bytes 786440 | tf_op jit(solution)/shard_map/ppermute | solution.py:49
  85.5 3.5 %collective-permute-done.27 = bf16[128,1024]{1,0:T(8,128)(2,1)S(1)} collective-permute-done((bf16[128,1024]{1,0:T(8,128)(2,1)S(1)}, bf16[128,1024]{1,0:T(8,128)(2,1)S(1)}, u32[]{:S(2)}, u32[]{:S(2)}) %collective-permute-start.27) | collective-permute-done | bytes 262176 | tf_op jit(solution)/shard_map/ppermute | solution.py:49
  89.6 4.3 %collective-permute-done.28 = bf16[128,1024]{1,0:T(8,128)(2,1)S(1)} collective-permute-done((bf16[128,1024]{1,0:T(8,128)(2,1)S(1)}, bf16[128,1024]{1,0:T(8,128)(2,1)S(1)}, u32[]{:S(2)}, u32[]{:S(2)}) %collective-permute-start.28) | collective-permute-done | bytes 262176 | tf_op jit(solution)/shard_map/ppermute | solution.py:49
  93.9 3.1 %collective-permute-start.23 = (bf16[384,256]{1,0:T(8,128)(2,1)}, bf16[384,256]{1,0:T(8,128)(2,1)S(1)}, u32[]{:S(2)}, u32[]{:S(2)}) collective-permute-start(bf16[384,256]{1,0:T(8,128)(2,1)} %get-tuple-element.28), channel_id=1, source_target_pairs={{0,64},{16,80},{32,96},{48,112},{64,0},{80,16},{96,32},{112,48},{1... | collective-permute-start | bytes 589832 | tf_op jit(solution)/shard_map/ppermute | solution.py:476
  98.5 8.8 %collective-permute-done.20.refs_1_ = bf16[384,256]{1,0:T(8,128)(2,1)S(1)} collective-permute-done((bf16[384,256]{1,0:T(8,128)(2,1)}, bf16[384,256]{1,0:T(8,128)(2,1)S(1)}, u32[]{:S(2)}, u32[]{:S(2)}) %collective-permute-start.20) | collective-permute-done | bytes 196640 | tf_op jit(solution)/shard_map/ppermute | solution.py:476
  108.1 3.9 %collective-permute-start.26 = (bf16[384,256]{1,0:T(8,128)(2,1)S(1)}, bf16[384,256]{1,0:T(8,128)(2,1)S(1)}, u32[]{:S(2)}, u32[]{:S(2)}) collective-permute-start(bf16[384,256]{1,0:T(8,128)(2,1)S(1)} %copy-done.24), channel_id=1, source_target_pairs={{0,112},{16,0},{32,16},{48,32},{64,48},{80,64},{96,80},{112,96},{1... | collective-permute-start | bytes 589832 | tf_op jit(solution)/shard_map/ppermute | solution.py:476
  112.7 3.2 %collective-permute-done.22.refs_3_ = bf16[384,256]{1,0:T(8,128)(2,1)S(1)} collective-permute-done((bf16[384,256]{1,0:T(8,128)(2,1)}, bf16[384,256]{1,0:T(8,128)(2,1)S(1)}, u32[]{:S(2)}, u32[]{:S(2)}) %collective-permute-start.22) | collective-permute-done | bytes 196640 | tf_op jit(solution)/shard_map/ppermute | solution.py:476
  119.3 2.3 %collective-permute-start.32 = (bf16[256,1024]{1,0:T(8,128)(2,1)}, bf16[256,1024]{1,0:T(8,128)(2,1)}, u32[]{:S(2)}, u32[]{:S(2)}) collective-permute-start(bf16[256,1024]{1,0:T(8,128)(2,1)} %constant_dynamic-update-slice_fusion.6.refs_0_), channel_id=1, source_target_pairs={{0,3},{1,0},{2,1},{3,2},{4,7},{5,4},{6,5},{7,6},{8,11},{9,8},{10,9... | collective-permute-start | bytes 1572872 | tf_op jit(solution)/shard_map/ppermute | solution.py:49
  130.2 4.6 %attend_early.1 = bf16[8,4,64,128]{3,2,1,0:T(8,128)(2,1)} custom-call(s32[4]{0:T(128)S(1)} %pad_add_fusion.place_ref, bf16[8,464,256]{2,1,0:T(8,128)(2,1)S(1)} %all-to-all-done.got, bf16[384,256]{1,0:T(8,128)(2,1)S(1)} %copy-done.5, bf16[384,256]{1,0:T(8,128)(2,1)S(1)} %collective-permute-done.20.refs_1_, bf16[384,256]{1,0:T(8,128)(2,1)S(1)} %copy-done.7, ...), custom_call_target="tpu_custom_call" | custom-call | flops 1073741824 | bytes 8388608 | tf_op jit(solution)/shard_map/attend_early/pallas_call | solution.py:509
  134.8 3.5 %all-to-all-start.1 = ((bf16[8,4,64,128]{3,2,1,0:T(8,128)(2,1)}), bf16[8,4,64,128]{3,2,1,0:T(8,128)(2,1)S(1)}, u32[]{:S(2)}, u32[]{:S(2)}) async-start(bf16[8,4,64,128]{3,2,1,0:T(8,128)(2,1)} %attend_early.1), calls=%async_computation.1 | async-start | bytes 1048576 | tf_op jit(solution)/shard_map/all_to_all | solution.py:519
  141.1 3.6 %collective-permute-done.33.refs_5_ = bf16[256,1024]{1,0:T(8,128)(2,1)} collective-permute-done((bf16[256,1024]{1,0:T(8,128)(2,1)S(1)}, bf16[256,1024]{1,0:T(8,128)(2,1)}, u32[]{:S(2)}, u32[]{:S(2)}) %collective-permute-start.33) | collective-permute-done | bytes 524320 | tf_op jit(solution)/shard_map/ppermute | solution.py:49
  144.6 2.9 %collective-permute-start.35 = (bf16[256,1024]{1,0:T(8,128)(2,1)}, bf16[256,1024]{1,0:T(8,128)(2,1)}, u32[]{:S(2)}, u32[]{:S(2)}) collective-permute-start(bf16[256,1024]{1,0:T(8,128)(2,1)} %collective-permute-done.33.refs_5_), channel_id=1, source_target_pairs={{0,3},{1,0},{2,1},{3,2},{4,7},{5,4},{6,5},{7,6},{8,11},{9,8},{10,9... | collective-permute-start | bytes 1572872 | tf_op jit(solution)/shard_map/ppermute | solution.py:49
  147.6 4.0 %attend_late.1 = bf16[8,4,64,128]{3,2,1,0:T(8,128)(2,1)} custom-call(bf16[8,464,256]{2,1,0:T(8,128)(2,1)S(1)} %all-to-all-done.got), custom_call_target="tpu_custom_call" | custom-call | flops 1073741824 | bytes 6291456 | tf_op jit(solution)/shard_map/attend_late/pallas_call | solution.py:497
  151.6 3.9 %all-to-all-start.2 = ((bf16[8,4,64,128]{3,2,1,0:T(8,128)(2,1)}), bf16[8,4,64,128]{3,2,1,0:T(8,128)(2,1)S(1)}, u32[]{:S(2)}, u32[]{:S(2)}) async-start(bf16[8,4,64,128]{3,2,1,0:T(8,128)(2,1)} %attend_late.1), calls=%async_computation.2 | async-start | bytes 1048576 | tf_op jit(solution)/shard_map/all_to_all | solution.py:507
  157.2 2.6 %collective-permute-done.35.refs_7_ = bf16[256,1024]{1,0:T(8,128)(2,1)} collective-permute-done((bf16[256,1024]{1,0:T(8,128)(2,1)}, bf16[256,1024]{1,0:T(8,128)(2,1)}, u32[]{:S(2)}, u32[]{:S(2)}) %collective-permute-start.35) | collective-permute-done | bytes 524320 | tf_op jit(solution)/shard_map/ppermute | solution.py:49
  160.4 5.4 %all-to-all-done.2 = bf16[8,4,64,128]{3,2,1,0:T(8,128)(2,1)S(1)} async-done(((bf16[8,4,64,128]{3,2,1,0:T(8,128)(2,1)}), bf16[8,4,64,128]{3,2,1,0:T(8,128)(2,1)S(1)}, u32[]{:S(2)}, u32[]{:S(2)}) %all-to-all-start.2) | async-done | bytes 524320 | tf_op jit(solution)/shard_map/all_to_all | solution.py:507
  165.7 3.9 %take_rows.1 = bf16[2048,128]{1,0:T(8,128)(2,1)} custom-call(s32[2048]{0:T(1024)S(1)} %fusion.2.index_ref, bf16[2048,128]{1,0:T(8,128)(2,1)S(1)} %bitcast.9, bf16[2048,128]{1,0:T(8,128)(2,1)S(1)} %bitcast.10), custom_call_target="tpu_custom_call" | custom-call | bytes 8388608 | tf_op jit(solution)/shard_map/take_rows/pallas_call | solution.py:521
  169.6 5.6 %all-to-all-start.3 = ((bf16[16,128,128]{2,1,0:T(8,128)(2,1)}), bf16[16,128,128]{2,1,0:T(8,128)(2,1)S(1)}, u32[]{:S(2)}, u32[]{:S(2)}) async-start(bf16[16,128,128]{2,1,0:T(8,128)(2,1)} %bitcast.8), calls=%async_computation.3 | async-start | bytes 1048576 | tf_op jit(solution)/shard_map/all_to_all | solution.py:531
  175.3 11.1 %all-to-all-done.3.rows_ref = bf16[16,128,128]{2,1,0:T(8,128)(2,1)S(1)} async-done(((bf16[16,128,128]{2,1,0:T(8,128)(2,1)}), bf16[16,128,128]{2,1,0:T(8,128)(2,1)S(1)}, u32[]{:S(2)}, u32[]{:S(2)}) %all-to-all-start.3) | async-done | bytes 524320 | tf_op jit(solution)/shard_map/all_to_all | solution.py:531
  186.4 5.7 %combine.1 = bf16[128,2048]{1,0:T(8,128)(2,1)} custom-call(s32[4]{0:T(128)S(1)} %pad_add_fusion.place_ref, bf16[16,128,128]{2,1,0:T(8,128)(2,1)S(1)} %all-to-all-done.3.rows_ref, bf16[256,1024]{1,0:T(8,128)(2,1)} %constant_dynamic-update-slice_fusion.6.refs_0_, bf16[256,1024]{1,0:T(8,128)(2,1)S(1)} %constant_dynamic-update-slice_fusion.8.refs_1_, ...), custom_call_target="tpu_custom_call" | custom-call | flops 1073741824 | bytes 10485760 | tf_op jit(solution)/shard_map/combine/pallas_call | solution.py:536
  (142 shorter events, 51.5 us)
Async XLA Ops:
  10.4 21.1 %collective-permute-start.4 = (bf16[2048,128]{1,0:T(8,128)(2,1)S(1)}, bf16[2048,128]{1,0:T(8,128)(2,1)S(1)}, u32[]{:S(2)}, u32[]{:S(2)}) collective-permute-start(bf16[2048,128]{1,0:T(8,128)(2,1)S(1)} %pad_maximum_fusion.refs_0_), channel_id=1, source_target_pairs={{0,1},{1,2},{2,3},{3,0},{4,5},{5,6},{6,7},{7,4},{8,9},{9,10},{10,1... | collective-permute-start | bytes 1572872 | tf_op jit(solution)/shard_map/ppermute | solution.py:49
  12.6 22.1 %collective-permute-start.6 = (bf16[2048,128]{1,0:T(8,128)(2,1)S(1)}, bf16[2048,128]{1,0:T(8,128)(2,1)S(1)}, u32[]{:S(2)}, u32[]{:S(2)}) collective-permute-start(bf16[2048,128]{1,0:T(8,128)(2,1)S(1)} %pad_maximum_fusion.refs_0_), channel_id=1, source_target_pairs={{0,3},{1,0},{2,1},{3,2},{4,7},{5,4},{6,5},{7,6},{8,11},{9,8},{10,9... | collective-permute-start | bytes 1572872 | tf_op jit(solution)/shard_map/ppermute | solution.py:49
  21.1 15.3 %collective-permute-start.12 = (bf16[2048,128]{1,0:T(8,128)(2,1)S(1)}, bf16[2048,128]{1,0:T(8,128)(2,1)}, u32[]{:S(2)}, u32[]{:S(2)}) collective-permute-start(bf16[2048,128]{1,0:T(8,128)(2,1)S(1)} %pad_maximum_fusion.1.refs_6_), channel_id=1, source_target_pairs={{0,4},{4,8},{8,12},{12,0},{1,5},{5,9},{9,13},{13,1},{2,6},{6,10},{... | collective-permute-start | bytes 1572872 | tf_op jit(solution)/shard_map/ppermute | solution.py:49
  31.5 15.4 %collective-permute-start.7 = (bf16[2048,128]{1,0:T(8,128)(2,1)}, bf16[2048,128]{1,0:T(8,128)(2,1)}, u32[]{:S(2)}, u32[]{:S(2)}) collective-permute-start(bf16[2048,128]{1,0:T(8,128)(2,1)} %constant_dynamic-update-slice_fusion.refs_1_), channel_id=1, source_target_pairs={{0,3},{1,0},{2,1},{3,2},{4,7},{5,4},{6,5},{7,6},{8,11},{9,8},{10,9... | collective-permute-start | bytes 1572872 | tf_op jit(solution)/shard_map/ppermute | solution.py:49
  35.6 16.7 %collective-permute-start.15 = (bf16[2048,128]{1,0:T(8,128)(2,1)}, bf16[2048,128]{1,0:T(8,128)(2,1)}, u32[]{:S(2)}, u32[]{:S(2)}) collective-permute-start(bf16[2048,128]{1,0:T(8,128)(2,1)} %constant_dynamic-update-slice_fusion.3.refs_7_), channel_id=1, source_target_pairs={{0,12},{4,0},{8,4},{12,8},{1,13},{5,1},{9,5},{13,9},{2,14},{6,2},{... | collective-permute-start | bytes 1572872 | tf_op jit(solution)/shard_map/ppermute | solution.py:49
  36.4 18.6 %collective-permute-start.13 = (bf16[2048,128]{1,0:T(8,128)(2,1)}, bf16[2048,128]{1,0:T(8,128)(2,1)}, u32[]{:S(2)}, u32[]{:S(2)}) collective-permute-start(bf16[2048,128]{1,0:T(8,128)(2,1)} %constant_dynamic-update-slice_fusion.3.refs_7_), channel_id=1, source_target_pairs={{0,4},{4,8},{8,12},{12,0},{1,5},{5,9},{9,13},{13,1},{2,6},{6,10},{... | collective-permute-start | bytes 1572872 | tf_op jit(solution)/shard_map/ppermute | solution.py:49
  43.5 21.0 %collective-permute-start.16 = (bf16[2048,128]{1,0:T(8,128)(2,1)}, bf16[2048,128]{1,0:T(8,128)(2,1)S(1)}, u32[]{:S(2)}, u32[]{:S(2)}) collective-permute-start(bf16[2048,128]{1,0:T(8,128)(2,1)} %copy-done.18), channel_id=1, source_target_pairs={{0,1},{1,2},{2,3},{3,0},{4,5},{5,6},{6,7},{7,4},{8,9},{9,10},{10,1... | collective-permute-start | bytes 1572872 | tf_op jit(solution)/shard_map/ppermute | solution.py:49
  45.8 18.8 %collective-permute-start.18 = (bf16[2048,128]{1,0:T(8,128)(2,1)}, bf16[2048,128]{1,0:T(8,128)(2,1)S(1)}, u32[]{:S(2)}, u32[]{:S(2)}) collective-permute-start(bf16[2048,128]{1,0:T(8,128)(2,1)} %collective-permute-done.12.refs_8_), channel_id=1, source_target_pairs={{0,4},{4,8},{8,12},{12,0},{1,5},{5,9},{9,13},{13,1},{2,6},{6,10},{... | collective-permute-start | bytes 1572872 | tf_op jit(solution)/shard_map/ppermute | solution.py:49
  46.9 17.7 %collective-permute-start.17 = (bf16[2048,128]{1,0:T(8,128)(2,1)}, bf16[2048,128]{1,0:T(8,128)(2,1)S(1)}, u32[]{:S(2)}, u32[]{:S(2)}) collective-permute-start(bf16[2048,128]{1,0:T(8,128)(2,1)} %collective-permute-done.7.refs_5_), channel_id=1, source_target_pairs={{0,3},{1,0},{2,1},{3,2},{4,7},{5,4},{6,5},{7,6},{8,11},{9,8},{10,9... | collective-permute-start | bytes 1572872 | tf_op jit(solution)/shard_map/ppermute | solution.py:49
  74.1 50.4 %all-to-all-start = ((bf16[8,464,256]{2,1,0:T(8,128)(2,1)}), bf16[8,464,256]{2,1,0:T(8,128)(2,1)S(1)}, u32[]{:S(2)}, u32[]{:S(2)}) async-start(bf16[8,464,256]{2,1,0:T(8,128)(2,1)} %get-tuple-element.23), calls=%async_computation | async-start | bytes 3801088 | tf_op jit(solution)/shard_map/all_to_all | solution.py:473
  78.9 15.0 %collective-permute-start.28 = (bf16[128,1024]{1,0:T(8,128)(2,1)S(1)}, bf16[128,1024]{1,0:T(8,128)(2,1)S(1)}, u32[]{:S(2)}, u32[]{:S(2)}) collective-permute-start(bf16[128,1024]{1,0:T(8,128)(2,1)S(1)} %constant_dynamic-slice_fusion), channel_id=1, source_target_pairs={{0,12},{4,0},{8,4},{12,8},{1,13},{5,1},{9,5},{13,9},{2,14},{6,2},{... | collective-permute-start | bytes 786440 | tf_op jit(solution)/shard_map/ppermute | solution.py:49
  83.5 23.9 %collective-permute-start.20 = (bf16[384,256]{1,0:T(8,128)(2,1)}, bf16[384,256]{1,0:T(8,128)(2,1)S(1)}, u32[]{:S(2)}, u32[]{:S(2)}) collective-permute-start(bf16[384,256]{1,0:T(8,128)(2,1)} %get-tuple-element.25), channel_id=1, source_target_pairs={{0,16},{16,32},{32,48},{48,64},{64,80},{80,96},{96,112},{112,0},{1... | collective-permute-start | bytes 589832 | tf_op jit(solution)/shard_map/ppermute | solution.py:476
  83.5 24.7 %collective-permute-start.21 = (bf16[384,256]{1,0:T(8,128)(2,1)}, bf16[384,256]{1,0:T(8,128)(2,1)S(1)}, u32[]{:S(2)}, u32[]{:S(2)}) collective-permute-start(bf16[384,256]{1,0:T(8,128)(2,1)} %get-tuple-element.26), channel_id=1, source_target_pairs={{0,32},{16,48},{32,64},{48,80},{64,96},{80,112},{96,0},{112,16},{1... | collective-permute-start | bytes 589832 | tf_op jit(solution)/shard_map/ppermute | solution.py:476
  89.0 27.0 %collective-permute-start.22 = (bf16[384,256]{1,0:T(8,128)(2,1)}, bf16[384,256]{1,0:T(8,128)(2,1)S(1)}, u32[]{:S(2)}, u32[]{:S(2)}) collective-permute-start(bf16[384,256]{1,0:T(8,128)(2,1)} %get-tuple-element.27), channel_id=1, source_target_pairs={{0,48},{16,64},{32,80},{48,96},{64,112},{80,0},{96,16},{112,32},{1... | collective-permute-start | bytes 589832 | tf_op jit(solution)/shard_map/ppermute | solution.py:476
  93.9 23.2 %collective-permute-start.23 = (bf16[384,256]{1,0:T(8,128)(2,1)}, bf16[384,256]{1,0:T(8,128)(2,1)S(1)}, u32[]{:S(2)}, u32[]{:S(2)}) collective-permute-start(bf16[384,256]{1,0:T(8,128)(2,1)} %get-tuple-element.28), channel_id=1, source_target_pairs={{0,64},{16,80},{32,96},{48,112},{64,0},{80,16},{96,32},{112,48},{1... | collective-permute-start | bytes 589832 | tf_op jit(solution)/shard_map/ppermute | solution.py:476
  97.1 21.6 %collective-permute-start.24 = (bf16[384,256]{1,0:T(8,128)(2,1)}, bf16[384,256]{1,0:T(8,128)(2,1)S(1)}, u32[]{:S(2)}, u32[]{:S(2)}) collective-permute-start(bf16[384,256]{1,0:T(8,128)(2,1)} %get-tuple-element.29), channel_id=1, source_target_pairs={{0,80},{16,96},{32,112},{48,0},{64,16},{80,32},{96,48},{112,64},{1... | collective-permute-start | bytes 589832 | tf_op jit(solution)/shard_map/ppermute | solution.py:476
  108.1 15.8 %collective-permute-start.26 = (bf16[384,256]{1,0:T(8,128)(2,1)S(1)}, bf16[384,256]{1,0:T(8,128)(2,1)S(1)}, u32[]{:S(2)}, u32[]{:S(2)}) collective-permute-start(bf16[384,256]{1,0:T(8,128)(2,1)S(1)} %copy-done.24), channel_id=1, source_target_pairs={{0,112},{16,0},{32,16},{48,32},{64,48},{80,64},{96,80},{112,96},{1... | collective-permute-start | bytes 589832 | tf_op jit(solution)/shard_map/ppermute | solution.py:476
  116.6 22.6 %collective-permute-start.30 = (bf16[256,1024]{1,0:T(8,128)(2,1)}, bf16[256,1024]{1,0:T(8,128)(2,1)}, u32[]{:S(2)}, u32[]{:S(2)}) collective-permute-start(bf16[256,1024]{1,0:T(8,128)(2,1)} %constant_dynamic-update-slice_fusion.6.refs_0_), channel_id=1, source_target_pairs={{0,1},{1,2},{2,3},{3,0},{4,5},{5,6},{6,7},{7,4},{8,9},{9,10},{10,1... | collective-permute-start | bytes 1572872 | tf_op jit(solution)/shard_map/ppermute | solution.py:49
  117.7 22.5 %collective-permute-start.31 = (bf16[256,1024]{1,0:T(8,128)(2,1)S(1)}, bf16[256,1024]{1,0:T(8,128)(2,1)}, u32[]{:S(2)}, u32[]{:S(2)}) collective-permute-start(bf16[256,1024]{1,0:T(8,128)(2,1)S(1)} %constant_dynamic-update-slice_fusion.8.refs_1_), channel_id=1, source_target_pairs={{0,1},{1,2},{2,3},{3,0},{4,5},{5,6},{6,7},{7,4},{8,9},{9,10},{10,1... | collective-permute-start | bytes 1572872 | tf_op jit(solution)/shard_map/ppermute | solution.py:49
  119.3 21.6 %collective-permute-start.32 = (bf16[256,1024]{1,0:T(8,128)(2,1)}, bf16[256,1024]{1,0:T(8,128)(2,1)}, u32[]{:S(2)}, u32[]{:S(2)}) collective-permute-start(bf16[256,1024]{1,0:T(8,128)(2,1)} %constant_dynamic-update-slice_fusion.6.refs_0_), channel_id=1, source_target_pairs={{0,3},{1,0},{2,1},{3,2},{4,7},{5,4},{6,5},{7,6},{8,11},{9,8},{10,9... | collective-permute-start | bytes 1572872 | tf_op jit(solution)/shard_map/ppermute | solution.py:49
  122.3 22.3 %collective-permute-start.33 = (bf16[256,1024]{1,0:T(8,128)(2,1)S(1)}, bf16[256,1024]{1,0:T(8,128)(2,1)}, u32[]{:S(2)}, u32[]{:S(2)}) collective-permute-start(bf16[256,1024]{1,0:T(8,128)(2,1)S(1)} %constant_dynamic-update-slice_fusion.8.refs_1_), channel_id=1, source_target_pairs={{0,3},{1,0},{2,1},{3,2},{4,7},{5,4},{6,5},{7,6},{8,11},{9,8},{10,9... | collective-permute-start | bytes 1572872 | tf_op jit(solution)/shard_map/ppermute | solution.py:49
  134.8 16.8 %all-to-all-start.1 = ((bf16[8,4,64,128]{3,2,1,0:T(8,128)(2,1)}), bf16[8,4,64,128]{3,2,1,0:T(8,128)(2,1)S(1)}, u32[]{:S(2)}, u32[]{:S(2)}) async-start(bf16[8,4,64,128]{3,2,1,0:T(8,128)(2,1)} %attend_early.1), calls=%async_computation.1 | async-start | bytes 1048576 | tf_op jit(solution)/shard_map/all_to_all | solution.py:519
  138.3 17.2 %collective-permute-start.36 = (bf16[256,1024]{1,0:T(8,128)(2,1)}, bf16[256,1024]{1,0:T(8,128)(2,1)}, u32[]{:S(2)}, u32[]{:S(2)}) collective-permute-start(bf16[256,1024]{1,0:T(8,128)(2,1)} %constant_dynamic-update-slice_fusion.6.refs_0_), channel_id=1, source_target_pairs={{0,16},{16,0},{32,48},{48,32},{64,80},{80,64},{96,112},{112,96},{1... | collective-permute-start | bytes 1572872 | tf_op jit(solution)/shard_map/ppermute | solution.py:489
  139.2 17.5 %collective-permute-start.37 = (bf16[256,1024]{1,0:T(8,128)(2,1)S(1)}, bf16[256,1024]{1,0:T(8,128)(2,1)}, u32[]{:S(2)}, u32[]{:S(2)}) collective-permute-start(bf16[256,1024]{1,0:T(8,128)(2,1)S(1)} %constant_dynamic-update-slice_fusion.8.refs_1_), channel_id=1, source_target_pairs={{0,16},{16,0},{32,48},{48,32},{64,80},{80,64},{96,112},{112,96},{1... | collective-permute-start | bytes 1572872 | tf_op jit(solution)/shard_map/ppermute | solution.py:489
  140.2 16.6 %collective-permute-start.34 = (bf16[256,1024]{1,0:T(8,128)(2,1)}, bf16[256,1024]{1,0:T(8,128)(2,1)}, u32[]{:S(2)}, u32[]{:S(2)}) collective-permute-start(bf16[256,1024]{1,0:T(8,128)(2,1)} %collective-permute-done.30.refs_2_), channel_id=1, source_target_pairs={{0,1},{1,2},{2,3},{3,0},{4,5},{5,6},{6,7},{7,4},{8,9},{9,10},{10,1... | collective-permute-start | bytes 1572872 | tf_op jit(solution)/shard_map/ppermute | solution.py:49
  140.9 19.4 %collective-permute-start.38 = (bf16[256,1024]{1,0:T(8,128)(2,1)}, bf16[256,1024]{1,0:T(8,128)(2,1)}, u32[]{:S(2)}, u32[]{:S(2)}) collective-permute-start(bf16[256,1024]{1,0:T(8,128)(2,1)} %collective-permute-done.30.refs_2_), channel_id=1, source_target_pairs={{0,16},{16,0},{32,48},{48,32},{64,80},{80,64},{96,112},{112,96},{1... | collective-permute-start | bytes 1572872 | tf_op jit(solution)/shard_map/ppermute | solution.py:489
  144.6 15.2 %collective-permute-start.35 = (bf16[256,1024]{1,0:T(8,128)(2,1)}, bf16[256,1024]{1,0:T(8,128)(2,1)}, u32[]{:S(2)}, u32[]{:S(2)}) collective-permute-start(bf16[256,1024]{1,0:T(8,128)(2,1)} %collective-permute-done.33.refs_5_), channel_id=1, source_target_pairs={{0,3},{1,0},{2,1},{3,2},{4,7},{5,4},{6,5},{7,6},{8,11},{9,8},{10,9... | collective-permute-start | bytes 1572872 | tf_op jit(solution)/shard_map/ppermute | solution.py:49
  155.5 19.7 %collective-permute-start.41 = (bf16[256,1024]{1,0:T(8,128)(2,1)}, bf16[256,1024]{1,0:T(8,128)(2,1)S(1)}, u32[]{:S(2)}, u32[]{:S(2)}) collective-permute-start(bf16[256,1024]{1,0:T(8,128)(2,1)} %collective-permute-done.33.refs_5_), channel_id=1, source_target_pairs={{0,16},{16,0},{32,48},{48,32},{64,80},{80,64},{96,112},{112,96},{1... | collective-permute-start | bytes 1572872 | tf_op jit(solution)/shard_map/ppermute | solution.py:489
  156.7 18.5 %collective-permute-start.39 = (bf16[256,1024]{1,0:T(8,128)(2,1)}, bf16[256,1024]{1,0:T(8,128)(2,1)}, u32[]{:S(2)}, u32[]{:S(2)}) collective-permute-start(bf16[256,1024]{1,0:T(8,128)(2,1)} %collective-permute-done.31.refs_3_), channel_id=1, source_target_pairs={{0,16},{16,0},{32,48},{48,32},{64,80},{80,64},{96,112},{112,96},{1... | collective-permute-start | bytes 1572872 | tf_op jit(solution)/shard_map/ppermute | solution.py:489
  156.8 18.4 %collective-permute-start.40 = (bf16[256,1024]{1,0:T(8,128)(2,1)}, bf16[256,1024]{1,0:T(8,128)(2,1)}, u32[]{:S(2)}, u32[]{:S(2)}) collective-permute-start(bf16[256,1024]{1,0:T(8,128)(2,1)} %collective-permute-done.32.refs_4_), channel_id=1, source_target_pairs={{0,16},{16,0},{32,48},{48,32},{64,80},{80,64},{96,112},{112,96},{1... | collective-permute-start | bytes 1572872 | tf_op jit(solution)/shard_map/ppermute | solution.py:489
  159.9 15.4 %collective-permute-start.42 = (bf16[256,1024]{1,0:T(8,128)(2,1)}, bf16[256,1024]{1,0:T(8,128)(2,1)}, u32[]{:S(2)}, u32[]{:S(2)}) collective-permute-start(bf16[256,1024]{1,0:T(8,128)(2,1)} %collective-permute-done.34.refs_6_), channel_id=1, source_target_pairs={{0,16},{16,0},{32,48},{48,32},{64,80},{80,64},{96,112},{112,96},{1... | collective-permute-start | bytes 1572872 | tf_op jit(solution)/shard_map/ppermute | solution.py:489
  169.6 16.8 %all-to-all-start.3 = ((bf16[16,128,128]{2,1,0:T(8,128)(2,1)}), bf16[16,128,128]{2,1,0:T(8,128)(2,1)S(1)}, u32[]{:S(2)}, u32[]{:S(2)}) async-start(bf16[16,128,128]{2,1,0:T(8,128)(2,1)} %bitcast.8), calls=%async_computation.3 | async-start | bytes 1048576 | tf_op jit(solution)/shard_map/all_to_all | solution.py:531
  (41 other events, 592.6 us)
